TPU v7x, 256 devices: a whole 4x4x8 slice. The times are simulated.
256 devices in a mesh: rep: 16 (over z, core), exp: 16 (over y, x).
Axes of the slice: x: 4, y: 4, z: 8, core: 2. Of those that a mesh axis runs over, the one named last changes fastest.
Arguments:
- latents: float32 [32, 32, 2048], P('rep', None, 'exp'), may hold values from -6 to 6
- latent_mean: float32 [32, 32, 2048], P('rep', None, 'exp'), may hold values from -0.12 to 0.12
- latent_square: float32 [32, 32, 2048], P('rep', None, 'exp'), may hold values from 0.0001 to 0.01
- weight_one: bfloat16 [64, 64, 256], P('exp'), may hold values from -0.75 to 0.75
- weight_two: bfloat16 [64, 256, 256], P('exp'), may hold values from -0.375 to 0.375
- weight_three: bfloat16 [64, 3, 256], P('exp'), may hold values from -0.375 to 0.375
- dir_table: bfloat16 [256, 32], replicated, may hold values from -6 to 6
- materials: int32 [524288, 1], P(('rep', 'exp')), may hold values from 0 to 63; in each aligned block of 2048 rows (0 to 2047, 2048 to 4095, ...) at most 64 rows name the same one
- tile_ids: int32 [524288], P(('rep', 'exp')), may hold values from 0 to 1
- texel_ids: int32 [524288], P(('rep', 'exp')), may hold values from 0 to 2047
- dir_ids: int32 [524288], P(('rep', 'exp')), may hold values from 0 to 255
- targets: float32 [3, 524288], P(None, ('rep', 'exp')), may hold values from -12 to 12
Outputs:
- new_latents: float32 [32, 32, 2048], P('rep', None, 'exp')
- new_mean: float32 [32, 32, 2048], P('rep', None, 'exp')
- new_square: float32 [32, 32, 2048], P('rep', None, 'exp')
- predictions: float32 [3, 524288], P(None, ('rep', 'exp'))
- grad_one: float32 [64, 64, 256], P('exp')
- grad_two: float32 [64, 256, 256], P('exp')
- grad_three: float32 [64, 3, 256], P('exp')
Inputs may be any that keep to these rules, and one draw needn't show every extreme that they name: `materials`: within the rows of one device no material is named by more than 64 rows, a bound that some block reaches.
All inputs are finite; a program needn't handle non-finite values.
Results may differ from a plain program's by a relative error of at most 0.02.
Values may be sent and summed in bfloat16 or wider, within the bound.
No kernel may reach another device: no remote copies, remote signals or barrier semaphores. Data moves between devices by JAX's collectives and lax.ppermute only.
A program may use at most 64 MiB of HBM per device.

v0:
```python
import jax
import jax.numpy as jnp
from jax import lax
from jax.sharding import PartitionSpec as P

LAT = 32
OUTC = 3


decay_one = 0.9
decay_two = 0.99
step_rate = 0.05
epsilon = 1e-08


def from_everyone(x, axis):
    peers = lax.axis_size(axis)
    return lax.all_to_all(jnp.broadcast_to(x[None], (peers, *x.shape)), axis, 0, 0, tiled=True)


def laid_out(parts, dim):
    lengths = list(parts.shape[1:])
    lengths[dim] *= parts.shape[0]
    return jnp.moveaxis(parts, 0, dim).reshape(lengths)


def collect(x, axis, dim):
    parts = from_everyone(x, axis)
    return laid_out(parts, dim)


def together(arrays, axis):
    ends = [0]
    for a in arrays:
        ends.append(ends[-1] + a.size)
    so_far = lax.psum(jnp.concatenate([a.ravel() for a in arrays]), axis)
    return tuple((so_far[b:e].reshape(a.shape) for a, b, e in zip(arrays, ends, ends[1:])))


def cut_along(x, dim, peers):
    lengths = x.shape
    parts = x.reshape(*lengths[:dim], peers, lengths[dim] // peers, *lengths[dim + 1 :])
    return jnp.moveaxis(parts, dim, 0)


def summed_on_arrival(x, axis, dim):
    peers = lax.axis_size(axis)
    parts = lax.all_to_all(cut_along(x, dim, peers), axis, 0, 0, tiled=True)
    return jnp.sum(parts.astype(jnp.float32), axis=0)


def silu_slope(preact):
    sigmoid_v = jax.nn.sigmoid(preact)
    return sigmoid_v * (1.0 + preact * (1.0 - sigmoid_v))


def expert_step(inputs, target_rows, layer_one, layer_two, layer_three):
    pre_one = jnp.dot(inputs, layer_one, preferred_element_type=jnp.float32)
    act_one = jax.nn.silu(pre_one).astype(jnp.bfloat16)
    pre_two = jnp.dot(act_one, layer_two, preferred_element_type=jnp.float32)
    act_two = jax.nn.silu(pre_two).astype(jnp.bfloat16)
    predicted = lax.dot_general(
        act_two, layer_three, (((1,), (1,)), ((), ())), preferred_element_type=jnp.float32
    )
    misfit = (predicted - target_rows).astype(jnp.bfloat16)
    grad_three = lax.dot_general(
        misfit, act_two, (((0,), (0,)), ((), ())), preferred_element_type=jnp.float32
    )
    back_two = jnp.dot(misfit, layer_three, preferred_element_type=jnp.float32)
    delta_two = (back_two * silu_slope(pre_two)).astype(jnp.bfloat16)
    grad_two = lax.dot_general(
        act_one, delta_two, (((0,), (0,)), ((), ())), preferred_element_type=jnp.float32
    )
    back_one = lax.dot_general(
        delta_two, layer_two, (((1,), (1,)), ((), ())), preferred_element_type=jnp.float32
    )
    delta_one = (back_one * silu_slope(pre_one)).astype(jnp.bfloat16)
    grad_one = lax.dot_general(
        inputs, delta_one, (((0,), (0,)), ((), ())), preferred_element_type=jnp.float32
    )
    latent_part = layer_one[:LAT]
    latent_rows = lax.dot_general(
        delta_one, latent_part, (((1,), (1,)), ((), ())), preferred_element_type=jnp.float32
    )
    return (latent_rows.astype(jnp.bfloat16), predicted, grad_one, grad_two, grad_three)


def direction_rows(entries, dir_table):
    table_hot = (
        entries[:, None] == jnp.arange(dir_table.shape[0], dtype=jnp.int32)[None, :]
    ).astype(jnp.bfloat16)
    return jnp.dot(table_hot, dir_table, preferred_element_type=jnp.float32).astype(jnp.bfloat16)


def on_device(
    latents,
    latent_mean,
    latent_square,
    weight_one,
    weight_two,
    weight_three,
    dir_table,
    materials,
    tile_ids,
    texel_ids,
    dir_ids,
    targets,
):
    exp_count = lax.axis_size("exp")
    local_experts = weight_one.shape[0]
    total_experts = local_experts * exp_count
    samples = materials.shape[0]
    capacity = 2 * samples // total_experts
    total_slots = total_experts * capacity
    latent_bf = latents.astype(jnp.bfloat16)
    texture = collect(latent_bf, "exp", 2)
    sample_latent = texture[tile_ids, :, texel_ids]
    material = materials[:, 0]
    one_hot = (material[:, None] == jnp.arange(total_experts, dtype=jnp.int32)[None, :]).astype(
        jnp.int32
    )
    position = jnp.sum((jnp.cumsum(one_hot, axis=0) - 1) * one_hot, axis=1)
    owner_dev = material // local_experts
    within = material % local_experts
    slot_index = (within * exp_count + owner_dev) * capacity + position
    send_targets = jnp.zeros((total_slots, OUTC), jnp.float32).at[slot_index].set(targets.T)
    send_targets = send_targets.reshape(local_experts, exp_count, capacity * OUTC)
    feature_rows = jnp.concatenate([sample_latent, direction_rows(dir_ids, dir_table)], axis=1)
    width = feature_rows.shape[1]
    send_rows = jnp.zeros((total_slots, width), jnp.bfloat16).at[slot_index].set(feature_rows)
    send_rows = send_rows.reshape(local_experts, exp_count, capacity * width)
    got_rows, got_targets = (
        lax.all_to_all(send_rows, "exp", split_axis=1, concat_axis=1, tiled=True),
        lax.all_to_all(
            send_targets.astype(jnp.bfloat16), "exp", split_axis=1, concat_axis=1, tiled=True
        ).astype(send_targets.dtype),
    )
    inputs = got_rows.reshape(local_experts, exp_count * capacity, width)
    wanted = got_targets.reshape(local_experts, exp_count * capacity, OUTC)

    def run_expert(packed):
        return expert_step(packed[0], packed[1], packed[2], packed[3], packed[4])

    latent_rows, predicted, grad_one, grad_two, grad_three = lax.map(
        run_expert, (inputs, wanted, weight_one, weight_two, weight_three)
    )
    back_latent, back_pred = (
        lax.all_to_all(
            latent_rows.reshape(local_experts, exp_count, capacity * LAT),
            "exp",
            split_axis=1,
            concat_axis=1,
            tiled=True,
        ),
        lax.all_to_all(
            predicted.reshape(local_experts, exp_count, capacity * OUTC).astype(jnp.bfloat16),
            "exp",
            split_axis=1,
            concat_axis=1,
            tiled=True,
        ).astype(jnp.float32),
    )
    grad_one, grad_two, grad_three = tuple(
        (
            part.astype(jnp.float32)
            for part in together(
                (
                    grad_one.astype(jnp.bfloat16),
                    grad_two.astype(jnp.bfloat16),
                    grad_three.astype(jnp.bfloat16),
                ),
                "rep",
            )
        )
    )
    sample_grad = back_latent.reshape(total_slots, LAT)[slot_index].astype(jnp.float32)
    sample_pred = back_pred.reshape(total_slots, OUTC)[slot_index]
    dense_grad = jnp.zeros(texture.shape, jnp.float32).at[tile_ids, :, texel_ids].add(sample_grad)
    texel_grad = summed_on_arrival(dense_grad.astype(jnp.bfloat16), "exp", 2)
    new_mean = decay_one * latent_mean + (1.0 - decay_one) * texel_grad
    new_square = decay_two * latent_square + (1.0 - decay_two) * texel_grad * texel_grad
    new_latents = latents - step_rate * new_mean / (jnp.sqrt(new_square) + epsilon)
    return (new_latents, new_mean, new_square, sample_pred.T, grad_one, grad_two, grad_three)


def solution(mesh):
    in_specs = (
        P("rep", None, "exp"),
        P("rep", None, "exp"),
        P("rep", None, "exp"),
        P("exp", None, None),
        P("exp", None, None),
        P("exp", None, None),
        P(),
        P(("rep", "exp"), None),
        P(("rep", "exp")),
        P(("rep", "exp")),
        P(("rep", "exp")),
        P(None, ("rep", "exp")),
    )
    out_specs = (
        P("rep", None, "exp"),
        P("rep", None, "exp"),
        P("rep", None, "exp"),
        P(None, ("rep", "exp")),
        P("exp", None, None),
        P("exp", None, None),
        P("exp", None, None),
    )
    return jax.shard_map(
        on_device, mesh=mesh, in_specs=in_specs, out_specs=out_specs, check_vma=False
    )
```

profile of v0, /device:TPU:1, one launch (start us, length us, event | category | flops | bytes accessed | tf_op | source)
XLA Modules:
  0.0 248.6 jit_solution(3087222375656345451)
XLA Ops:
  8.7 7.6 %all-to-all-start = ((bf16[16,2,32,128]{3,2,1,0:T(8,128)(2,1)}), bf16[16,2,32,128]{3,2,1,0:T(8,128)(2,1)S(1)}, u32[]{:S(2)}, u32[]{:S(2)}) async-start(bf16[16,2,32,128]{3,2,1,0:T(8,128)(2,1)} %broadcast_in_dim.74), calls=%async_computation | async-start | bytes 524288 | tf_op jit(solution)/shard_map/all_to_all | solution.py:18
  17.2 18.1 %reduce-window.6 = s32[64,16,128]{2,1,0:T(8,128)S(1)} reduce-window(s32[64,16,128]{2,1,0:T(8,128)S(1)} %fusion.39, s32[]{:T(128)} %copy.178), window={size=1x1x128 pad=0_0x0_0x127_0}, to_apply=%region_0.0 | reduce-window | flops 16646144 | bytes 1048580 | tf_op jit(solution)/shard_map/reduce-window
  37.2 6.1 %scatter_custom_fusion.1 = f32[4096,3]{1,0:T(8,128)S(1)} fusion(s32[2048]{0:T(1024)S(1)} %bitcast.160, f32[2048,3]{1,0:T(8,128)S(1)} %copy.128, f32[]{:T(128)} %constant.48.clone.1), kind=kCustom, calls=%fused_computation.52 | custom fusion | bytes 49156 | tf_op jit(solution)/shard_map/scatter | solution.py:126
  43.4 1.6 convert_element_type.84
  46.2 6.7 %all-to-all-start.2 = ((bf16[4,16,192]{2,0,1:T(4,128)(2,1)}), bf16[4,16,192]{2,0,1:T(4,128)(2,1)S(1)}, u32[]{:S(2)}, u32[]{:S(2)}) async-start(bf16[4,16,192]{2,0,1:T(4,128)(2,1)} %copy.129), calls=%async_computation.2 | async-start | bytes 65536 | tf_op jit(solution)/shard_map/all_to_all | solution.py:134
  53.4 11.1 %gather_fusion = bf16[2048,32]{1,0:T(8,128)(2,1)S(1)} fusion(bf16[2,32,2048]{1,2,0:T(8,128)(2,1)S(1)} %bitcast.138, s32[2048]{0:T(1024)S(1)} %bitcast.137), kind=kCustom, calls=%fused_computation | custom fusion | bytes 278528 | tf_op jit(solution)/shard_map/gather | solution.py:117
  65.0 6.1 %scatter_custom_fusion = bf16[4096,64]{1,0:T(8,128)(2,1)S(1)} fusion(s32[2048]{0:T(1024)S(1)} %bitcast.161, bf16[2048,64]{1,0:T(8,128)(2,1)S(1)} %copy.125, bf16[]{:T(256)} %constant.56.clone.1), kind=kCustom, calls=%fused_computation.64 | custom fusion | bytes 524290 | tf_op jit(solution)/shard_map/scatter | solution.py:130
  71.9 1.2 copy.126
  73.1 6.7 %all-to-all-start.1 = ((bf16[4,16,4096]{2,0,1:T(4,128)(2,1)}), bf16[4,16,4096]{2,0,1:T(4,128)(2,1)S(1)}, u32[]{:S(2)}, u32[]{:S(2)}) async-start(bf16[4,16,4096]{2,0,1:T(4,128)(2,1)} %copy.126), calls=%async_computation.1 | async-start | bytes 1048576 | tf_op jit(solution)/shard_map/all_to_all | solution.py:133
  80.6 2.1 reshape.107
  83.4 6.0 %all-to-all-done.1 = bf16[4,16,4096]{2,0,1:T(4,128)(2,1)S(1)} async-done(((bf16[4,16,4096]{2,0,1:T(4,128)(2,1)}), bf16[4,16,4096]{2,0,1:T(4,128)(2,1)S(1)}, u32[]{:S(2)}, u32[]{:S(2)}) %all-to-all-start.1) | async-done | bytes 524320 | tf_op jit(solution)/shard_map/all_to_all | solution.py:133
  89.7 1.1 reshape.91
  90.8 19.9 %while.18 = (s32[]{:T(128)}, bf16[4,1024,32]{1,2,0:T(8,128)(2,1)S(1)}, bf16[4,1024,3]{1,2,0:T(4,128)(2,1)S(1)}, bf16[4,64,256]{2,1,0:T(8,128)(2,1)S(1)}, bf16[4,...) while((s32[]{:T(128)}, ...), condition=%wide.region_6.7_spmd, body=%wide.region_5.6_spmd.sunk | while | flops 499950592 | bytes 12312717 | solution.py:144
  90.8 1.0 fusion.88
  94.5 1.0 fusion.92
  95.8 1.0 fusion.88
  99.5 1.0 fusion.92
  100.8 1.0 fusion.88
  104.5 1.0 fusion.92
  105.7 1.0 fusion.88
  111.8 1.6 convert_element_type.89
  114.0 3.5 %all-to-all-start.5 = ((bf16[4,16,192]{2,0,1:T(4,128)(2,1)}), bf16[4,16,192]{2,0,1:T(4,128)(2,1)S(1)}, u32[]{:S(2)}, u32[]{:S(2)}) async-start(bf16[4,16,192]{2,0,1:T(4,128)(2,1)} %copy.140), calls=%async_computation.5 | async-start | bytes 65536 | tf_op jit(solution)/shard_map/all_to_all | solution.py:155
  118.9 1.1 reshape.94
  121.0 2.9 %all-to-all-done.5 = bf16[4,16,192]{2,0,1:T(4,128)(2,1)S(1)} async-done(((bf16[4,16,192]{2,0,1:T(4,128)(2,1)}), bf16[4,16,192]{2,0,1:T(4,128)(2,1)S(1)}, u32[]{:S(2)}, u32[]{:S(2)}) %all-to-all-start.5) | async-done | bytes 24608 | tf_op jit(solution)/shard_map/all_to_all | solution.py:155
  123.9 3.8 %all-to-all-start.3 = ((bf16[4,16,2048]{2,0,1:T(4,128)(2,1)}), bf16[4,16,2048]{2,0,1:T(4,128)(2,1)S(1)}, u32[]{:S(2)}, u32[]{:S(2)}) async-start(bf16[4,16,2048]{2,0,1:T(4,128)(2,1)} %copy.134), calls=%async_computation.3 | async-start | bytes 524288 | tf_op jit(solution)/shard_map/all_to_all | solution.py:148
  127.7 2.1 reshape.109
  129.8 5.5 %gather_fusion.1 = f32[2048,3]{1,0:T(8,128)S(1)} fusion(f32[4096,3]{1,0:T(8,128)S(1)} %reshape.109, s32[2048]{0:T(1024)S(1)} %broadcast_clamp_fusion), kind=kCustom, calls=%fused_computation.2 | custom fusion | bytes 57344 | tf_op jit(solution)/shard_map/gather | solution.py:177
  137.2 18.2 %scatter_custom_fusion.2 = f32[4096,32]{1,0:T(8,128)S(1)} fusion(s32[2048]{0:T(1024)} %broadcast_select_fusion, f32[]{:T(128)} %constant.48.clone.1, bf16[4096,32]{1,0:T(8,128)(2,1)S(1)} %reshape.95, s32[2048]{0:T(1024)S(1)} %broadcast_clamp_fusion), kind=kCustom, calls=%fused_computation.49 | custom fusion | flops 131072 | bytes 795136
  157.0 6.5 %all-to-all-start.4 = ((bf16[16,2,32,128]{3,2,1,0:T(8,128)(2,1)}), bf16[16,2,32,128]{3,2,1,0:T(8,128)(2,1)S(1)}, u32[]{:S(2)}, u32[]{:S(2)}) async-start(bf16[16,2,32,128]{3,2,1,0:T(8,128)(2,1)} %copy.138), calls=%async_computation.4 | async-start | bytes 524288 | tf_op jit(solution)/shard_map/all_to_all | solution.py:48
  163.6 72.0 %all-reduce.2.cloned.1.call-done = bf16[330752]{0:T(1024)(128)(2,1)} async-done(((bf16[330752]{0:T(1024)(128)(2,1)}), bf16[330752]{0:T(1024)(128)(2,1)}) %all-reduce.2.cloned.1.call-update) | async-done | bytes 661520 | tf_op jit(solution)/shard_map/psum | solution.py:36
  235.6 1.1 slice_convert_fusion
  237.6 1.3 reshape.111
  (124 shorter events, 32.7 us)
Async XLA Ops:
  7.2 38.5 %copy-start = (bf16[256,32]{0,1:T(8,128)(2,1)S(1)}, bf16[256,32]{0,1:T(8,128)(2,1)}, u32[]{:S(2)}) copy-start(bf16[256,32]{0,1:T(8,128)(2,1)} %param.20) | copy-start | bytes 49156
  8.7 37.5 %all-to-all-start = ((bf16[16,2,32,128]{3,2,1,0:T(8,128)(2,1)}), bf16[16,2,32,128]{3,2,1,0:T(8,128)(2,1)S(1)}, u32[]{:S(2)}, u32[]{:S(2)}) async-start(bf16[16,2,32,128]{3,2,1,0:T(8,128)(2,1)} %broadcast_in_dim.74), calls=%async_computation | async-start | bytes 524288 | tf_op jit(solution)/shard_map/all_to_all | solution.py:18
  16.3 20.1 %copy-start.3 = (s32[2048,1]{0,1:T(1,128)S(1)}, s32[2048,1]{0,1:T(1,128)}, u32[]{:S(2)}) copy-start(s32[2048,1]{0,1:T(1,128)} %param.21) | copy-start | bytes 24580
  17.1 19.5 %copy-start.7 = (s32[2048]{0:T(1024)S(1)}, s32[2048]{0:T(1024)}, u32[]{:S(2)}) copy-start(s32[2048]{0:T(1024)} %param.22) | copy-start | bytes 24580
  17.1 19.5 %copy-start.8 = (s32[2048]{0:T(1024)S(1)}, s32[2048]{0:T(1024)}, u32[]{:S(2)}) copy-start(s32[2048]{0:T(1024)} %param.23) | copy-start | bytes 24580
  17.1 19.6 %copy-start.11 = (s32[2]{0:T(128)S(1)}, s32[2]{0:T(128)}, u32[]{:S(2)}) copy-start(s32[2]{0:T(128)} %constant.107) | copy-start | bytes 28
  17.1 19.7 %copy-start.4 = (f32[3,2048]{1,0:T(4,128)S(1)}, f32[3,2048]{1,0:T(4,128)}, u32[]{:S(2)}) copy-start(f32[3,2048]{1,0:T(4,128)} %param.25) | copy-start | bytes 73732
  43.3 2.4 copy-start.13
  46.2 26.9 %all-to-all-start.2 = ((bf16[4,16,192]{2,0,1:T(4,128)(2,1)}), bf16[4,16,192]{2,0,1:T(4,128)(2,1)S(1)}, u32[]{:S(2)}, u32[]{:S(2)}) async-start(bf16[4,16,192]{2,0,1:T(4,128)(2,1)} %copy.129), calls=%async_computation.2 | async-start | bytes 65536 | tf_op jit(solution)/shard_map/all_to_all | solution.py:134
  71.1 8.7 %copy-start.10 = (s32[2]{0:T(128)S(1)}, s32[2]{0:T(128)}, u32[]{:S(2)}) copy-start(s32[2]{0:T(128)} %constant.104) | copy-start | bytes 28
  71.1 8.9 %copy-start.9 = (bf16[4,3,256]{2,0,1:T(4,128)(2,1)S(1)}, bf16[4,3,256]{2,0,1:T(4,128)(2,1)}, u32[]{:S(2)}) copy-start(bf16[4,3,256]{2,0,1:T(4,128)(2,1)} %param.19) | copy-start | bytes 18436
  73.1 16.2 %all-to-all-start.1 = ((bf16[4,16,4096]{2,0,1:T(4,128)(2,1)}), bf16[4,16,4096]{2,0,1:T(4,128)(2,1)S(1)}, u32[]{:S(2)}, u32[]{:S(2)}) async-start(bf16[4,16,4096]{2,0,1:T(4,128)(2,1)} %copy.126), calls=%async_computation.1 | async-start | bytes 1048576 | tf_op jit(solution)/shard_map/all_to_all | solution.py:133
  83.4 7.5 %copy-start.2 = (bf16[4,64,256]{2,1,0:T(8,128)(2,1)S(1)}, bf16[4,64,256]{2,1,0:T(8,128)(2,1)}, u32[]{:S(2)}) copy-start(bf16[4,64,256]{2,1,0:T(8,128)(2,1)} %custom-call.8) | copy-start | bytes 393220
  83.4 7.5 %copy-start.12 = (bf16[4,256,256]{2,1,0:T(8,128)(2,1)S(1)}, bf16[4,256,256]{2,1,0:T(8,128)(2,1)}, u32[]{:S(2)}) copy-start(bf16[4,256,256]{2,1,0:T(8,128)(2,1)} %param.18) | copy-start | bytes 1572868
  114.0 9.9 %all-to-all-start.5 = ((bf16[4,16,192]{2,0,1:T(4,128)(2,1)}), bf16[4,16,192]{2,0,1:T(4,128)(2,1)S(1)}, u32[]{:S(2)}, u32[]{:S(2)}) async-start(bf16[4,16,192]{2,0,1:T(4,128)(2,1)} %copy.140), calls=%async_computation.5 | async-start | bytes 65536 | tf_op jit(solution)/shard_map/all_to_all | solution.py:155
  117.5 118.1 %all-reduce.2.cloned.1.call-start = ((), (), s32[]{:S(2)}) async-start(), calls=%async_computation.6 | async-start | bytes 1323008 | tf_op jit(solution)/shard_map/psum | solution.py:36
  123.9 12.4 %all-to-all-start.3 = ((bf16[4,16,2048]{2,0,1:T(4,128)(2,1)}), bf16[4,16,2048]{2,0,1:T(4,128)(2,1)S(1)}, u32[]{:S(2)}, u32[]{:S(2)}) async-start(bf16[4,16,2048]{2,0,1:T(4,128)(2,1)} %copy.134), calls=%async_computation.3 | async-start | bytes 524288 | tf_op jit(solution)/shard_map/all_to_all | solution.py:148
  157.0 84.0 %all-to-all-start.4 = ((bf16[16,2,32,128]{3,2,1,0:T(8,128)(2,1)}), bf16[16,2,32,128]{3,2,1,0:T(8,128)(2,1)S(1)}, u32[]{:S(2)}, u32[]{:S(2)}) async-start(bf16[16,2,32,128]{3,2,1,0:T(8,128)(2,1)} %copy.138), calls=%async_computation.4 | async-start | bytes 524288 | tf_op jit(solution)/shard_map/all_to_all | solution.py:48
  163.5 77.5 %copy-start.1 = (f32[2,32,128]{2,1,0:T(8,128)S(1)}, f32[2,32,128]{2,1,0:T(8,128)}, u32[]{:S(2)}) copy-start(f32[2,32,128]{2,1,0:T(8,128)} %param.14) | copy-start | bytes 98308
  163.5 77.5 %copy-start.5 = (f32[2,32,128]{2,1,0:T(8,128)S(1)}, f32[2,32,128]{2,1,0:T(8,128)}, u32[]{:S(2)}) copy-start(f32[2,32,128]{2,1,0:T(8,128)} %param.15) | copy-start | bytes 98308
  163.5 77.5 %copy-start.6 = (f32[2,32,128]{2,1,0:T(8,128)S(1)}, f32[2,32,128]{2,1,0:T(8,128)}, u32[]{:S(2)}) copy-start(f32[2,32,128]{2,1,0:T(8,128)} %param.16) | copy-start | bytes 98308
Sparse Core Ops, SparseCore 0:
  121.3 114.2 all-reduce.1
where the time goes:
time: 250 us; the launch traced here: 249 us
  waiting for transfers between devices  81 us (32%)
  local copies, waits for them, and re-layouts  53.9 us (22%)
  other arithmetic  43.9 us (18%)
  starting transfers between devices  34.8 us (14%)
  matrix products  20.1 us (8%)
  between operations  14.6 us (6%)
    psum x1, waiting for transfers between devices, together(): so_far = lax.psum(jnp.concatenate([a.ravel() for a in arrays]), axis)  72 us
    unnamed x4, other arithmetic  19 us
    another operation x2, other arithmetic  18.3 us
    gather x2, local copies, waits for them, and re-layouts, on_device(): sample_latent = texture[tile_ids, :, texel_ids]  11.3 us
    all_to_all x1, starting transfers between devices, from_everyone(): lax.all_to_all(jnp.broadcast_to(x[None], (peers, *x.shape)), axis, 0, 0,...  7.58 us
    all_to_all x1, starting transfers between devices, on_device(): lax.all_to_all(send_targets.astype(jnp.bfloat16), 'exp', split_axis=1, co...  6.67 us
    all_to_all x1, starting transfers between devices, on_device(): lax.all_to_all(send_rows, 'exp', split_axis=1, concat_axis=1, tiled=True)  6.67 us
    all_to_all x1, starting transfers between devices, summed_on_arrival(): parts = lax.all_to_all(cut_along(x, dim, peers), axis, 0, 0, tiled=True)  6.54 us
  transfers between devices with their start and end apart: 7, of which 3 were waited for; matrix products, arithmetic and copies ran while one was open for 37% of the time, Pallas kernels for 0%

commit v1 on v0

v1 whole, which is shorter than its diff:
```python
import jax
import jax.numpy as jnp
from jax import lax
from jax.experimental import pallas as pl
from jax.experimental.pallas import tpu as pltpu
from jax.sharding import PartitionSpec as P

LAT = 32
HID = 256
OUTC = 3
LANES = 128
N_EXP = 16
N_REP = 16
CAP = 64
ROWS = 2048
CHUNKS = ROWS // LANES
SLOTS = N_EXP * CAP
GROUPS = 16
TEX_ROWS = 64
SEND_ROWS = TEX_ROWS + 16
GRAD_ROWS = 168

decay_one = 0.9
decay_two = 0.99
step_rate = 0.05
epsilon = 1e-08

f32 = jnp.float32
bf16 = jnp.bfloat16


def dot(a, b):
    return jnp.dot(a, b, preferred_element_type=f32)


def dot_nt(a, b):
    return lax.dot_general(a, b, (((1,), (1,)), ((), ())), preferred_element_type=f32)


def iota(shape, dim):
    return lax.broadcasted_iota(jnp.int32, shape, dim)


def hot(index, count, start=0):
    same = iota((count, index.shape[1]), 0) + start == index
    return jnp.where(same, 1.0, 0.0).astype(bf16)


def route_kernel(mat, tile, texel, direction, targets, latents, send, slot):
    material = mat[...]
    hots = [hot(material[i : i + 1], 64) for i in range(CHUNKS)]
    upper = jnp.where(iota((LANES, LANES), 0) <= iota((LANES, LANES), 1), 1.0, 0.0).astype(bf16)
    counted = dot(jnp.concatenate(hots, axis=0), upper)
    before = jnp.zeros((64, 1), f32)
    places = []
    for i in range(CHUNKS):
        here = counted[i * 64 : (i + 1) * 64]
        places.append(jnp.sum(hots[i].astype(f32) * (here + before), axis=0, keepdims=True))
        before = before + here[:, LANES - 1 :]
    place = jnp.concatenate(places, axis=0).astype(jnp.int32) - 1
    lane = (material & 1) * CAP + place
    pair = material >> 1
    slot[...] = pair * LANES + lane
    texels = texel[...]
    block = texels >> 8
    high = (block * 2 + tile[...] + 1).astype(f32)
    low = (texels & 255).astype(f32)
    heading = (direction[...] + 1).astype(f32)
    values = []
    lanes_hot = []
    for i in range(CHUNKS):
        row = slice(i, i + 1)
        val = jnp.concatenate(
            [
                targets[:, i * LANES : (i + 1) * LANES],
                high[row],
                low[row],
                heading[row],
                jnp.zeros((2, LANES), f32),
            ],
            axis=0,
        )
        parts = [jnp.where(pair[row] == g, val, 0.0) for g in range(32)]
        values.append(jnp.concatenate(parts, axis=0).astype(bf16))
        lanes_hot.append(hot(lane[row], LANES))
    out = dot_nt(jnp.concatenate(values, axis=1), jnp.concatenate(lanes_hot, axis=1)).astype(bf16)
    own = latents[...].astype(bf16)
    for j in range(N_EXP):
        send[j, :TEX_ROWS] = own
        send[j, TEX_ROWS:] = out[j * 16 : (j + 1) * 16]


def experts_kernel(recv, w_one, w_one_t, w_two, w_two_t, w_three, w_three_t, dir_t, back, grads, tex, acc):
    for b in range(8):
        for h in range(2):
            tex[b * TEX_ROWS : (b + 1) * TEX_ROWS, h * LANES : (h + 1) * LANES] = recv[2 * b + h, :TEX_ROWS]
    acc[...] = jnp.zeros(acc.shape, f32)
    left = iota((8, LANES), 1) < CAP
    for h in range(2):
        sides = ([], [])
        for j in range(N_EXP // 2):
            first = recv[2 * j, TEX_ROWS + 8 * h : TEX_ROWS + 8 * h + 8].astype(f32)
            second = recv[2 * j + 1, TEX_ROWS + 8 * h : TEX_ROWS + 8 * h + 8].astype(f32)
            sides[0].append(jnp.where(left, first, pltpu.roll(second, CAP, 1)))
            sides[1].append(jnp.where(left, pltpu.roll(first, CAP, 1), second))
        preds = []
        for b in range(2):
            e = 2 * h + b
            rows = jnp.concatenate(sides[b], axis=1)
            group = rows[3:4].astype(jnp.int32)
            low_hot = hot(rows[4:5].astype(jnp.int32), 256)
            dir_hot = hot(rows[5:6].astype(jnp.int32), 256, 1)
            picked = dot(tex[...], low_hot)
            lat = jnp.zeros((LAT, SLOTS), f32)
            for r in range(GROUPS):
                lat = lat + jnp.where(group == r + 1, picked[r * LAT : (r + 1) * LAT], 0.0)
            x = jnp.concatenate([lat, dot(dir_t[...], dir_hot)], axis=0).astype(bf16)
            pre_one = dot(w_one_t[e], x)
            sig_one = 0.5 * jnp.tanh(0.5 * pre_one) + 0.5
            raw_one = pre_one * sig_one
            act_one = raw_one.astype(bf16)
            slope_one = sig_one + raw_one * (1.0 - sig_one)
            pre_two = dot(w_two_t[e], act_one)
            sig_two = 0.5 * jnp.tanh(0.5 * pre_two) + 0.5
            raw_two = pre_two * sig_two
            act_two = raw_two.astype(bf16)
            slope_two = sig_two + raw_two * (1.0 - sig_two)
            pred = dot(w_three[e], act_two)
            preds.append(pred)
            misfit = jnp.where(iota((8, SLOTS), 0) < OUTC, pred - rows, 0.0).astype(bf16)
            delta_two = (dot(w_three_t[e], misfit) * slope_two).astype(bf16)
            delta_one = (dot(w_two[e], delta_two) * slope_one).astype(bf16)
            grad_three = dot_nt(misfit, act_two).astype(bf16)
            grad_two = dot_nt(act_one, delta_two).astype(bf16)
            grad_one = dot_nt(x, delta_one).astype(bf16)
            for q in range(4):
                for s in range(2):
                    cols = slice(s * LANES, (s + 1) * LANES)
                    grads[4 * e + q, s * 64 : (s + 1) * 64] = grad_two[q * 64 : (q + 1) * 64, cols]
                    grads[4 * e + q, 128 + s * 16 : 128 + (s + 1) * 16] = grad_one[q * 16 : (q + 1) * 16, cols]
                grads[4 * e + q, 160:168] = grad_three[:, (q % 2) * LANES : (q % 2 + 1) * LANES]
            rows_back = dot(w_one[e, :LAT], delta_one)
            spread = [jnp.where(group == r + 1, rows_back, 0.0).astype(bf16) for r in range(GROUPS)]
            acc[...] += dot_nt(jnp.concatenate(spread, axis=0), low_hot)
        for j in range(N_EXP // 2):
            one = preds[0][:, j * LANES : (j + 1) * LANES]
            two = preds[1][:, j * LANES : (j + 1) * LANES]
            back[2 * j, TEX_ROWS + 8 * h : TEX_ROWS + 8 * h + 8] = jnp.where(
                left, one, pltpu.roll(two, CAP, 1)
            ).astype(bf16)
            back[2 * j + 1, TEX_ROWS + 8 * h : TEX_ROWS + 8 * h + 8] = jnp.where(
                left, pltpu.roll(one, CAP, 1), two
            ).astype(bf16)
    for b in range(8):
        for h in range(2):
            back[2 * b + h, :TEX_ROWS] = acc[
                b * TEX_ROWS : (b + 1) * TEX_ROWS, h * LANES : (h + 1) * LANES
            ].astype(bf16)


def finish_kernel(got, slot, latents, mean, square, new_latents, new_mean, new_square, predictions):
    texel_grad = jnp.zeros((TEX_ROWS, LANES), f32)
    for j in range(N_EXP):
        texel_grad = texel_grad + got[j, :TEX_ROWS].astype(f32)
    next_mean = decay_one * mean[...] + (1.0 - decay_one) * texel_grad
    next_square = decay_two * square[...] + (1.0 - decay_two) * texel_grad * texel_grad
    new_mean[...] = next_mean
    new_square[...] = next_square
    new_latents[...] = latents[...] - step_rate * next_mean / (jnp.sqrt(next_square) + epsilon)
    table = jnp.concatenate([got[j, TEX_ROWS:] for j in range(N_EXP)], axis=0)
    place = slot[...]
    lane = place & (LANES - 1)
    pair = place >> 7
    for i in range(CHUNKS):
        row = slice(i, i + 1)
        picked = dot(table, hot(lane[row], LANES))
        total = jnp.zeros((8, LANES), f32)
        for g in range(32):
            total = total + jnp.where(pair[row] == g, picked[g * 8 : (g + 1) * 8], 0.0)
        predictions[:, i * LANES : (i + 1) * LANES] = total[:OUTC]


def unpack_kernel(packed, grad_one, grad_two, grad_three):
    for e in range(4):
        for q in range(4):
            for s in range(2):
                cols = slice(s * LANES, (s + 1) * LANES)
                grad_two[e, q * 64 : (q + 1) * 64, cols] = packed[4 * e + q, s * 64 : (s + 1) * 64].astype(f32)
                grad_one[e, q * 16 : (q + 1) * 16, cols] = packed[
                    4 * e + q, 128 + s * 16 : 128 + (s + 1) * 16
                ].astype(f32)
        for s in range(2):
            grad_three[e, :, s * LANES : (s + 1) * LANES] = packed[4 * e + s, 160:168].astype(f32)[:OUTC]


def call(kernel, outs, scratch=()):
    return pl.pallas_call(
        kernel,
        out_shape=outs,
        scratch_shapes=list(scratch),
        compiler_params=pltpu.CompilerParams(vmem_limit_bytes=48 << 20),
    )


def shape(dims, kind=f32):
    return jax.ShapeDtypeStruct(dims, kind)


def on_device(
    latents,
    latent_mean,
    latent_square,
    weight_one,
    weight_two,
    weight_three,
    dir_table,
    materials,
    tile_ids,
    texel_ids,
    dir_ids,
    targets,
):
    flat = lambda a: a.reshape(TEX_ROWS, LANES)
    rows = lambda a: a.reshape(CHUNKS, LANES)
    send, slot = call(
        route_kernel,
        (shape((N_EXP, SEND_ROWS, LANES), bf16), shape((CHUNKS, LANES), jnp.int32)),
    )(rows(materials), rows(tile_ids), rows(texel_ids), rows(dir_ids), targets, flat(latents))
    recv = lax.all_to_all(send, "exp", 0, 0, tiled=True)
    three = jnp.pad(weight_three, ((0, 0), (0, 8 - OUTC), (0, 0)))
    back, grads = call(
        experts_kernel,
        (shape((N_EXP, SEND_ROWS, LANES), bf16), shape((N_REP, GRAD_ROWS, LANES), bf16)),
        [pltpu.VMEM((GROUPS * LAT, 256), bf16), pltpu.VMEM((GROUPS * LAT, 256), f32)],
    )(
        recv,
        weight_one,
        jnp.swapaxes(weight_one, 1, 2),
        weight_two,
        jnp.swapaxes(weight_two, 1, 2),
        three,
        jnp.swapaxes(three, 1, 2),
        dir_table.T,
    )
    parts = lax.all_to_all(grads, "rep", 0, 0, tiled=True)
    got = lax.all_to_all(back, "exp", 0, 0, tiled=True)
    own = jnp.sum(parts.astype(f32), axis=0).astype(bf16)
    packed = lax.all_gather(own, "rep", axis=0, tiled=False)
    new_latents, new_mean, new_square, predictions = call(
        finish_kernel,
        (shape((TEX_ROWS, LANES)), shape((TEX_ROWS, LANES)), shape((TEX_ROWS, LANES)), shape((OUTC, ROWS))),
    )(got, slot, flat(latents), flat(latent_mean), flat(latent_square))
    grad_one, grad_two, grad_three = call(
        unpack_kernel,
        (shape(weight_one.shape), shape(weight_two.shape), shape(weight_three.shape)),
    )(packed)
    whole = lambda a: a.reshape(latents.shape)
    return (
        whole(new_latents),
        whole(new_mean),
        whole(new_square),
        predictions,
        grad_one,
        grad_two,
        grad_three,
    )


def solution(mesh):
    in_specs = (
        P("rep", None, "exp"),
        P("rep", None, "exp"),
        P("rep", None, "exp"),
        P("exp", None, None),
        P("exp", None, None),
        P("exp", None, None),
        P(),
        P(("rep", "exp"), None),
        P(("rep", "exp")),
        P(("rep", "exp")),
        P(("rep", "exp")),
        P(None, ("rep", "exp")),
    )
    out_specs = (
        P("rep", None, "exp"),
        P("rep", None, "exp"),
        P("rep", None, "exp"),
        P(None, ("rep", "exp")),
        P("exp", None, None),
        P("exp", None, None),
        P("exp", None, None),
    )
    return jax.shard_map(on_device, mesh=mesh, in_specs=in_specs, out_specs=out_specs, check_vma=False)
```

time: 250 us -> 94.4 us (0.38)
  waiting for transfers between devices: 81 us -> 26.6 us
  local copies, waits for them, and re-layouts: 53.9 us -> 6.21 us
  other arithmetic: 43.9 us -> 0.1 us
  blocking collectives: 0 us -> 26.9 us
  matrix products: 20.1 us -> 0 us
  starting transfers between devices: 34.8 us -> 19.6 us
  between operations: 14.6 us -> 0.74 us
  Pallas kernels: 0 us -> 13.6 us
    psum x1 -> x0, waiting for transfers between devices: 72 us -> none  [together(): so_far = lax.psum(jnp.concatenate([a.ravel() for a in arrays]), axis)]
    dot_general x37 -> x0, matrix products: 20.1 us -> none  [the longest x4 4.09 us: expert_step(): pre_one = jnp.dot(inputs, layer_one, preferred_element_type=jnp.float32)]
    unnamed x4 -> x0, other arithmetic: 19 us -> none
    another operation x2 -> x0, other arithmetic: 18.3 us -> none
    all_to_all x6 -> x2, waiting for transfers between devices: 8.97 us -> 26.6 us  [the longest x1 19.4 us: on_device(): parts = lax.all_to_all(grads, 'rep', 0, 0, tiled=True)]
    gather x3 -> x0, local copies, waits for them, and re-layouts: 16.8 us -> none  [the longest x2 11.3 us: on_device(): sample_latent = texture[tile_ids, :, texel_ids]]
    all_gather x0 -> x1, blocking collectives: none -> 16.4 us  [on_device(): packed = lax.all_gather(own, 'rep', axis=0, tiled=False)]
    all_to_all x6 -> x2, starting transfers between devices: 34.7 us -> 19.6 us  [the longest x1 11.9 us: on_device(): parts = lax.all_to_all(grads, 'rep', 0, 0, tiled=True)]
  transfers between devices with their start and end apart: 7 -> 2, of which waited for: 3 -> 2; matrix products, arithmetic and copies ran while one was open for 37% -> 1% of each run, Pallas kernels for 0% -> 1%
where the time goes in v1:
time: 94.4 us; the launch traced here: 93.6 us
  blocking collectives  26.9 us (28%)
  waiting for transfers between devices  26.6 us (28%)
  starting transfers between devices  19.6 us (21%)
  Pallas kernels  13.6 us (14%)
  local copies, waits for them, and re-layouts  6.21 us (7%)
    all_to_all x1, waiting for transfers between devices, on_device(): parts = lax.all_to_all(grads, 'rep', 0, 0, tiled=True)  19.4 us
    all_gather x1, blocking collectives, on_device(): packed = lax.all_gather(own, 'rep', axis=0, tiled=False)  16.4 us
    all_to_all x1, starting transfers between devices, on_device(): parts = lax.all_to_all(grads, 'rep', 0, 0, tiled=True)  11.9 us
    all_to_all x1, blocking collectives, on_device(): got = lax.all_to_all(back, 'exp', 0, 0, tiled=True)  10.5 us
    pallas_call x1, Pallas kernels, on_device(): call(experts_kernel, (shape((N_EXP, SEND_ROWS, LANES), bf16), shape((N_RE...  9.69 us
    all_to_all x1, starting transfers between devices, on_device(): recv = lax.all_to_all(send, 'exp', 0, 0, tiled=True)  7.72 us
    all_to_all x1, waiting for transfers between devices, on_device(): recv = lax.all_to_all(send, 'exp', 0, 0, tiled=True)  7.12 us
    unnamed x31, local copies, waits for them, and re-layouts  6.14 us
  transfers between devices with their start and end apart: 2, of which 2 were waited for; matrix products, arithmetic and copies ran while one was open for 1% of the time, Pallas kernels for 1%

profile of v1, /device:TPU:1, one launch (start us, length us, event | category | flops | bytes accessed | tf_op | source)
XLA Modules:
  0.0 93.6 jit_solution(892394773316730044)
XLA Ops:
  0.6 0.0 copy-start.8
  0.6 0.7 copy-done.8
  1.3 0.8 copy-done.2
  2.1 0.8 copy-done.4
  2.9 0.7 copy-done.9
  3.5 0.7 copy-done.10
  4.2 0.7 copy-done.11
  4.9 1.6 %shard_map.171 = (bf16[16,80,128]{2,1,0:T(8,128)(2,1)}, s32[16,128]{1,0:T(8,128)S(1)}) custom-call(s32[16,128]{1,0:T(8,128)S(1)} %bitcast.24, s32[16,128]{1,0:T(8,128)S(1)} %bitcast.25, s32[16,128]{1,0:T(8,128)S(1)} %bitcast.26, s32[16,128]{1,0:T(8,128)S(1)} %bitcast.27, f32[3,2048]{1,0:T(4,128)S(1)} %copy-done.4, f32[64,128]{1,0:T(8,128)S(1)} %bitcast.19), custom_call_target="tpu_custom_call" | custom-call | tf_op jit(solution)/shard_map/pallas_call | solution.py:225
  6.5 7.7 %all-to-all-start = ((bf16[16,80,128]{2,1,0:T(8,128)(2,1)}), bf16[16,80,128]{2,1,0:T(8,128)(2,1)S(1)}, u32[]{:S(2)}, u32[]{:S(2)}) async-start(bf16[16,80,128]{2,1,0:T(8,128)(2,1)} %get-tuple-element.18), calls=%async_computation | async-start | bytes 655360 | tf_op jit(solution)/shard_map/all_to_all | solution.py:229
  14.2 0.0 copy-done.12
  14.2 0.0 copy-start
  14.3 0.2 copy.21
  14.5 0.2 copy.24
  14.6 0.0 copy-done.1
  14.7 0.2 copy.19
  14.8 0.5 copy-done
  15.3 0.2 copy.20
  15.5 0.0 copy-start.7
  15.5 0.1 pad_bitcast_fusion.w_three_t
  15.6 7.1 %all-to-all-done.recv = bf16[16,80,128]{2,1,0:T(8,128)(2,1)S(1)} async-done(((bf16[16,80,128]{2,1,0:T(8,128)(2,1)}), bf16[16,80,128]{2,1,0:T(8,128)(2,1)S(1)}, u32[]{:S(2)}, u32[]{:S(2)}) %all-to-all-start) | async-done | bytes 327712 | tf_op jit(solution)/shard_map/all_to_all | solution.py:229
  22.7 0.0 copy-done.7
  22.7 9.7 %shard_map.172 = (bf16[16,80,128]{2,1,0:T(8,128)(2,1)S(1)}, bf16[16,168,128]{2,1,0:T(8,128)(2,1)}) custom-call(bf16[16,80,128]{2,1,0:T(8,128)(2,1)S(1)} %all-to-all-done.recv, bf16[4,64,256]{2,1,0:T(8,128)(2,1)S(1)} %copy-done.1, bf16[4,256,64]{2,1,0:T(8,128)(2,1)S(1)} %bitcast.18, bf16[4,256,256]{2,1,0:T(8,128)(2,1)S(1)} %copy-done, ...), custom_call_target="tpu_custom_call" | custom-call | tf_op jit(solution)/shard_map/pallas_call | solution.py:231
  32.4 10.5 %all_to_all.15.got = bf16[16,80,128]{2,1,0:T(8,128)(2,1)S(1)} all-to-all(bf16[16,80,128]{2,1,0:T(8,128)(2,1)S(1)} %get-tuple-element.19), channel_id=1, replica_groups=mesh['rep'=16,'exp'=16] {'exp'}, dimensions={0} | all-to-all | bytes 655360 | tf_op jit(solution)/shard_map/all_to_all | solution.py:246
  42.9 11.9 %all-to-all-start.2 = ((bf16[16,168,128]{2,1,0:T(8,128)(2,1)}), bf16[16,168,128]{2,1,0:T(8,128)(2,1)S(1)}, u32[]{:S(2)}, u32[]{:S(2)}) async-start(bf16[16,168,128]{2,1,0:T(8,128)(2,1)} %get-tuple-element.25), calls=%async_computation.2 | async-start | bytes 1376256 | tf_op jit(solution)/shard_map/all_to_all | solution.py:245
  54.8 0.0 copy-done.3
  54.8 0.0 copy-done.5
  54.8 1.2 %shard_map.173 = (f32[64,128]{1,0:T(8,128)}, f32[64,128]{1,0:T(8,128)}, f32[64,128]{1,0:T(8,128)}, f32[3,2048]{1,0:T(4,128)}) custom-call(bf16[16,80,128]{2,1,0:T(8,128)(2,1)S(1)} %all_to_all.15.got, s32[16,128]{1,0:T(8,128)S(1)} %get-tuple-element.20.slot, f32[64,128]{1,0:T(8,128)S(1)} %bitcast.20, f32[64,128]{1,0:T(8,128)S(1)} %bitcast.21, ...), custom_call_target="tpu_custom_call" | custom-call | tf_op jit(solution)/shard_map/pallas_call | solution.py:249
  56.0 19.4 %all-to-all-done.2 = bf16[16,168,128]{2,1,0:T(8,128)(2,1)S(1)} async-done(((bf16[16,168,128]{2,1,0:T(8,128)(2,1)}), bf16[16,168,128]{2,1,0:T(8,128)(2,1)S(1)}, u32[]{:S(2)}, u32[]{:S(2)}) %all-to-all-start.2) | async-done | bytes 688160 | tf_op jit(solution)/shard_map/all_to_all | solution.py:245
  75.4 0.1 reduce_sum.12
  75.5 16.4 %all-gather = bf16[2688,128]{1,0:T(8,128)(2,1)S(1)} all-gather(bf16[168,128]{1,0:T(8,128)(2,1)S(1)} %reduce_sum.12), channel_id=2, replica_groups=mesh['rep'=16,'exp'=16] {'rep'}, dimensions={0}, use_global_device_ids=true | all-gather | bytes 731136 | tf_op jit(solution)/shard_map/all_gather | solution.py:248
  91.9 1.1 %shard_map.174 = (f32[4,64,256]{2,1,0:T(8,128)}, f32[4,256,256]{2,1,0:T(8,128)}, f32[4,3,256]{2,1,0:T(4,128)S(1)}) custom-call(bf16[16,168,128]{2,1,0:T(8,128)(2,1)S(1)} %bitcast.16), custom_call_target="tpu_custom_call" | custom-call | tf_op jit(solution)/shard_map/pallas_call | solution.py:253
  93.0 0.6 copy.23
  (12 shorter events, 0.0 us)
Async XLA Ops:
  0.6 0.7 copy-start.8
  1.3 0.8 copy-start.2
  2.1 0.8 copy-start.4
  2.8 0.7 copy-start.9
  3.5 0.7 copy-start.10
  4.2 0.7 copy-start.11
  6.5 7.7 %copy-start.12 = (bf16[4,3,256]{2,0,1:T(4,128)(2,1)S(1)}, bf16[4,3,256]{2,0,1:T(4,128)(2,1)}, u32[]{:S(2)}) copy-start(bf16[4,3,256]{2,0,1:T(4,128)(2,1)} %param.17) | copy-start | bytes 18436
  6.5 8.1 %copy-start.1 = (bf16[4,64,256]{2,1,0:T(8,128)(2,1)S(1)}, bf16[4,64,256]{2,1,0:T(8,128)(2,1)}, u32[]{:S(2)}) copy-start(bf16[4,64,256]{2,1,0:T(8,128)(2,1)} %w_one.1) | copy-start | bytes 393220
  6.5 16.2 %all-to-all-start = ((bf16[16,80,128]{2,1,0:T(8,128)(2,1)}), bf16[16,80,128]{2,1,0:T(8,128)(2,1)S(1)}, u32[]{:S(2)}, u32[]{:S(2)}) async-start(bf16[16,80,128]{2,1,0:T(8,128)(2,1)} %get-tuple-element.18), calls=%async_computation | async-start | bytes 655360 | tf_op jit(solution)/shard_map/all_to_all | solution.py:229
  14.2 1.0 %copy-start = (bf16[4,256,256]{2,1,0:T(8,128)(2,1)S(1)}, bf16[4,256,256]{2,1,0:T(8,128)(2,1)}, u32[]{:S(2)}) copy-start(bf16[4,256,256]{2,1,0:T(8,128)(2,1)} %w_two.1) | copy-start | bytes 1572868
  15.5 7.2 %copy-start.7 = (bf16[256,32]{0,1:T(8,128)(2,1)S(1)}, bf16[256,32]{0,1:T(8,128)(2,1)}, u32[]{:S(2)}) copy-start(bf16[256,32]{0,1:T(8,128)(2,1)} %param.18) | copy-start | bytes 49156
  42.9 11.9 %copy-start.3 = (f32[2,32,128]{2,1,0:T(8,128)S(1)}, f32[2,32,128]{2,1,0:T(8,128)}, u32[]{:S(2)}) copy-start(f32[2,32,128]{2,1,0:T(8,128)} %param.12) | copy-start | bytes 98308
  42.9 11.9 %copy-start.5 = (f32[2,32,128]{2,1,0:T(8,128)S(1)}, f32[2,32,128]{2,1,0:T(8,128)}, u32[]{:S(2)}) copy-start(f32[2,32,128]{2,1,0:T(8,128)} %param.13) | copy-start | bytes 98308
  42.9 11.9 %copy-start.6 = (f32[2,32,128]{2,1,0:T(8,128)S(1)}, f32[2,32,128]{2,1,0:T(8,128)}, u32[]{:S(2)}) copy-start(f32[2,32,128]{2,1,0:T(8,128)} %param.14) | copy-start | bytes 98308
  42.9 32.5 %all-to-all-start.2 = ((bf16[16,168,128]{2,1,0:T(8,128)(2,1)}), bf16[16,168,128]{2,1,0:T(8,128)(2,1)S(1)}, u32[]{:S(2)}, u32[]{:S(2)}) async-start(bf16[16,168,128]{2,1,0:T(8,128)(2,1)} %get-tuple-element.25), calls=%async_computation.2 | async-start | bytes 1376256 | tf_op jit(solution)/shard_map/all_to_all | solution.py:245

commit v2 on v1

v2 whole, which is shorter than its diff:
```python
import jax
import jax.numpy as jnp
from jax import lax
from jax.experimental import pallas as pl
from jax.experimental.pallas import tpu as pltpu
from jax.sharding import PartitionSpec as P

LAT = 32
HID = 256
OUTC = 3
LANES = 128
N_EXP = 16
N_REP = 16
CAP = 64
ROWS = 2048
CHUNKS = ROWS // LANES
SLOTS = N_EXP * CAP
GROUPS = 16
TEX_ROWS = 64
SEND_ROWS = TEX_ROWS + 16
GRAD_ROWS = 168

decay_one = 0.9
decay_two = 0.99
step_rate = 0.05
epsilon = 1e-08

f32 = jnp.float32
bf16 = jnp.bfloat16


def dot(a, b):
    return jnp.dot(a, b, preferred_element_type=f32)


def dot_nt(a, b):
    return lax.dot_general(a, b, (((1,), (1,)), ((), ())), preferred_element_type=f32)


def iota(shape, dim):
    return lax.broadcasted_iota(jnp.int32, shape, dim)


def hot(index, count, start=0):
    same = iota((count, index.shape[1]), 0) + start == index
    return jnp.where(same, 1.0, 0.0).astype(bf16)


def route_kernel(mat, tile_in, texel_in, direction_in, targets_in, latents_in, send, slot, *scratch):
    material_in, tile, texel, direction, targets, latents, sems = scratch
    copies = [
        pltpu.make_async_copy(source, target, sems.at[n])
        for n, (source, target) in enumerate(
            [
                (mat, material_in),
                (tile_in, tile),
                (texel_in, texel),
                (direction_in, direction),
                (targets_in, targets),
                (latents_in, latents),
            ]
        )
    ]
    for copy in copies:
        copy.start()
    for copy in copies:
        copy.wait()
    material = material_in[...]
    hots = [hot(material[i : i + 1], 64) for i in range(CHUNKS)]
    upper = jnp.where(iota((LANES, LANES), 0) <= iota((LANES, LANES), 1), 1.0, 0.0).astype(bf16)
    counted = dot(jnp.concatenate(hots, axis=0), upper)
    before = jnp.zeros((64, 1), f32)
    places = []
    for i in range(CHUNKS):
        here = counted[i * 64 : (i + 1) * 64]
        places.append(jnp.sum(hots[i].astype(f32) * (here + before), axis=0, keepdims=True))
        before = before + here[:, LANES - 1 :]
    place = jnp.concatenate(places, axis=0).astype(jnp.int32) - 1
    lane = (material & 1) * CAP + place
    pair = material >> 1
    slot[...] = pair * LANES + lane
    texels = texel[...]
    block = texels >> 8
    high = (block * 2 + tile[...] + 1).astype(f32)
    low = (texels & 255).astype(f32)
    heading = (direction[...] + 1).astype(f32)
    values = []
    lanes_hot = []
    for i in range(CHUNKS):
        row = slice(i, i + 1)
        val = jnp.concatenate(
            [
                targets[:, i * LANES : (i + 1) * LANES],
                high[row],
                low[row],
                heading[row],
                jnp.zeros((2, LANES), f32),
            ],
            axis=0,
        )
        parts = [jnp.where(pair[row] == g, val, 0.0) for g in range(32)]
        values.append(jnp.concatenate(parts, axis=0).astype(bf16))
        lanes_hot.append(hot(lane[row], LANES))
    out = dot_nt(jnp.concatenate(values, axis=1), jnp.concatenate(lanes_hot, axis=1)).astype(bf16)
    own = latents[...].astype(bf16)
    for j in range(N_EXP):
        send[j, :TEX_ROWS] = own
        send[j, TEX_ROWS:] = out[j * 16 : (j + 1) * 16]


def half_kernel(
    half, recv, w_one, w_one_t, w_two, w_two_t, w_three, w_three_t, dir_t, grads, back, preds, index, tex
):
    h = half[0]
    for b in range(8):
        for s in range(2):
            tex[b * TEX_ROWS : (b + 1) * TEX_ROWS, s * LANES : (s + 1) * LANES] = recv[2 * b + s, :TEX_ROWS]
    left = iota((8, LANES), 1) < CAP
    sides = ([], [])
    for j in range(N_EXP // 2):
        both = [recv[2 * j + s, TEX_ROWS:].astype(f32) for s in range(2)]
        first, second = [jnp.where(h == 0, v[:8], v[8:]) for v in both]
        sides[0].append(jnp.where(left, first, pltpu.roll(second, CAP, 1)))
        sides[1].append(jnp.where(left, pltpu.roll(first, CAP, 1), second))
    for b in range(2):
        e = 2 * h + b
        rows = jnp.concatenate(sides[b], axis=1)
        index[b] = rows
        group = rows[3:4].astype(jnp.int32)
        low_hot = hot(rows[4:5].astype(jnp.int32), 256)
        dir_hot = hot(rows[5:6].astype(jnp.int32), 256, 1)
        picked = dot(tex[...], low_hot)
        lat = jnp.zeros((LAT, SLOTS), f32)
        for r in range(GROUPS):
            lat = lat + jnp.where(group == r + 1, picked[r * LAT : (r + 1) * LAT], 0.0)
        x = jnp.concatenate([lat, dot(dir_t[...], dir_hot)], axis=0).astype(bf16)
        pre_one = dot(w_one_t[e], x)
        sig_one = 0.5 * jnp.tanh(0.5 * pre_one) + 0.5
        raw_one = pre_one * sig_one
        act_one = raw_one.astype(bf16)
        slope_one = sig_one + raw_one * (1.0 - sig_one)
        pre_two = dot(w_two_t[e], act_one)
        sig_two = 0.5 * jnp.tanh(0.5 * pre_two) + 0.5
        raw_two = pre_two * sig_two
        act_two = raw_two.astype(bf16)
        slope_two = sig_two + raw_two * (1.0 - sig_two)
        pred = dot(w_three[e], act_two)
        preds[b] = pred
        misfit = jnp.where(iota((8, SLOTS), 0) < OUTC, pred - rows, 0.0).astype(bf16)
        delta_two = (dot(w_three_t[e], misfit) * slope_two).astype(bf16)
        delta_one = (dot(w_two[e], delta_two) * slope_one).astype(bf16)
        grad_three = dot_nt(misfit, act_two).astype(grads.dtype)
        grad_two = dot_nt(act_one, delta_two).astype(grads.dtype)
        grad_one = dot_nt(x, delta_one).astype(grads.dtype)
        for q in range(4):
            n = 4 * b + q
            for s in range(2):
                cols = slice(s * LANES, (s + 1) * LANES)
                grads[n, s * 64 : (s + 1) * 64] = grad_two[q * 64 : (q + 1) * 64, cols]
                grads[n, 128 + s * 16 : 128 + (s + 1) * 16] = grad_one[q * 16 : (q + 1) * 16, cols]
            grads[n, 160:168] = grad_three[:, (q % 2) * LANES : (q % 2 + 1) * LANES]
        back[b] = dot(w_one[e, :LAT], delta_one).astype(bf16)


def texels_kernel(half, back_a, back_b, preds_a, preds_b, index_a, index_b, out):
    acc = jnp.zeros((GROUPS * LAT, 256), f32)
    for rows_back, index in ((back_a, index_a), (back_b, index_b)):
        for b in range(2):
            rows = index[b]
            group = rows[3:4].astype(jnp.int32)
            low_hot = hot(rows[4:5].astype(jnp.int32), 256)
            grad = rows_back[b].astype(f32)
            spread = [jnp.where(group == r + 1, grad, 0.0).astype(bf16) for r in range(GROUPS)]
            acc = acc + dot_nt(jnp.concatenate(spread, axis=0), low_hot)
    for b in range(8):
        for s in range(2):
            out[2 * b + s, :TEX_ROWS] = acc[b * TEX_ROWS : (b + 1) * TEX_ROWS, s * LANES : (s + 1) * LANES].astype(bf16)
    left = iota((8, LANES), 1) < CAP
    keep = half[0]
    for j in range(N_EXP // 2):
        cols = slice(j * LANES, (j + 1) * LANES)
        low, high = [], []
        for h in range(2):
            one = jnp.where(keep == h, preds_b[0, :, cols], preds_a[0, :, cols])
            two = jnp.where(keep == h, preds_b[1, :, cols], preds_a[1, :, cols])
            low.append(jnp.where(left, one, pltpu.roll(two, CAP, 1)))
            high.append(jnp.where(left, pltpu.roll(one, CAP, 1), two))
        out[2 * j, TEX_ROWS:] = jnp.concatenate(low, axis=0).astype(bf16)
        out[2 * j + 1, TEX_ROWS:] = jnp.concatenate(high, axis=0).astype(bf16)


def finish_kernel(got, slot, latents, mean, square, new_latents, new_mean, new_square, predictions):
    texel_grad = jnp.zeros((TEX_ROWS, LANES), f32)
    for j in range(N_EXP):
        texel_grad = texel_grad + got[j, :TEX_ROWS].astype(f32)
    next_mean = decay_one * mean[...] + (1.0 - decay_one) * texel_grad
    next_square = decay_two * square[...] + (1.0 - decay_two) * texel_grad * texel_grad
    new_mean[...] = next_mean
    new_square[...] = next_square
    new_latents[...] = latents[...] - step_rate * next_mean / (jnp.sqrt(next_square) + epsilon)
    table = jnp.concatenate([got[j, TEX_ROWS:] for j in range(N_EXP)], axis=0)
    place = slot[...]
    lane = place & (LANES - 1)
    pair = place >> 7
    for i in range(CHUNKS):
        row = slice(i, i + 1)
        picked = dot(table, hot(lane[row], LANES))
        total = jnp.zeros((8, LANES), f32)
        for g in range(32):
            total = total + jnp.where(pair[row] == g, picked[g * 8 : (g + 1) * 8], 0.0)
        predictions[:, i * LANES : (i + 1) * LANES] = total[:OUTC]


def unpack_kernel(packed, grad_one, grad_two, grad_three):
    for e in range(4):
        for q in range(4):
            n = 2 * (4 * (e % 2) + q) + e // 2
            for s in range(2):
                cols = slice(s * LANES, (s + 1) * LANES)
                grad_two[e, q * 64 : (q + 1) * 64, cols] = packed[n, s * 64 : (s + 1) * 64].astype(f32)
                grad_one[e, q * 16 : (q + 1) * 16, cols] = packed[n, 128 + s * 16 : 128 + (s + 1) * 16].astype(f32)
            if q < 2:
                for c in range(OUTC):
                    grad_three[c, e : e + 1, q * LANES : (q + 1) * LANES] = packed[n, 160:168].astype(f32)[c : c + 1]


def call(kernel, outs, scratch=(), in_specs=None, flops=0):
    more = {} if in_specs is None else {"in_specs": in_specs}
    cost = pl.CostEstimate(flops=flops, transcendentals=0, bytes_accessed=0) if flops else None
    return pl.pallas_call(
        kernel,
        out_shape=outs,
        scratch_shapes=list(scratch),
        compiler_params=pltpu.CompilerParams(vmem_limit_bytes=48 << 20),
        cost_estimate=cost,
        **more,
    )


def shape(dims, kind=f32):
    return jax.ShapeDtypeStruct(dims, kind)


def on_device(
    latents,
    latent_mean,
    latent_square,
    weight_one,
    weight_two,
    weight_three,
    dir_table,
    materials,
    tile_ids,
    texel_ids,
    dir_ids,
    targets,
):
    flat = lambda a: a.reshape(TEX_ROWS, LANES)
    rows = lambda a: a.reshape(CHUNKS, LANES)
    hbm = pl.BlockSpec(memory_space=pltpu.HBM)
    vmem = pl.BlockSpec(memory_space=pltpu.VMEM)
    smem = pl.BlockSpec(memory_space=pltpu.SMEM)
    index_rows = pltpu.VMEM((CHUNKS, LANES), jnp.int32)
    send, slot = call(
        route_kernel,
        (shape((N_EXP, SEND_ROWS, LANES), bf16), shape((CHUNKS, LANES), jnp.int32)),
        [index_rows] * 4
        + [pltpu.VMEM((OUTC, ROWS), f32), pltpu.VMEM((TEX_ROWS, LANES), f32), pltpu.SemaphoreType.DMA((6,))],
        [hbm] * 6,
    )(*[
        pltpu.with_memory_space_constraint(a, pltpu.HBM)
        for a in (rows(materials), rows(tile_ids), rows(texel_ids), rows(dir_ids), targets, flat(latents))
    ])
    recv = lax.all_to_all(send, "exp", 0, 0, tiled=True)
    three = jnp.pad(weight_three, ((0, 0), (0, 8 - OUTC), (0, 0)))
    weights = (
        weight_one,
        jnp.swapaxes(weight_one, 1, 2),
        weight_two,
        jnp.swapaxes(weight_two, 1, 2),
        three,
        jnp.swapaxes(three, 1, 2),
        dir_table.T,
    )
    core = (lax.axis_index("rep") % 2).astype(jnp.int32).reshape(1)
    half = lambda kind: call(
        half_kernel,
        (
            shape((N_REP // 2, GRAD_ROWS, LANES), kind),
            shape((2, LAT, SLOTS), bf16),
            shape((2, 8, SLOTS)),
            shape((2, 8, SLOTS)),
        ),
        [pltpu.VMEM((GROUPS * LAT, 256), bf16)],
        [smem] + [vmem] * 8,
        2000000000,
    )
    grads_a, back_a, preds_a, index_a = half(bf16)(1 - core, recv, *weights)
    from_core = lax.ppermute(grads_a, "rep", [(i, i ^ 1) for i in range(N_REP)])
    grads_b, back_b, preds_b, index_b = half(f32)(core, recv, *weights)
    chip = (grads_b + from_core.astype(f32)).astype(bf16)
    chips = [list(range(c, N_REP, 2)) for c in range(2)]
    parts = lax.all_to_all(chip, "rep", 0, 0, tiled=True, axis_index_groups=chips)
    back = call(
        texels_kernel,
        shape((N_EXP, SEND_ROWS, LANES), bf16),
        (),
        [smem] + [vmem] * 6,
        2000000000,
    )(core, back_a, back_b, preds_a, preds_b, index_a, index_b)
    own = jnp.sum(parts.astype(f32), axis=0).astype(bf16)
    back, own = lax.optimization_barrier((back, own))
    got = lax.all_to_all(back, "exp", 0, 0, tiled=True)
    packed = lax.all_gather(own, "rep", axis=0, tiled=False)
    new_latents, new_mean, new_square, predictions = call(
        finish_kernel,
        (shape((TEX_ROWS, LANES)), shape((TEX_ROWS, LANES)), shape((TEX_ROWS, LANES)), shape((OUTC, ROWS))),
    )(got, slot, flat(latents), flat(latent_mean), flat(latent_square))
    grad_one, grad_two, grad_three = call(
        unpack_kernel,
        (shape(weight_one.shape), shape(weight_two.shape), shape((OUTC, 4, HID))),
    )(packed)
    grad_three = jnp.swapaxes(grad_three, 0, 1)
    whole = lambda a: a.reshape(latents.shape)
    return (
        whole(new_latents),
        whole(new_mean),
        whole(new_square),
        predictions,
        grad_one,
        grad_two,
        grad_three,
    )


def solution(mesh):
    in_specs = (
        P("rep", None, "exp"),
        P("rep", None, "exp"),
        P("rep", None, "exp"),
        P("exp", None, None),
        P("exp", None, None),
        P("exp", None, None),
        P(),
        P(("rep", "exp"), None),
        P(("rep", "exp")),
        P(("rep", "exp")),
        P(("rep", "exp")),
        P(None, ("rep", "exp")),
    )
    out_specs = (
        P("rep", None, "exp"),
        P("rep", None, "exp"),
        P("rep", None, "exp"),
        P(None, ("rep", "exp")),
        P("exp", None, None),
        P("exp", None, None),
        P("exp", None, None),
    )
    return jax.shard_map(on_device, mesh=mesh, in_specs=in_specs, out_specs=out_specs, check_vma=False)
```

time: 94.4 us -> 75.5 us (0.80)
  blocking collectives: 26.9 us -> 16.9 us
  waiting for transfers between devices: 26.6 us -> 19.2 us
  local copies, waits for them, and re-layouts: 6.21 us -> 1.3 us
  starting transfers between devices: 19.6 us -> 21.4 us
  Pallas kernels: 13.6 us -> 14.6 us
    all_to_all x1 -> x0, blocking collectives: 10.5 us -> none  [on_device(): got = lax.all_to_all(back, 'exp', 0, 0, tiled=True)]
    all_to_all x1 -> x2, waiting for transfers between devices: 19.4 us -> 12.1 us  [the longest x1 12.1 us: on_device(): lax.all_to_all(chip, 'rep', 0, 0, tiled=True, axis_index_groups=chips)]
    unnamed x31 -> x18, local copies, waits for them, and re-layouts: 6.14 us -> 1.24 us
    ppermute x0 -> x1, starting transfers between devices: none -> 1.96 us  [on_device(): from_core = lax.ppermute(grads_a, 'rep', [(i, i ^ 1) for i in range(N_REP)])]
    all_to_all x1 -> x2, starting transfers between devices: 11.9 us -> 11.7 us  [the longest x1 8.18 us: on_device(): lax.all_to_all(chip, 'rep', 0, 0, tiled=True, axis_index_groups=chips)]
    pallas_call x1 -> x3, Pallas kernels: 9.69 us -> 9.8 us  [the longest x1 3.89 us: on_device(): grads_b, back_b, preds_b, index_b = half(f32)(core, recv, *weights)]
  transfers between devices with their start and end apart: 2 -> 4, of which waited for: 2 -> 2; matrix products, arithmetic and copies ran while one was open for 1% -> 1% of each run, Pallas kernels for 1% -> 9%
where the time goes in v2:
time: 75.5 us; the launch traced here: 75 us
  starting transfers between devices  21.4 us (28%)
  waiting for transfers between devices  19.2 us (25%)
  blocking collectives  16.9 us (22%)
  Pallas kernels  14.6 us (19%)
  local copies, waits for them, and re-layouts  1.3 us (2%)
  other arithmetic  0.85 us (1%)
  between operations  0.78 us (1%)
    all_gather x1, blocking collectives, on_device(): packed = lax.all_gather(own, 'rep', axis=0, tiled=False)  16.9 us
    all_to_all x1, waiting for transfers between devices, on_device(): lax.all_to_all(chip, 'rep', 0, 0, tiled=True, axis_index_groups=chips)  12.1 us
    all_to_all x1, starting transfers between devices, on_device(): lax.all_to_all(chip, 'rep', 0, 0, tiled=True, axis_index_groups=chips)  8.18 us
    all_to_all x1, starting transfers between devices, on_device(): recv = lax.all_to_all(send, 'exp', 0, 0, tiled=True)  7.73 us
    all_to_all x1, waiting for transfers between devices, on_device(): recv = lax.all_to_all(send, 'exp', 0, 0, tiled=True)  7.13 us
    pallas_call x1, Pallas kernels, on_device(): grads_b, back_b, preds_b, index_b = half(f32)(core, recv, *weights)  3.89 us
    pallas_call x1, Pallas kernels, on_device(): grads_a, back_a, preds_a, index_a = half(bf16)(1 - core, recv, *weights)  3.89 us
    all_to_all x1, starting transfers between devices, on_device(): got = lax.all_to_all(back, 'exp', 0, 0, tiled=True)  3.55 us
  transfers between devices with their start and end apart: 4, of which 2 were waited for; matrix products, arithmetic and copies ran while one was open for 1% of the time, Pallas kernels for 9%

profile of v2, /device:TPU:1, one launch (start us, length us, event | category | flops | bytes accessed | tf_op | source)
XLA Modules:
  0.0 75.0 jit_solution(15737490897986619833)
XLA Ops:
  0.6 2.5 %shard_map.171 = (bf16[16,80,128]{2,1,0:T(8,128)(2,1)}, s32[16,128]{1,0:T(8,128)S(1)}) custom-call(s32[16,128]{1,0:T(8,128)} %bitcast.29, s32[16,128]{1,0:T(8,128)} %bitcast.30, s32[16,128]{1,0:T(8,128)} %bitcast.31, s32[16,128]{1,0:T(8,128)} %bitcast.32, f32[3,2048]{1,0:T(4,128)} %targets_in.1, f32[64,128]{1,0:T(8,128)} %bitcast.23), custom_call_target="tpu_custom_call" | custom-call | tf_op jit(solution)/shard_map/pallas_call | solution.py:264
  3.1 0.0 copy-start.6
  3.1 0.0 copy-start.1
  3.1 7.7 %all-to-all-start = ((bf16[16,80,128]{2,1,0:T(8,128)(2,1)}), bf16[16,80,128]{2,1,0:T(8,128)(2,1)S(1)}, u32[]{:S(2)}, u32[]{:S(2)}) async-start(bf16[16,80,128]{2,1,0:T(8,128)(2,1)} %get-tuple-element.26), calls=%async_computation | async-start | bytes 655360 | tf_op jit(solution)/shard_map/all_to_all | solution.py:274
  10.9 0.0 copy-start
  10.9 0.0 copy-done.6
  10.9 0.2 copy.21
  11.1 0.2 copy.24
  11.3 0.0 copy-done.1
  11.3 0.2 copy.19
  11.5 0.4 copy-done
  11.9 0.2 copy.20
  12.1 0.0 copy-start.5
  12.1 0.1 pad_bitcast_fusion.w_three_t
  12.2 7.1 %all-to-all-done.recv = bf16[16,80,128]{2,1,0:T(8,128)(2,1)S(1)} async-done(((bf16[16,80,128]{2,1,0:T(8,128)(2,1)}), bf16[16,80,128]{2,1,0:T(8,128)(2,1)S(1)}, u32[]{:S(2)}, u32[]{:S(2)}) %all-to-all-start) | async-done | bytes 327712 | tf_op jit(solution)/shard_map/all_to_all | solution.py:274
  19.3 0.0 copy-done.5
  19.3 3.9 %shard_map.172 = (bf16[8,168,128]{2,1,0:T(8,128)(2,1)S(1)}, bf16[2,32,1024]{2,1,0:T(8,128)(2,1)S(1)}, f32[2,8,1024]{2,1,0:T(8,128)S(1)}, f32[2,8,1024]{2,1,0:T(8,128)S(1)}) custom-call(s32[1]{0:T(128)S(6)} %sub.3.half, bf16[16,80,128]{2,1,0:T(8,128)(2,1)S(1)} %all-to-all-done.recv, bf16[4,64,256]{2,1,0:T(8,128)(2,1)S(1)} %copy-done.1, ...), custom_call_target="tpu_custom_call" | custom-call | flops 2000000000 | tf_op jit(solution)/shard_map/pallas_call | solution.py:298
  23.2 2.0 %collective-permute-start = (bf16[8,168,128]{2,1,0:T(8,128)(2,1)S(1)}, bf16[8,168,128]{2,1,0:T(8,128)(2,1)S(1)}, u32[]{:S(2)}, u32[]{:S(2)}) collective-permute-start(bf16[8,168,128]{2,1,0:T(8,128)(2,1)S(1)} %get-tuple-element.34), channel_id=1, source_target_pairs={{0,16},{16,0},{32,48},{48,32},{64,80},{80,64},{96,112},{112,96},{1... | collective-permute-start | bytes 1032200 | tf_op jit(solution)/shard_map/ppermute | solution.py:299
  25.2 3.9 %shard_map.173 = (f32[8,168,128]{2,1,0:T(8,128)S(1)}, bf16[2,32,1024]{2,1,0:T(8,128)(2,1)S(1)}, f32[2,8,1024]{2,1,0:T(8,128)S(1)}, f32[2,8,1024]{2,1,0:T(8,128)S(1)}) custom-call(s32[1]{0:T(128)} %bitcast.half, bf16[16,80,128]{2,1,0:T(8,128)(2,1)S(1)} %all-to-all-done.recv, bf16[4,64,256]{2,1,0:T(8,128)(2,1)S(1)} %copy-done.1, ...), custom_call_target="tpu_custom_call" | custom-call | flops 2000000000 | tf_op jit(solution)/shard_map/pallas_call | solution.py:300
  29.1 0.0 collective-permute-done
  29.1 0.8 %add_convert_fusion = bf16[8,168,128]{2,1,0:T(8,128)(2,1)} fusion(f32[8,168,128]{2,1,0:T(8,128)S(1)} %get-tuple-element.33, bf16[8,168,128]{2,1,0:T(8,128)(2,1)S(1)} %collective-permute-done), kind=kLoop, calls=%fused_computation | loop fusion | flops 516096 | bytes 1376256 | tf_op jit(solution)/shard_map/convert_element_type | solution.py:301
  29.9 8.2 %all-to-all-start.1 = ((bf16[8,168,128]{2,1,0:T(8,128)(2,1)}), bf16[8,168,128]{2,1,0:T(8,128)(2,1)S(1)}, u32[]{:S(2)}, u32[]{:S(2)}) async-start(bf16[8,168,128]{2,1,0:T(8,128)(2,1)} %add_convert_fusion), calls=%async_computation.1 | async-start | bytes 688128 | tf_op jit(solution)/shard_map/all_to_all | solution.py:303
  38.1 2.0 %shard_map.174 = bf16[16,80,128]{2,1,0:T(8,128)(2,1)} custom-call(s32[1]{0:T(128)} %bitcast.half, bf16[2,32,1024]{2,1,0:T(8,128)(2,1)S(1)} %get-tuple-element.27.back_a, bf16[2,32,1024]{2,1,0:T(8,128)(2,1)S(1)} %get-tuple-element.28.back_b, f32[2,8,1024]{2,1,0:T(8,128)S(1)} %get-tuple-element.29.preds_a, f32[2,8,1024]{2,1,0:T(8,128)S(1)} %get-tuple-element.30.preds_b, ...), custom_call_target="tpu_custom_call" | custom-call | flops 2000000000 | tf_op jit(solution)/shard_map/pallas_call | solution.py:304
  40.1 12.1 %all-to-all-done.1 = bf16[8,168,128]{2,1,0:T(8,128)(2,1)S(1)} async-done(((bf16[8,168,128]{2,1,0:T(8,128)(2,1)}), bf16[8,168,128]{2,1,0:T(8,128)(2,1)S(1)}, u32[]{:S(2)}, u32[]{:S(2)}) %all-to-all-start.1) | async-done | bytes 344096 | tf_op jit(solution)/shard_map/all_to_all | solution.py:303
  52.2 0.1 reduce_sum.12
  52.2 3.6 %all-to-all-start.2 = ((bf16[16,80,128]{2,1,0:T(8,128)(2,1)}), bf16[16,80,128]{2,1,0:T(8,128)(2,1)S(1)}, u32[]{:S(2)}, u32[]{:S(2)}) async-start(bf16[16,80,128]{2,1,0:T(8,128)(2,1)} %shard_map.174), calls=%async_computation.2 | async-start | bytes 655360 | tf_op jit(solution)/shard_map/all_to_all | solution.py:313
  55.8 16.9 %all-gather = bf16[2688,128]{1,0:T(8,128)(2,1)S(1)} all-gather(bf16[168,128]{1,0:T(8,128)(2,1)S(1)} %reduce_sum.12), channel_id=2, replica_groups=mesh['rep'=16,'exp'=16] {'rep'}, dimensions={0}, use_global_device_ids=true | all-gather | bytes 731136 | tf_op jit(solution)/shard_map/all_gather | solution.py:314
  72.7 1.1 %shard_map.176 = (f32[4,64,256]{2,1,0:T(8,128)}, f32[4,256,256]{2,1,0:T(8,128)}, f32[3,4,256]{2,1,0:T(4,128)}) custom-call(bf16[16,168,128]{2,1,0:T(8,128)(2,1)S(1)} %bitcast.18), custom_call_target="tpu_custom_call" | custom-call | tf_op jit(solution)/shard_map/pallas_call | solution.py:319
  73.8 0.0 all-to-all-done.2.got
  73.8 0.0 copy-done.2
  73.8 0.0 copy-done.3
  73.8 1.2 %shard_map.175 = (f32[64,128]{1,0:T(8,128)}, f32[64,128]{1,0:T(8,128)}, f32[64,128]{1,0:T(8,128)}, f32[3,2048]{1,0:T(4,128)}) custom-call(bf16[16,80,128]{2,1,0:T(8,128)(2,1)S(1)} %all-to-all-done.2.got, s32[16,128]{1,0:T(8,128)S(1)} %get-tuple-element.36.slot, f32[64,128]{1,0:T(8,128)S(1)} %bitcast.24, f32[64,128]{1,0:T(8,128)S(1)} %bitcast.25, ...), custom_call_target="tpu_custom_call" | custom-call | tf_op jit(solution)/shard_map/pallas_call | solution.py:315
  (5 shorter events, 0.0 us)
Async XLA Ops:
  3.1 7.8 %copy-start.6 = (bf16[4,3,256]{2,0,1:T(4,128)(2,1)S(1)}, bf16[4,3,256]{2,0,1:T(4,128)(2,1)}, u32[]{:S(2)}) copy-start(bf16[4,3,256]{2,0,1:T(4,128)(2,1)} %param.17) | copy-start | bytes 18436
  3.1 8.2 %copy-start.1 = (bf16[4,64,256]{2,1,0:T(8,128)(2,1)S(1)}, bf16[4,64,256]{2,1,0:T(8,128)(2,1)}, u32[]{:S(2)}) copy-start(bf16[4,64,256]{2,1,0:T(8,128)(2,1)} %w_one.3) | copy-start | bytes 393220
  3.1 16.2 %all-to-all-start = ((bf16[16,80,128]{2,1,0:T(8,128)(2,1)}), bf16[16,80,128]{2,1,0:T(8,128)(2,1)S(1)}, u32[]{:S(2)}, u32[]{:S(2)}) async-start(bf16[16,80,128]{2,1,0:T(8,128)(2,1)} %get-tuple-element.26), calls=%async_computation | async-start | bytes 655360 | tf_op jit(solution)/shard_map/all_to_all | solution.py:274
  10.9 1.0 %copy-start = (bf16[4,256,256]{2,1,0:T(8,128)(2,1)S(1)}, bf16[4,256,256]{2,1,0:T(8,128)(2,1)}, u32[]{:S(2)}) copy-start(bf16[4,256,256]{2,1,0:T(8,128)(2,1)} %w_two.3) | copy-start | bytes 1572868
  12.1 7.2 %copy-start.5 = (bf16[256,32]{0,1:T(8,128)(2,1)S(1)}, bf16[256,32]{0,1:T(8,128)(2,1)}, u32[]{:S(2)}) copy-start(bf16[256,32]{0,1:T(8,128)(2,1)} %param.18) | copy-start | bytes 49156
  23.2 5.9 %collective-permute-start = (bf16[8,168,128]{2,1,0:T(8,128)(2,1)S(1)}, bf16[8,168,128]{2,1,0:T(8,128)(2,1)S(1)}, u32[]{:S(2)}, u32[]{:S(2)}) collective-permute-start(bf16[8,168,128]{2,1,0:T(8,128)(2,1)S(1)} %get-tuple-element.34), channel_id=1, source_target_pairs={{0,16},{16,0},{32,48},{48,32},{64,80},{80,64},{96,112},{112,96},{1... | collective-permute-start | bytes 1032200 | tf_op jit(solution)/shard_map/ppermute | solution.py:299
  29.9 22.3 %all-to-all-start.1 = ((bf16[8,168,128]{2,1,0:T(8,128)(2,1)}), bf16[8,168,128]{2,1,0:T(8,128)(2,1)S(1)}, u32[]{:S(2)}, u32[]{:S(2)}) async-start(bf16[8,168,128]{2,1,0:T(8,128)(2,1)} %add_convert_fusion), calls=%async_computation.1 | async-start | bytes 688128 | tf_op jit(solution)/shard_map/all_to_all | solution.py:303
  52.2 21.6 %all-to-all-start.2 = ((bf16[16,80,128]{2,1,0:T(8,128)(2,1)}), bf16[16,80,128]{2,1,0:T(8,128)(2,1)S(1)}, u32[]{:S(2)}, u32[]{:S(2)}) async-start(bf16[16,80,128]{2,1,0:T(8,128)(2,1)} %shard_map.174), calls=%async_computation.2 | async-start | bytes 655360 | tf_op jit(solution)/shard_map/all_to_all | solution.py:313
  72.7 1.1 %copy-start.2 = (f32[2,32,128]{2,1,0:T(8,128)S(1)}, f32[2,32,128]{2,1,0:T(8,128)}, u32[]{:S(2)}) copy-start(f32[2,32,128]{2,1,0:T(8,128)} %param.12) | copy-start | bytes 98308
  72.7 1.1 %copy-start.3 = (f32[2,32,128]{2,1,0:T(8,128)S(1)}, f32[2,32,128]{2,1,0:T(8,128)}, u32[]{:S(2)}) copy-start(f32[2,32,128]{2,1,0:T(8,128)} %param.13) | copy-start | bytes 98308
  72.7 1.1 %copy-start.4 = (f32[2,32,128]{2,1,0:T(8,128)S(1)}, f32[2,32,128]{2,1,0:T(8,128)}, u32[]{:S(2)}) copy-start(f32[2,32,128]{2,1,0:T(8,128)} %param.14) | copy-start | bytes 98308

commit v3 on v2

--- a/solution.py
+++ b/solution.py
@@ -15,7 +15,9 @@
 ROWS = 2048
 CHUNKS = ROWS // LANES
 SLOTS = N_EXP * CAP
-GROUPS = 16
+GROUPS = 8
+LOW = 512
+PIECES = 2
 TEX_ROWS = 64
 SEND_ROWS = TEX_ROWS + 16
 GRAD_ROWS = 168
@@ -44,6 +46,24 @@
 def hot(index, count, start=0):
     same = iota((count, index.shape[1]), 0) + start == index
     return jnp.where(same, 1.0, 0.0).astype(bf16)
+
+
+def hot_wide(keys, start=0):
+    column = (iota((256, LANES), 0) + start).astype(bf16)
+    spread = jnp.broadcast_to(keys.astype(bf16), (256, keys.shape[1]))
+    parts = [
+        jnp.where(column == spread[:, i : i + LANES], jnp.ones((), bf16), jnp.zeros((), bf16))
+        for i in range(0, keys.shape[1], LANES)
+    ]
+    return jnp.concatenate(parts, axis=1)
+
+
+def split_index(rows):
+    high = rows[3:4].astype(jnp.int32) - 1
+    group = high >> 1
+    bit = high & 1
+    low = jnp.concatenate([hot_wide(jnp.where(bit == b, rows[4:5], -1.0)) for b in range(2)], axis=0)
+    return group, low
 
 
 def route_kernel(mat, tile_in, texel_in, direction_in, targets_in, latents_in, send, slot, *scratch):
@@ -80,8 +100,8 @@
     pair = material >> 1
     slot[...] = pair * LANES + lane
     texels = texel[...]
-    block = texels >> 8
-    high = (block * 2 + tile[...] + 1).astype(f32)
+    group = (texels >> 9) * 2 + tile[...]
+    high = (group * 2 + ((texels >> 8) & 1) + 1).astype(f32)
     low = (texels & 255).astype(f32)
     heading = (direction[...] + 1).astype(f32)
     values = []
@@ -112,9 +132,9 @@
     half, recv, w_one, w_one_t, w_two, w_two_t, w_three, w_three_t, dir_t, grads, back, preds, index, tex
 ):
     h = half[0]
-    for b in range(8):
-        for s in range(2):
-            tex[b * TEX_ROWS : (b + 1) * TEX_ROWS, s * LANES : (s + 1) * LANES] = recv[2 * b + s, :TEX_ROWS]
+    for b in range(4):
+        for s in range(4):
+            tex[b * TEX_ROWS : (b + 1) * TEX_ROWS, s * LANES : (s + 1) * LANES] = recv[4 * b + s, :TEX_ROWS]
     left = iota((8, LANES), 1) < CAP
     sides = ([], [])
     for j in range(N_EXP // 2):
@@ -122,59 +142,81 @@
         first, second = [jnp.where(h == 0, v[:8], v[8:]) for v in both]
         sides[0].append(jnp.where(left, first, pltpu.roll(second, CAP, 1)))
         sides[1].append(jnp.where(left, pltpu.roll(first, CAP, 1), second))
+    units = [(b, c) for b in range(2) for c in range(PIECES)]
+    width = SLOTS // PIECES
+    full = [jnp.concatenate(side, axis=1) for side in sides]
     for b in range(2):
-        e = 2 * h + b
-        rows = jnp.concatenate(sides[b], axis=1)
-        index[b] = rows
-        group = rows[3:4].astype(jnp.int32)
-        low_hot = hot(rows[4:5].astype(jnp.int32), 256)
-        dir_hot = hot(rows[5:6].astype(jnp.int32), 256, 1)
-        picked = dot(tex[...], low_hot)
-        lat = jnp.zeros((LAT, SLOTS), f32)
-        for r in range(GROUPS):
-            lat = lat + jnp.where(group == r + 1, picked[r * LAT : (r + 1) * LAT], 0.0)
-        x = jnp.concatenate([lat, dot(dir_t[...], dir_hot)], axis=0).astype(bf16)
-        pre_one = dot(w_one_t[e], x)
-        sig_one = 0.5 * jnp.tanh(0.5 * pre_one) + 0.5
-        raw_one = pre_one * sig_one
-        act_one = raw_one.astype(bf16)
-        slope_one = sig_one + raw_one * (1.0 - sig_one)
-        pre_two = dot(w_two_t[e], act_one)
-        sig_two = 0.5 * jnp.tanh(0.5 * pre_two) + 0.5
-        raw_two = pre_two * sig_two
-        act_two = raw_two.astype(bf16)
-        slope_two = sig_two + raw_two * (1.0 - sig_two)
-        pred = dot(w_three[e], act_two)
-        preds[b] = pred
-        misfit = jnp.where(iota((8, SLOTS), 0) < OUTC, pred - rows, 0.0).astype(bf16)
-        delta_two = (dot(w_three_t[e], misfit) * slope_two).astype(bf16)
-        delta_one = (dot(w_two[e], delta_two) * slope_one).astype(bf16)
-        grad_three = dot_nt(misfit, act_two).astype(grads.dtype)
-        grad_two = dot_nt(act_one, delta_two).astype(grads.dtype)
-        grad_one = dot_nt(x, delta_one).astype(grads.dtype)
+        index[b] = full[b]
+    rows = {(b, c): full[b][:, c * width : (c + 1) * width] for b, c in units}
+    split = {n: split_index(rows[n]) for n in units}
+    picked = {n: dot(tex[...], split[n][1]).reshape(GROUPS, LAT // 8, 8, width) for n in units}
+    heading = {n: dot(dir_t[...], hot_wide(rows[n][5:6], 1)) for n in units}
+    x = {}
+    for n in units:
+        wide = jnp.broadcast_to(split[n][0], (8, width))
+        lat = jnp.where((wide == 0)[None], picked[n][0], 0.0)
+        for r in range(1, GROUPS):
+            lat = jnp.where((wide == r)[None], picked[n][r], lat)
+        x[n] = jnp.concatenate([lat.reshape(LAT, width), heading[n]], axis=0).astype(bf16)
+    act_one, slope_one, act_two, slope_two, misfit, delta_two, delta_one = ({} for _ in range(7))
+    u = {n: dot(w_one_t[2 * h + n[0]], x[n]) for n in units}
+    for n in units:
+        t = jnp.tanh(u[n])
+        act_one[n] = (u[n] * (1.0 + t)).astype(bf16)
+        slope_one[n] = (1.0 + t) * (1.0 + u[n] * (1.0 - t))
+    u = {n: dot(w_two_t[2 * h + n[0]], act_one[n]) for n in units}
+    for n in units:
+        t = jnp.tanh(u[n])
+        act_two[n] = (u[n] * (1.0 + t)).astype(bf16)
+        slope_two[n] = (1.0 + t) * (1.0 + u[n] * (1.0 - t))
+    for n in units:
+        b, c = n
+        pred = dot(w_three[2 * h + b], act_two[n])
+        preds[b, :, c * width : (c + 1) * width] = pred
+        misfit[n] = jnp.where(iota((8, width), 0) < OUTC, pred - rows[n], 0.0).astype(bf16)
+    half_back = {n: dot(w_three_t[2 * h + n[0]], misfit[n]) for n in units}
+    for n in units:
+        delta_two[n] = (half_back[n] * slope_two[n]).astype(bf16)
+    half_back = {n: dot(w_two[2 * h + n[0]], delta_two[n]) for n in units}
+    for b in range(2):
+        pieces = [(b, c) for c in range(PIECES)]
+        grad_two = sum(dot_nt(act_one[n], delta_two[n]) for n in pieces).astype(grads.dtype)
+        grad_three = sum(dot_nt(misfit[n], act_two[n]) for n in pieces).astype(grads.dtype)
         for q in range(4):
-            n = 4 * b + q
             for s in range(2):
-                cols = slice(s * LANES, (s + 1) * LANES)
-                grads[n, s * 64 : (s + 1) * 64] = grad_two[q * 64 : (q + 1) * 64, cols]
-                grads[n, 128 + s * 16 : 128 + (s + 1) * 16] = grad_one[q * 16 : (q + 1) * 16, cols]
-            grads[n, 160:168] = grad_three[:, (q % 2) * LANES : (q % 2 + 1) * LANES]
-        back[b] = dot(w_one[e, :LAT], delta_one).astype(bf16)
+                grads[4 * b + q, s * 64 : (s + 1) * 64] = grad_two[q * 64 : (q + 1) * 64, s * LANES : (s + 1) * LANES]
+            grads[4 * b + q, 160:168] = grad_three[:, (q % 2) * LANES : (q % 2 + 1) * LANES]
+    for n in units:
+        delta_one[n] = (half_back[n] * slope_one[n]).astype(bf16)
+    for b in range(2):
+        pieces = [(b, c) for c in range(PIECES)]
+        grad_one = sum(dot_nt(x[n], delta_one[n]) for n in pieces).astype(grads.dtype)
+        for q in range(4):
+            for s in range(2):
+                grads[4 * b + q, 128 + s * 16 : 128 + (s + 1) * 16] = grad_one[
+                    q * 16 : (q + 1) * 16, s * LANES : (s + 1) * LANES
+                ]
+    for n in units:
+        b, c = n
+        back[b, :, c * width : (c + 1) * width] = dot(w_one[2 * h + b, :LAT], delta_one[n]).astype(bf16)
 
 
 def texels_kernel(half, back_a, back_b, preds_a, preds_b, index_a, index_b, out):
-    acc = jnp.zeros((GROUPS * LAT, 256), f32)
+    acc = jnp.zeros((GROUPS * LAT, LOW), f32)
     for rows_back, index in ((back_a, index_a), (back_b, index_b)):
         for b in range(2):
             rows = index[b]
-            group = rows[3:4].astype(jnp.int32)
-            low_hot = hot(rows[4:5].astype(jnp.int32), 256)
-            grad = rows_back[b].astype(f32)
-            spread = [jnp.where(group == r + 1, grad, 0.0).astype(bf16) for r in range(GROUPS)]
+            group, low_hot = split_index(rows)
+            wide = jnp.broadcast_to(group.astype(bf16), (16, SLOTS))
+            grad = rows_back[b].reshape(LAT // 16, 16, SLOTS)
+            spread = [
+                jnp.where((wide == jnp.array(r, bf16))[None], grad, jnp.zeros((), bf16)).reshape(LAT, SLOTS)
+                for r in range(GROUPS)
+            ]
             acc = acc + dot_nt(jnp.concatenate(spread, axis=0), low_hot)
-    for b in range(8):
-        for s in range(2):
-            out[2 * b + s, :TEX_ROWS] = acc[b * TEX_ROWS : (b + 1) * TEX_ROWS, s * LANES : (s + 1) * LANES].astype(bf16)
+    for b in range(4):
+        for s in range(4):
+            out[4 * b + s, :TEX_ROWS] = acc[b * TEX_ROWS : (b + 1) * TEX_ROWS, s * LANES : (s + 1) * LANES].astype(bf16)
     left = iota((8, LANES), 1) < CAP
     keep = half[0]
     for j in range(N_EXP // 2):
@@ -189,29 +231,16 @@
         out[2 * j + 1, TEX_ROWS:] = jnp.concatenate(high, axis=0).astype(bf16)
 
 
-def finish_kernel(got, slot, latents, mean, square, new_latents, new_mean, new_square, predictions):
-    texel_grad = jnp.zeros((TEX_ROWS, LANES), f32)
-    for j in range(N_EXP):
-        texel_grad = texel_grad + got[j, :TEX_ROWS].astype(f32)
-    next_mean = decay_one * mean[...] + (1.0 - decay_one) * texel_grad
-    next_square = decay_two * square[...] + (1.0 - decay_two) * texel_grad * texel_grad
-    new_mean[...] = next_mean
-    new_square[...] = next_square
-    new_latents[...] = latents[...] - step_rate * next_mean / (jnp.sqrt(next_square) + epsilon)
-    table = jnp.concatenate([got[j, TEX_ROWS:] for j in range(N_EXP)], axis=0)
-    place = slot[...]
-    lane = place & (LANES - 1)
-    pair = place >> 7
-    for i in range(CHUNKS):
-        row = slice(i, i + 1)
-        picked = dot(table, hot(lane[row], LANES))
-        total = jnp.zeros((8, LANES), f32)
-        for g in range(32):
-            total = total + jnp.where(pair[row] == g, picked[g * 8 : (g + 1) * 8], 0.0)
-        predictions[:, i * LANES : (i + 1) * LANES] = total[:OUTC]
-
-
-def unpack_kernel(packed, grad_one, grad_two, grad_three):
+def finish_kernel(
+    packed, got, slot, latents, mean, square, out_one, out_two, out_three, out_latents, out_mean, out_square, out_pred, *scratch
+):
+    grad_one, grad_two, grad_three, new_latents, new_mean, new_square, predictions, sems = scratch
+    copies = []
+
+    def leave(source, target):
+        copies.append(pltpu.make_async_copy(source, target, sems.at[len(copies)]))
+        copies[-1].start()
+
     for e in range(4):
         for q in range(4):
             n = 2 * (4 * (e % 2) + q) + e // 2
@@ -222,10 +251,41 @@
             if q < 2:
                 for c in range(OUTC):
                     grad_three[c, e : e + 1, q * LANES : (q + 1) * LANES] = packed[n, 160:168].astype(f32)[c : c + 1]
-
-
-def call(kernel, outs, scratch=(), in_specs=None, flops=0):
+        leave(grad_two.at[e], out_two.at[e])
+    leave(grad_one, out_one)
+    leave(grad_three, out_three)
+    texel_grad = jnp.zeros((TEX_ROWS, LANES), f32)
+    for j in range(N_EXP):
+        texel_grad = texel_grad + got[j, :TEX_ROWS].astype(f32)
+    next_mean = decay_one * mean[...] + (1.0 - decay_one) * texel_grad
+    next_square = decay_two * square[...] + (1.0 - decay_two) * texel_grad * texel_grad
+    new_mean[...] = next_mean
+    new_square[...] = next_square
+    new_latents[...] = latents[...] - step_rate * next_mean / (jnp.sqrt(next_square) + epsilon)
+    leave(new_mean, out_mean)
+    leave(new_square, out_square)
+    leave(new_latents, out_latents)
+    table = jnp.concatenate([got[j, TEX_ROWS:] for j in range(N_EXP)], axis=0)
+    place = slot[...]
+    lane = place & (LANES - 1)
+    pair = place >> 7
+    for i in range(CHUNKS):
+        row = slice(i, i + 1)
+        picked = dot(table, hot(lane[row], LANES))
+        wide = jnp.broadcast_to(pair[row], (8, LANES))
+        total = jnp.where(wide == 0, picked[:8], 0.0)
+        for g in range(1, 32):
+            total = jnp.where(wide == g, picked[g * 8 : (g + 1) * 8], total)
+        predictions[:, i * LANES : (i + 1) * LANES] = total[:OUTC]
+    leave(predictions, out_pred)
+    for copy in copies:
+        copy.wait()
+
+
+def call(kernel, outs, scratch=(), in_specs=None, flops=0, out_specs=None):
     more = {} if in_specs is None else {"in_specs": in_specs}
+    if out_specs is not None:
+        more["out_specs"] = out_specs
     cost = pl.CostEstimate(flops=flops, transcendentals=0, bytes_accessed=0) if flops else None
     return pl.pallas_call(
         kernel,
@@ -275,11 +335,11 @@
     three = jnp.pad(weight_three, ((0, 0), (0, 8 - OUTC), (0, 0)))
     weights = (
         weight_one,
-        jnp.swapaxes(weight_one, 1, 2),
-        weight_two,
-        jnp.swapaxes(weight_two, 1, 2),
+        jnp.swapaxes(weight_one, 1, 2) * 0.5,
+        weight_two * 0.5,
+        jnp.swapaxes(weight_two, 1, 2) * 0.5,
         three,
-        jnp.swapaxes(three, 1, 2),
+        jnp.swapaxes(three, 1, 2) * 0.5,
         dir_table.T,
     )
     core = (lax.axis_index("rep") % 2).astype(jnp.int32).reshape(1)
@@ -291,7 +351,7 @@
             shape((2, 8, SLOTS)),
             shape((2, 8, SLOTS)),
         ),
-        [pltpu.VMEM((GROUPS * LAT, 256), bf16)],
+        [pltpu.VMEM((GROUPS * LAT, LOW), bf16)],
         [smem] + [vmem] * 8,
         2000000000,
     )
@@ -312,14 +372,16 @@
     back, own = lax.optimization_barrier((back, own))
     got = lax.all_to_all(back, "exp", 0, 0, tiled=True)
     packed = lax.all_gather(own, "rep", axis=0, tiled=False)
-    new_latents, new_mean, new_square, predictions = call(
+    plane = (TEX_ROWS, LANES)
+    outs = (weight_one.shape, weight_two.shape, (OUTC, 4, HID), plane, plane, plane, (OUTC, ROWS))
+    grad_one, grad_two, grad_three, new_latents, new_mean, new_square, predictions = call(
         finish_kernel,
-        (shape((TEX_ROWS, LANES)), shape((TEX_ROWS, LANES)), shape((TEX_ROWS, LANES)), shape((OUTC, ROWS))),
-    )(got, slot, flat(latents), flat(latent_mean), flat(latent_square))
-    grad_one, grad_two, grad_three = call(
-        unpack_kernel,
-        (shape(weight_one.shape), shape(weight_two.shape), shape((OUTC, 4, HID))),
-    )(packed)
+        tuple(shape(dims) for dims in outs),
+        [pltpu.VMEM(dims, f32) for dims in outs] + [pltpu.SemaphoreType.DMA((10,))],
+        [vmem] * 6,
+        0,
+        tuple([hbm] * 7),
+    )(packed, got, slot, flat(latents), flat(latent_mean), flat(latent_square))
     grad_three = jnp.swapaxes(grad_three, 0, 1)
     whole = lambda a: a.reshape(latents.shape)
     return (

time: 75.5 us -> 74.1 us (0.981)
  Pallas kernels: 14.6 us -> 13.1 us
  waiting for transfers between devices: 19.2 us -> 17.9 us
  local copies, waits for them, and re-layouts: 1.3 us -> 2.41 us
    all_to_all x1, waiting for transfers between devices: 7.13 us -> 5.82 us  [on_device(): recv = lax.all_to_all(send, 'exp', 0, 0, tiled=True)]
    unnamed x18, local copies, waits for them, and re-layouts: 1.24 us -> 2.2 us
    pallas_call x2 -> x1, Pallas kernels: 2.33 us -> 1.54 us  [on_device(): call(finish_kernel, tuple((shape(dims) for dims in outs)), [pltpu.VMEM(di...]
  transfers between devices with their start and end apart: 4 -> 4, of which waited for: 2 -> 2; matrix products, arithmetic and copies ran while one was open for 1% -> 2% of each run, Pallas kernels for 9% -> 8%
where the time goes in v3:
time: 74.1 us; the launch traced here: 73.5 us
  starting transfers between devices  21.4 us (29%)
  waiting for transfers between devices  17.9 us (24%)
  blocking collectives  16.9 us (23%)
  Pallas kernels  13.1 us (18%)
  local copies, waits for them, and re-layouts  2.41 us (3%)
  other arithmetic  1.02 us (1%)
  between operations  0.81 us (1%)
    all_gather x1, blocking collectives, on_device(): packed = lax.all_gather(own, 'rep', axis=0, tiled=False)  16.9 us
    all_to_all x1, waiting for transfers between devices, on_device(): lax.all_to_all(chip, 'rep', 0, 0, tiled=True, axis_index_groups=chips)  12.1 us
    all_to_all x1, starting transfers between devices, on_device(): lax.all_to_all(chip, 'rep', 0, 0, tiled=True, axis_index_groups=chips)  8.18 us
    all_to_all x1, starting transfers between devices, on_device(): recv = lax.all_to_all(send, 'exp', 0, 0, tiled=True)  7.73 us
    all_to_all x1, waiting for transfers between devices, on_device(): recv = lax.all_to_all(send, 'exp', 0, 0, tiled=True)  5.82 us
    all_to_all x1, starting transfers between devices, on_device(): got = lax.all_to_all(back, 'exp', 0, 0, tiled=True)  3.55 us
    pallas_call x1, Pallas kernels, on_device(): grads_a, back_a, preds_a, index_a = half(bf16)(1 - core, recv, *weights)  3.52 us
    pallas_call x1, Pallas kernels, on_device(): grads_b, back_b, preds_b, index_b = half(f32)(core, recv, *weights)  3.52 us
  transfers between devices with their start and end apart: 4, of which 2 were waited for; matrix products, arithmetic and copies ran while one was open for 2% of the time, Pallas kernels for 8%

profile of v3, /device:TPU:1, one launch (start us, length us, event | category | flops | bytes accessed | tf_op | source)
XLA Modules:
  0.0 73.5 jit_solution(6631341387683655811)
XLA Ops:
  0.6 2.5 %shard_map.171 = (bf16[16,80,128]{2,1,0:T(8,128)(2,1)}, s32[16,128]{1,0:T(8,128)S(1)}) custom-call(s32[16,128]{1,0:T(8,128)} %bitcast.27, s32[16,128]{1,0:T(8,128)} %bitcast.28, s32[16,128]{1,0:T(8,128)} %bitcast.29, s32[16,128]{1,0:T(8,128)} %bitcast.30, f32[3,2048]{1,0:T(4,128)} %targets_in.1, f32[64,128]{1,0:T(8,128)} %bitcast.21), custom_call_target="tpu_custom_call" | custom-call | tf_op jit(solution)/shard_map/pallas_call | solution.py:324
  3.1 0.0 copy-start.5
  3.1 7.7 %all-to-all-start = ((bf16[16,80,128]{2,1,0:T(8,128)(2,1)}), bf16[16,80,128]{2,1,0:T(8,128)(2,1)S(1)}, u32[]{:S(2)}, u32[]{:S(2)}) async-start(bf16[16,80,128]{2,1,0:T(8,128)(2,1)} %get-tuple-element.26), calls=%async_computation | async-start | bytes 655360 | tf_op jit(solution)/shard_map/all_to_all | solution.py:334
  10.9 0.0 copy-start.6
  10.9 0.7 copy-done.6
  11.5 0.2 copy.29
  11.8 0.0 copy-start
  11.8 0.1 copy.34
  11.9 0.8 %copy-done = bf16[4,64,256]{2,1,0:T(8,128)(2,1)S(1)} copy-done((bf16[4,64,256]{2,1,0:T(8,128)(2,1)S(1)}, bf16[4,64,256]{2,1,0:T(8,128)(2,1)}, u32[]{:S(2)}) %copy-start) | copy-done | bytes 131096
  12.7 0.2 copy.26
  12.9 0.2 copy.28
  13.1 0.1 fusion
  13.1 0.2 copy.30.w_two
  13.4 0.1 multiply_bitcast_fusion.w_three_t
  13.5 0.0 copy-start.4
  13.5 5.8 %all-to-all-done.recv = bf16[16,80,128]{2,1,0:T(8,128)(2,1)S(1)} async-done(((bf16[16,80,128]{2,1,0:T(8,128)(2,1)}), bf16[16,80,128]{2,1,0:T(8,128)(2,1)S(1)}, u32[]{:S(2)}, u32[]{:S(2)}) %all-to-all-start) | async-done | bytes 327712 | tf_op jit(solution)/shard_map/all_to_all | solution.py:334
  19.3 3.5 %shard_map.172 = (bf16[8,168,128]{2,1,0:T(8,128)(2,1)S(1)}, bf16[2,32,1024]{2,1,0:T(8,128)(2,1)S(1)}, f32[2,8,1024]{2,1,0:T(8,128)S(1)}, f32[2,8,1024]{2,1,0:T(8,128)S(1)}) custom-call(s32[1]{0:T(128)S(6)} %sub.3.half, bf16[16,80,128]{2,1,0:T(8,128)(2,1)S(1)} %all-to-all-done.recv, bf16[4,64,256]{2,1,0:T(8,128)(2,1)S(1)} %copy-done, ...), custom_call_target="tpu_custom_call" | custom-call | flops 2000000000 | tf_op jit(solution)/shard_map/pallas_call | solution.py:358
  22.8 1.9 %collective-permute-start = (bf16[8,168,128]{2,1,0:T(8,128)(2,1)S(1)}, bf16[8,168,128]{2,1,0:T(8,128)(2,1)S(1)}, u32[]{:S(2)}, u32[]{:S(2)}) collective-permute-start(bf16[8,168,128]{2,1,0:T(8,128)(2,1)S(1)} %get-tuple-element.34), channel_id=1, source_target_pairs={{0,16},{16,0},{32,48},{48,32},{64,80},{80,64},{96,112},{112,96},{1... | collective-permute-start | bytes 1032200 | tf_op jit(solution)/shard_map/ppermute | solution.py:359
  24.8 3.5 %shard_map.173 = (f32[8,168,128]{2,1,0:T(8,128)S(1)}, bf16[2,32,1024]{2,1,0:T(8,128)(2,1)S(1)}, f32[2,8,1024]{2,1,0:T(8,128)S(1)}, f32[2,8,1024]{2,1,0:T(8,128)S(1)}) custom-call(s32[1]{0:T(128)} %bitcast.half, bf16[16,80,128]{2,1,0:T(8,128)(2,1)S(1)} %all-to-all-done.recv, bf16[4,64,256]{2,1,0:T(8,128)(2,1)S(1)} %copy-done, ...), custom_call_target="tpu_custom_call" | custom-call | flops 2000000000 | tf_op jit(solution)/shard_map/pallas_call | solution.py:360
  28.3 0.0 collective-permute-done
  28.3 0.8 %add_convert_fusion = bf16[8,168,128]{2,1,0:T(8,128)(2,1)} fusion(f32[8,168,128]{2,1,0:T(8,128)S(1)} %get-tuple-element.33, bf16[8,168,128]{2,1,0:T(8,128)(2,1)S(1)} %collective-permute-done), kind=kLoop, calls=%fused_computation | loop fusion | flops 516096 | bytes 1376256 | tf_op jit(solution)/shard_map/convert_element_type | solution.py:361
  29.1 8.2 %all-to-all-start.1 = ((bf16[8,168,128]{2,1,0:T(8,128)(2,1)}), bf16[8,168,128]{2,1,0:T(8,128)(2,1)S(1)}, u32[]{:S(2)}, u32[]{:S(2)}) async-start(bf16[8,168,128]{2,1,0:T(8,128)(2,1)} %add_convert_fusion), calls=%async_computation.1 | async-start | bytes 688128 | tf_op jit(solution)/shard_map/all_to_all | solution.py:363
  37.3 2.0 %shard_map.174 = bf16[16,80,128]{2,1,0:T(8,128)(2,1)} custom-call(s32[1]{0:T(128)} %bitcast.half, bf16[2,32,1024]{2,1,0:T(8,128)(2,1)S(1)} %get-tuple-element.27.back_a, bf16[2,32,1024]{2,1,0:T(8,128)(2,1)S(1)} %get-tuple-element.28.back_b, f32[2,8,1024]{2,1,0:T(8,128)S(1)} %get-tuple-element.29.preds_a, f32[2,8,1024]{2,1,0:T(8,128)S(1)} %get-tuple-element.30.preds_b, ...), custom_call_target="tpu_custom_call" | custom-call | flops 2000000000 | tf_op jit(solution)/shard_map/pallas_call | solution.py:364
  39.3 12.1 %all-to-all-done.1 = bf16[8,168,128]{2,1,0:T(8,128)(2,1)S(1)} async-done(((bf16[8,168,128]{2,1,0:T(8,128)(2,1)}), bf16[8,168,128]{2,1,0:T(8,128)(2,1)S(1)}, u32[]{:S(2)}, u32[]{:S(2)}) %all-to-all-start.1) | async-done | bytes 344096 | tf_op jit(solution)/shard_map/all_to_all | solution.py:363
  51.4 0.1 reduce_sum.12
  51.5 3.6 %all-to-all-start.2 = ((bf16[16,80,128]{2,1,0:T(8,128)(2,1)}), bf16[16,80,128]{2,1,0:T(8,128)(2,1)S(1)}, u32[]{:S(2)}, u32[]{:S(2)}) async-start(bf16[16,80,128]{2,1,0:T(8,128)(2,1)} %shard_map.174), calls=%async_computation.2 | async-start | bytes 655360 | tf_op jit(solution)/shard_map/all_to_all | solution.py:373
  55.0 0.0 copy-start.1
  55.1 0.0 copy-start.2
  55.1 0.0 copy-start.3
  55.1 16.9 %all-gather = bf16[2688,128]{1,0:T(8,128)(2,1)S(1)} all-gather(bf16[168,128]{1,0:T(8,128)(2,1)S(1)} %reduce_sum.12), channel_id=2, replica_groups=mesh['rep'=16,'exp'=16] {'rep'}, dimensions={0}, use_global_device_ids=true | all-gather | bytes 731136 | tf_op jit(solution)/shard_map/all_gather | solution.py:374
  72.0 0.0 all-to-all-done.2.got
  72.0 1.5 %shard_map.175 = (f32[4,64,256]{2,1,0:T(8,128)}, f32[4,256,256]{2,1,0:T(8,128)}, f32[3,4,256]{2,1,0:T(4,128)}, f32[64,128]{1,0:T(8,128)}, f32[64,128]{1,0:T(8,12...) custom-call(bf16[16,168,128]{2,1,0:T(8,128)(2,1)S(1)} %bitcast.20, bf16[16,80,128]{2,1,0:T(8,128)(2,1)S(1)} %all-to-all-done.2.got, ...), custom_call_target="tpu_custom_call" | custom-call | tf_op jit(solution)/shard_map/pallas_call | solution.py:377
  (7 shorter events, 0.0 us)
Async XLA Ops:
  3.1 9.8 %copy-start.5 = (bf16[4,256,256]{2,1,0:T(8,128)(2,1)S(1)}, bf16[4,256,256]{2,1,0:T(8,128)(2,1)}, u32[]{:S(2)}) copy-start(bf16[4,256,256]{2,1,0:T(8,128)(2,1)} %param.16) | copy-start | bytes 1572868
  3.1 16.2 %all-to-all-start = ((bf16[16,80,128]{2,1,0:T(8,128)(2,1)}), bf16[16,80,128]{2,1,0:T(8,128)(2,1)S(1)}, u32[]{:S(2)}, u32[]{:S(2)}) async-start(bf16[16,80,128]{2,1,0:T(8,128)(2,1)} %get-tuple-element.26), calls=%async_computation | async-start | bytes 655360 | tf_op jit(solution)/shard_map/all_to_all | solution.py:334
  10.9 0.7 copy-start.6
  11.8 0.9 %copy-start = (bf16[4,64,256]{2,1,0:T(8,128)(2,1)S(1)}, bf16[4,64,256]{2,1,0:T(8,128)(2,1)}, u32[]{:S(2)}) copy-start(bf16[4,64,256]{2,1,0:T(8,128)(2,1)} %w_one.3) | copy-start | bytes 393220
  13.5 5.9 %copy-start.4 = (bf16[256,32]{0,1:T(8,128)(2,1)S(1)}, bf16[256,32]{0,1:T(8,128)(2,1)}, u32[]{:S(2)}) copy-start(bf16[256,32]{0,1:T(8,128)(2,1)} %param.18) | copy-start | bytes 49156
  22.8 5.5 %collective-permute-start = (bf16[8,168,128]{2,1,0:T(8,128)(2,1)S(1)}, bf16[8,168,128]{2,1,0:T(8,128)(2,1)S(1)}, u32[]{:S(2)}, u32[]{:S(2)}) collective-permute-start(bf16[8,168,128]{2,1,0:T(8,128)(2,1)S(1)} %get-tuple-element.34), channel_id=1, source_target_pairs={{0,16},{16,0},{32,48},{48,32},{64,80},{80,64},{96,112},{112,96},{1... | collective-permute-start | bytes 1032200 | tf_op jit(solution)/shard_map/ppermute | solution.py:359
  29.1 22.3 %all-to-all-start.1 = ((bf16[8,168,128]{2,1,0:T(8,128)(2,1)}), bf16[8,168,128]{2,1,0:T(8,128)(2,1)S(1)}, u32[]{:S(2)}, u32[]{:S(2)}) async-start(bf16[8,168,128]{2,1,0:T(8,128)(2,1)} %add_convert_fusion), calls=%async_computation.1 | async-start | bytes 688128 | tf_op jit(solution)/shard_map/all_to_all | solution.py:363
  51.5 20.5 %all-to-all-start.2 = ((bf16[16,80,128]{2,1,0:T(8,128)(2,1)}), bf16[16,80,128]{2,1,0:T(8,128)(2,1)S(1)}, u32[]{:S(2)}, u32[]{:S(2)}) async-start(bf16[16,80,128]{2,1,0:T(8,128)(2,1)} %shard_map.174), calls=%async_computation.2 | async-start | bytes 655360 | tf_op jit(solution)/shard_map/all_to_all | solution.py:373
  55.0 16.9 %copy-start.1 = (f32[2,32,128]{2,1,0:T(8,128)S(1)}, f32[2,32,128]{2,1,0:T(8,128)}, u32[]{:S(2)}) copy-start(f32[2,32,128]{2,1,0:T(8,128)} %param.12) | copy-start | bytes 98308
  55.1 16.9 %copy-start.2 = (f32[2,32,128]{2,1,0:T(8,128)S(1)}, f32[2,32,128]{2,1,0:T(8,128)}, u32[]{:S(2)}) copy-start(f32[2,32,128]{2,1,0:T(8,128)} %param.13) | copy-start | bytes 98308
  55.1 16.9 %copy-start.3 = (f32[2,32,128]{2,1,0:T(8,128)S(1)}, f32[2,32,128]{2,1,0:T(8,128)}, u32[]{:S(2)}) copy-start(f32[2,32,128]{2,1,0:T(8,128)} %param.14) | copy-start | bytes 98308

commit v4 on v3

--- a/solution.py
+++ b/solution.py
@@ -67,7 +67,7 @@
 
 
 def route_kernel(mat, tile_in, texel_in, direction_in, targets_in, latents_in, send, slot, *scratch):
-    material_in, tile, texel, direction, targets, latents, sems = scratch
+    material_in, tile, texel, direction, targets, latents, own, packets, sems = scratch
     copies = [
         pltpu.make_async_copy(source, target, sems.at[n])
         for n, (source, target) in enumerate(
@@ -81,9 +81,16 @@
             ]
         )
     ]
-    for copy in copies:
+    for copy in reversed(copies):
         copy.start()
-    for copy in copies:
+    copies[5].wait()
+    own[...] = latents[...].astype(bf16)
+    leaving = [
+        pltpu.make_async_copy(own, send.at[j, pl.ds(0, TEX_ROWS)], sems.at[6 + j]) for j in range(N_EXP)
+    ]
+    for copy in leaving:
+        copy.start()
+    for copy in copies[:5]:
         copy.wait()
     material = material_in[...]
     hots = [hot(material[i : i + 1], 64) for i in range(CHUNKS)]
@@ -122,16 +129,44 @@
         values.append(jnp.concatenate(parts, axis=0).astype(bf16))
         lanes_hot.append(hot(lane[row], LANES))
     out = dot_nt(jnp.concatenate(values, axis=1), jnp.concatenate(lanes_hot, axis=1)).astype(bf16)
-    own = latents[...].astype(bf16)
     for j in range(N_EXP):
-        send[j, :TEX_ROWS] = own
-        send[j, TEX_ROWS:] = out[j * 16 : (j + 1) * 16]
-
-
-def half_kernel(
-    half, recv, w_one, w_one_t, w_two, w_two_t, w_three, w_three_t, dir_t, grads, back, preds, index, tex
-):
+        packets[j] = out[j * 16 : (j + 1) * 16]
+    last = pltpu.make_async_copy(packets, send.at[:, pl.ds(TEX_ROWS, 16)], sems.at[6 + N_EXP])
+    last.start()
+    for copy in leaving:
+        copy.wait()
+    last.wait()
+
+
+def put(grads, n, rows, value, more):
+    if more is not None:
+        value = value + more[n, rows].astype(f32)
+    grads[n, rows] = value.astype(bf16)
+
+
+def put_two(grads, b, value, more=None):
+    for q in range(4):
+        for s in range(2):
+            part = value[q * 64 : (q + 1) * 64, s * LANES : (s + 1) * LANES]
+            put(grads, 4 * b + q, slice(s * 64, (s + 1) * 64), part, more)
+
+
+def put_one(grads, b, value, more=None):
+    for q in range(4):
+        for s in range(2):
+            part = value[q * 16 : (q + 1) * 16, s * LANES : (s + 1) * LANES]
+            put(grads, 4 * b + q, slice(128 + s * 16, 128 + (s + 1) * 16), part, more)
+
+
+def put_three(grads, b, value, more=None):
+    for q in range(4):
+        part = value[:, (q % 2) * LANES : (q % 2 + 1) * LANES]
+        put(grads, 4 * b + q, slice(160, 168), part, more)
+
+
+def half_kernel(half, recv, w_one, w_one_t, w_two, w_two_t, w_three, w_three_t, dir_t, back, preds, index, *rest):
     h = half[0]
+    tex = rest[-1]
     for b in range(4):
         for s in range(4):
             tex[b * TEX_ROWS : (b + 1) * TEX_ROWS, s * LANES : (s + 1) * LANES] = recv[4 * b + s, :TEX_ROWS]
@@ -178,27 +213,43 @@
     for n in units:
         delta_two[n] = (half_back[n] * slope_two[n]).astype(bf16)
     half_back = {n: dot(w_two[2 * h + n[0]], delta_two[n]) for n in units}
-    for b in range(2):
-        pieces = [(b, c) for c in range(PIECES)]
-        grad_two = sum(dot_nt(act_one[n], delta_two[n]) for n in pieces).astype(grads.dtype)
-        grad_three = sum(dot_nt(misfit[n], act_two[n]) for n in pieces).astype(grads.dtype)
-        for q in range(4):
-            for s in range(2):
-                grads[4 * b + q, s * 64 : (s + 1) * 64] = grad_two[q * 64 : (q + 1) * 64, s * LANES : (s + 1) * LANES]
-            grads[4 * b + q, 160:168] = grad_three[:, (q % 2) * LANES : (q % 2 + 1) * LANES]
+    if len(rest) == 2:
+        for b in range(2):
+            pieces = [(b, c) for c in range(PIECES)]
+            put_two(rest[0], b, sum(dot_nt(act_one[n], delta_two[n]) for n in pieces))
+            put_three(rest[0], b, sum(dot_nt(misfit[n], act_two[n]) for n in pieces))
+    else:
+        for n in units:
+            b, c = n
+            kept = (act_one, delta_two, misfit, act_two, x)
+            for ref, value in zip(rest[:5], kept):
+                ref[b, :, c * width : (c + 1) * width] = value[n]
     for n in units:
         delta_one[n] = (half_back[n] * slope_one[n]).astype(bf16)
-    for b in range(2):
-        pieces = [(b, c) for c in range(PIECES)]
-        grad_one = sum(dot_nt(x[n], delta_one[n]) for n in pieces).astype(grads.dtype)
-        for q in range(4):
-            for s in range(2):
-                grads[4 * b + q, 128 + s * 16 : 128 + (s + 1) * 16] = grad_one[
-                    q * 16 : (q + 1) * 16, s * LANES : (s + 1) * LANES
-                ]
+    if len(rest) == 2:
+        for b in range(2):
+            put_one(rest[0], b, sum(dot_nt(x[b, c], delta_one[b, c]) for c in range(PIECES)))
+    else:
+        for n in units:
+            b, c = n
+            rest[5][b, :, c * width : (c + 1) * width] = delta_one[n]
     for n in units:
         b, c = n
         back[b, :, c * width : (c + 1) * width] = dot(w_one[2 * h + b, :LAT], delta_one[n]).astype(bf16)
+
+
+def weights_kernel(act_one, delta_two, misfit, act_two, x, delta_one, from_core, out, grads, sems):
+    copies = []
+    for b in range(2):
+        put_two(grads, b, dot_nt(act_one[b], delta_two[b]), from_core)
+        put_one(grads, b, dot_nt(x[b], delta_one[b]), from_core)
+        put_three(grads, b, dot_nt(misfit[b], act_two[b]), from_core)
+        copies.append(
+            pltpu.make_async_copy(grads.at[pl.ds(4 * b, 4)], out.at[pl.ds(4 * b, 4)], sems.at[b])
+        )
+        copies[-1].start()
+    for copy in copies:
+        copy.wait()
 
 
 def texels_kernel(half, back_a, back_b, preds_a, preds_b, index_a, index_b, out):
@@ -291,7 +342,7 @@
         kernel,
         out_shape=outs,
         scratch_shapes=list(scratch),
-        compiler_params=pltpu.CompilerParams(vmem_limit_bytes=48 << 20),
+        compiler_params=pltpu.CompilerParams(vmem_limit_bytes=24 << 20),
         cost_estimate=cost,
         **more,
     )
@@ -325,8 +376,16 @@
         route_kernel,
         (shape((N_EXP, SEND_ROWS, LANES), bf16), shape((CHUNKS, LANES), jnp.int32)),
         [index_rows] * 4
-        + [pltpu.VMEM((OUTC, ROWS), f32), pltpu.VMEM((TEX_ROWS, LANES), f32), pltpu.SemaphoreType.DMA((6,))],
+        + [
+            pltpu.VMEM((OUTC, ROWS), f32),
+            pltpu.VMEM((TEX_ROWS, LANES), f32),
+            pltpu.VMEM((TEX_ROWS, LANES), bf16),
+            pltpu.VMEM((N_EXP, 16, LANES), bf16),
+            pltpu.SemaphoreType.DMA((7 + N_EXP,)),
+        ],
         [hbm] * 6,
+        0,
+        (hbm, vmem),
     )(*[
         pltpu.with_memory_space_constraint(a, pltpu.HBM)
         for a in (rows(materials), rows(tile_ids), rows(texel_ids), rows(dir_ids), targets, flat(latents))
@@ -343,22 +402,28 @@
         dir_table.T,
     )
     core = (lax.axis_index("rep") % 2).astype(jnp.int32).reshape(1)
-    half = lambda kind: call(
+    gradient = shape((N_REP // 2, GRAD_ROWS, LANES), bf16)
+    wide = lambda height: shape((2, height, SLOTS), bf16)
+    half = lambda *outs: call(
         half_kernel,
-        (
-            shape((N_REP // 2, GRAD_ROWS, LANES), kind),
-            shape((2, LAT, SLOTS), bf16),
-            shape((2, 8, SLOTS)),
-            shape((2, 8, SLOTS)),
-        ),
+        (wide(LAT), shape((2, 8, SLOTS)), shape((2, 8, SLOTS)), *outs),
         [pltpu.VMEM((GROUPS * LAT, LOW), bf16)],
         [smem] + [vmem] * 8,
         2000000000,
     )
-    grads_a, back_a, preds_a, index_a = half(bf16)(1 - core, recv, *weights)
+    back_a, preds_a, index_a, grads_a = half(gradient)(1 - core, recv, *weights)
     from_core = lax.ppermute(grads_a, "rep", [(i, i ^ 1) for i in range(N_REP)])
-    grads_b, back_b, preds_b, index_b = half(f32)(core, recv, *weights)
-    chip = (grads_b + from_core.astype(f32)).astype(bf16)
+    back_b, preds_b, index_b, *kept = half(wide(HID), wide(HID), wide(8), wide(HID), wide(2 * LAT), wide(HID))(
+        core, recv, *weights
+    )
+    chip = call(
+        weights_kernel,
+        gradient,
+        [pltpu.VMEM((N_REP // 2, GRAD_ROWS, LANES), bf16), pltpu.SemaphoreType.DMA((2,))],
+        [vmem] * 7,
+        0,
+        hbm,
+    )(*kept, from_core)
     chips = [list(range(c, N_REP, 2)) for c in range(2)]
     parts = lax.all_to_all(chip, "rep", 0, 0, tiled=True, axis_index_groups=chips)
     back = call(

time: 74.1 us -> 74.6 us (level)
  Pallas kernels: 13.1 us -> 14.4 us
  other arithmetic: 1.02 us -> 0.22 us
    pallas_call x2 -> x3, Pallas kernels: 7.04 us -> 8.35 us  [the longest x1 3.53 us: on_device(): back_a, preds_a, index_a, grads_a = half(gradient)(1 - core, recv, *weights)]
    convert_element_type x1 -> x0, other arithmetic: 0.8 us -> none  [on_device(): chip = (grads_b + from_core.astype(f32)).astype(bf16)]
  transfers between devices with their start and end apart: 4 -> 4, of which waited for: 2 -> 2; matrix products, arithmetic and copies ran while one was open for 2% -> 1% of each run, Pallas kernels for 8% -> 7%
where the time goes in v4:
time: 74.6 us; the launch traced here: 74.1 us
  starting transfers between devices  21.4 us (29%)
  waiting for transfers between devices  17.9 us (24%)
  blocking collectives  16.9 us (23%)
  Pallas kernels  14.4 us (19%)
  local copies, waits for them, and re-layouts  2.41 us (3%)
  between operations  0.82 us (1%)
    all_gather x1, blocking collectives, on_device(): packed = lax.all_gather(own, 'rep', axis=0, tiled=False)  16.9 us
    all_to_all x1, waiting for transfers between devices, on_device(): lax.all_to_all(chip, 'rep', 0, 0, tiled=True, axis_index_groups=chips)  12.1 us
    all_to_all x1, starting transfers between devices, on_device(): lax.all_to_all(chip, 'rep', 0, 0, tiled=True, axis_index_groups=chips)  8.21 us
    all_to_all x1, starting transfers between devices, on_device(): recv = lax.all_to_all(send, 'exp', 0, 0, tiled=True)  7.72 us
    all_to_all x1, waiting for transfers between devices, on_device(): recv = lax.all_to_all(send, 'exp', 0, 0, tiled=True)  5.82 us
    all_to_all x1, starting transfers between devices, on_device(): got = lax.all_to_all(back, 'exp', 0, 0, tiled=True)  3.55 us
    pallas_call x1, Pallas kernels, on_device(): back_a, preds_a, index_a, grads_a = half(gradient)(1 - core, recv, *weights)  3.53 us
    pallas_call x1, Pallas kernels, on_device(): half(wide(HID), wide(HID), wide(8), wide(HID), wide(2 * LAT), wide(HID))  3.16 us
  transfers between devices with their start and end apart: 4, of which 2 were waited for; matrix products, arithmetic and copies ran while one was open for 1% of the time, Pallas kernels for 7%

profile of v4, /device:TPU:1, one launch (start us, length us, event | category | flops | bytes accessed | tf_op | source)
XLA Modules:
  0.0 74.1 jit_solution(10599350202435309285)
XLA Ops:
  0.6 2.5 %shard_map.171 = (bf16[16,80,128]{2,1,0:T(8,128)(2,1)}, s32[16,128]{1,0:T(8,128)S(1)}) custom-call(s32[16,128]{1,0:T(8,128)} %bitcast.27, s32[16,128]{1,0:T(8,128)} %bitcast.28, s32[16,128]{1,0:T(8,128)} %bitcast.29, s32[16,128]{1,0:T(8,128)} %bitcast.30, f32[3,2048]{1,0:T(4,128)} %targets_in.1, f32[64,128]{1,0:T(8,128)} %bitcast.21), custom_call_target="tpu_custom_call" | custom-call | tf_op jit(solution)/shard_map/pallas_call | solution.py:375
  3.1 0.0 copy-start.5
  3.1 7.7 %all-to-all-start = ((bf16[16,80,128]{2,1,0:T(8,128)(2,1)}), bf16[16,80,128]{2,1,0:T(8,128)(2,1)S(1)}, u32[]{:S(2)}, u32[]{:S(2)}) async-start(bf16[16,80,128]{2,1,0:T(8,128)(2,1)} %get-tuple-element.31), calls=%async_computation | async-start | bytes 655360 | tf_op jit(solution)/shard_map/all_to_all | solution.py:393
  10.9 0.0 copy-start.6
  10.9 0.7 copy-done.6
  11.5 0.2 copy.29
  11.8 0.0 copy-start
  11.8 0.1 copy.34
  11.9 0.8 %copy-done = bf16[4,64,256]{2,1,0:T(8,128)(2,1)S(1)} copy-done((bf16[4,64,256]{2,1,0:T(8,128)(2,1)S(1)}, bf16[4,64,256]{2,1,0:T(8,128)(2,1)}, u32[]{:S(2)}) %copy-start) | copy-done | bytes 131096
  12.7 0.2 copy.26
  12.9 0.2 copy.28
  13.1 0.1 fusion
  13.1 0.2 copy.30.w_two
  13.4 0.1 multiply_bitcast_fusion.w_three_t
  13.5 0.0 copy-start.4
  13.5 5.8 %all-to-all-done.recv = bf16[16,80,128]{2,1,0:T(8,128)(2,1)S(1)} async-done(((bf16[16,80,128]{2,1,0:T(8,128)(2,1)}), bf16[16,80,128]{2,1,0:T(8,128)(2,1)S(1)}, u32[]{:S(2)}, u32[]{:S(2)}) %all-to-all-start) | async-done | bytes 327712 | tf_op jit(solution)/shard_map/all_to_all | solution.py:393
  19.3 3.5 %shard_map.172 = (bf16[2,32,1024]{2,1,0:T(8,128)(2,1)S(1)}, f32[2,8,1024]{2,1,0:T(8,128)S(1)}, f32[2,8,1024]{2,1,0:T(8,128)S(1)}, bf16[8,168,128]{2,1,0:T(8,128)(2,1)S(1)}) custom-call(s32[1]{0:T(128)S(6)} %sub.3.half, bf16[16,80,128]{2,1,0:T(8,128)(2,1)S(1)} %all-to-all-done.recv, bf16[4,64,256]{2,1,0:T(8,128)(2,1)S(1)} %copy-done, ...), custom_call_target="tpu_custom_call" | custom-call | flops 2000000000 | tf_op jit(solution)/shard_map/pallas_call | solution.py:414
  22.8 1.9 %collective-permute-start = (bf16[8,168,128]{2,1,0:T(8,128)(2,1)S(1)}, bf16[8,168,128]{2,1,0:T(8,128)(2,1)S(1)}, u32[]{:S(2)}, u32[]{:S(2)}) collective-permute-start(bf16[8,168,128]{2,1,0:T(8,128)(2,1)S(1)} %get-tuple-element.44), channel_id=1, source_target_pairs={{0,16},{16,0},{32,48},{48,32},{64,80},{80,64},{96,112},{112,96},{1... | collective-permute-start | bytes 1032200 | tf_op jit(solution)/shard_map/ppermute | solution.py:415
  24.8 3.2 %shard_map.173 = (bf16[2,32,1024]{2,1,0:T(8,128)(2,1)S(1)}, f32[2,8,1024]{2,1,0:T(8,128)S(1)}, f32[2,8,1024]{2,1,0:T(8,128)S(1)}, bf16[2,256,1024]{2,1,0:T(8,128...) custom-call(s32[1]{0:T(128)} %bitcast.half, ...), custom_call_target="tpu_custom_call" | custom-call | flops 2000000000 | tf_op jit(solution)/shard_map/pallas_call | solution.py:416
  27.9 0.0 collective-permute-done.from_core
  28.0 1.7 %shard_map.175 = bf16[8,168,128]{2,1,0:T(8,128)(2,1)} custom-call(bf16[2,256,1024]{2,1,0:T(8,128)(2,1)S(1)} %get-tuple-element.38.act_one, bf16[2,256,1024]{2,1,0:T(8,128)(2,1)S(1)} %get-tuple-element.39.delta_two, bf16[2,8,1024]{2,1,0:T(8,128)(2,1)S(1)} %get-tuple-element.40.misfit, bf16[2,256,1024]{2,1,0:T(8,128)(2,1)S(1)} %get-tuple-element.41.act_two, ...), custom_call_target="tpu_custom_call" | custom-call | tf_op jit(solution)/shard_map/pallas_call | solution.py:419
  29.6 8.2 %all-to-all-start.1 = ((bf16[8,168,128]{2,1,0:T(8,128)(2,1)}), bf16[8,168,128]{2,1,0:T(8,128)(2,1)S(1)}, u32[]{:S(2)}, u32[]{:S(2)}) async-start(bf16[8,168,128]{2,1,0:T(8,128)(2,1)} %shard_map.175), calls=%async_computation.1 | async-start | bytes 688128 | tf_op jit(solution)/shard_map/all_to_all | solution.py:428
  37.8 2.0 %shard_map.174 = bf16[16,80,128]{2,1,0:T(8,128)(2,1)} custom-call(s32[1]{0:T(128)} %bitcast.half, bf16[2,32,1024]{2,1,0:T(8,128)(2,1)S(1)} %get-tuple-element.32.back_a, bf16[2,32,1024]{2,1,0:T(8,128)(2,1)S(1)} %get-tuple-element.33.back_b, f32[2,8,1024]{2,1,0:T(8,128)S(1)} %get-tuple-element.34.preds_a, f32[2,8,1024]{2,1,0:T(8,128)S(1)} %get-tuple-element.35.preds_b, ...), custom_call_target="tpu_custom_call" | custom-call | flops 2000000000 | tf_op jit(solution)/shard_map/pallas_call | solution.py:429
  39.9 12.1 %all-to-all-done.1 = bf16[8,168,128]{2,1,0:T(8,128)(2,1)S(1)} async-done(((bf16[8,168,128]{2,1,0:T(8,128)(2,1)}), bf16[8,168,128]{2,1,0:T(8,128)(2,1)S(1)}, u32[]{:S(2)}, u32[]{:S(2)}) %all-to-all-start.1) | async-done | bytes 344096 | tf_op jit(solution)/shard_map/all_to_all | solution.py:428
  52.0 0.1 reduce_sum.12
  52.0 3.6 %all-to-all-start.2 = ((bf16[16,80,128]{2,1,0:T(8,128)(2,1)}), bf16[16,80,128]{2,1,0:T(8,128)(2,1)S(1)}, u32[]{:S(2)}, u32[]{:S(2)}) async-start(bf16[16,80,128]{2,1,0:T(8,128)(2,1)} %shard_map.174), calls=%async_computation.2 | async-start | bytes 655360 | tf_op jit(solution)/shard_map/all_to_all | solution.py:438
  55.6 0.0 copy-start.1
  55.6 0.0 copy-start.2
  55.6 0.0 copy-start.3
  55.6 16.9 %all-gather = bf16[2688,128]{1,0:T(8,128)(2,1)S(1)} all-gather(bf16[168,128]{1,0:T(8,128)(2,1)S(1)} %reduce_sum.12), channel_id=2, replica_groups=mesh['rep'=16,'exp'=16] {'rep'}, dimensions={0}, use_global_device_ids=true | all-gather | bytes 731136 | tf_op jit(solution)/shard_map/all_gather | solution.py:439
  72.5 0.0 all-to-all-done.2.got
  72.5 1.5 %shard_map.176 = (f32[4,64,256]{2,1,0:T(8,128)}, f32[4,256,256]{2,1,0:T(8,128)}, f32[3,4,256]{2,1,0:T(4,128)}, f32[64,128]{1,0:T(8,128)}, f32[64,128]{1,0:T(8,12...) custom-call(bf16[16,168,128]{2,1,0:T(8,128)(2,1)S(1)} %bitcast.20, bf16[16,80,128]{2,1,0:T(8,128)(2,1)S(1)} %all-to-all-done.2.got, ...), custom_call_target="tpu_custom_call" | custom-call | tf_op jit(solution)/shard_map/pallas_call | solution.py:442
  (7 shorter events, 0.0 us)
Async XLA Ops:
  3.1 9.7 %copy-start.5 = (bf16[4,256,256]{2,1,0:T(8,128)(2,1)S(1)}, bf16[4,256,256]{2,1,0:T(8,128)(2,1)}, u32[]{:S(2)}) copy-start(bf16[4,256,256]{2,1,0:T(8,128)(2,1)} %param.16) | copy-start | bytes 1572868
  3.1 16.2 %all-to-all-start = ((bf16[16,80,128]{2,1,0:T(8,128)(2,1)}), bf16[16,80,128]{2,1,0:T(8,128)(2,1)S(1)}, u32[]{:S(2)}, u32[]{:S(2)}) async-start(bf16[16,80,128]{2,1,0:T(8,128)(2,1)} %get-tuple-element.31), calls=%async_computation | async-start | bytes 655360 | tf_op jit(solution)/shard_map/all_to_all | solution.py:393
  10.9 0.7 copy-start.6
  11.8 0.9 %copy-start = (bf16[4,64,256]{2,1,0:T(8,128)(2,1)S(1)}, bf16[4,64,256]{2,1,0:T(8,128)(2,1)}, u32[]{:S(2)}) copy-start(bf16[4,64,256]{2,1,0:T(8,128)(2,1)} %w_one.3) | copy-start | bytes 393220
  13.5 5.9 %copy-start.4 = (bf16[256,32]{0,1:T(8,128)(2,1)S(1)}, bf16[256,32]{0,1:T(8,128)(2,1)}, u32[]{:S(2)}) copy-start(bf16[256,32]{0,1:T(8,128)(2,1)} %param.18) | copy-start | bytes 49156
  22.8 5.1 %collective-permute-start = (bf16[8,168,128]{2,1,0:T(8,128)(2,1)S(1)}, bf16[8,168,128]{2,1,0:T(8,128)(2,1)S(1)}, u32[]{:S(2)}, u32[]{:S(2)}) collective-permute-start(bf16[8,168,128]{2,1,0:T(8,128)(2,1)S(1)} %get-tuple-element.44), channel_id=1, source_target_pairs={{0,16},{16,0},{32,48},{48,32},{64,80},{80,64},{96,112},{112,96},{1... | collective-permute-start | bytes 1032200 | tf_op jit(solution)/shard_map/ppermute | solution.py:415
  29.6 22.3 %all-to-all-start.1 = ((bf16[8,168,128]{2,1,0:T(8,128)(2,1)}), bf16[8,168,128]{2,1,0:T(8,128)(2,1)S(1)}, u32[]{:S(2)}, u32[]{:S(2)}) async-start(bf16[8,168,128]{2,1,0:T(8,128)(2,1)} %shard_map.175), calls=%async_computation.1 | async-start | bytes 688128 | tf_op jit(solution)/shard_map/all_to_all | solution.py:428
  52.0 20.5 %all-to-all-start.2 = ((bf16[16,80,128]{2,1,0:T(8,128)(2,1)}), bf16[16,80,128]{2,1,0:T(8,128)(2,1)S(1)}, u32[]{:S(2)}, u32[]{:S(2)}) async-start(bf16[16,80,128]{2,1,0:T(8,128)(2,1)} %shard_map.174), calls=%async_computation.2 | async-start | bytes 655360 | tf_op jit(solution)/shard_map/all_to_all | solution.py:438
  55.6 16.9 %copy-start.1 = (f32[2,32,128]{2,1,0:T(8,128)S(1)}, f32[2,32,128]{2,1,0:T(8,128)}, u32[]{:S(2)}) copy-start(f32[2,32,128]{2,1,0:T(8,128)} %param.12) | copy-start | bytes 98308
  55.6 16.9 %copy-start.2 = (f32[2,32,128]{2,1,0:T(8,128)S(1)}, f32[2,32,128]{2,1,0:T(8,128)}, u32[]{:S(2)}) copy-start(f32[2,32,128]{2,1,0:T(8,128)} %param.13) | copy-start | bytes 98308
  55.6 16.9 %copy-start.3 = (f32[2,32,128]{2,1,0:T(8,128)S(1)}, f32[2,32,128]{2,1,0:T(8,128)}, u32[]{:S(2)}) copy-start(f32[2,32,128]{2,1,0:T(8,128)} %param.14) | copy-start | bytes 98308

commit v5 on v3

--- a/solution.py
+++ b/solution.py
@@ -1,3 +1,5 @@
+import functools
+
 import jax
 import jax.numpy as jnp
 from jax import lax
@@ -129,9 +131,10 @@
 
 
 def half_kernel(
-    half, recv, w_one, w_one_t, w_two, w_two_t, w_three, w_three_t, dir_t, grads, back, preds, index, tex
+    keep, position, recv, w_one, w_one_t, w_two, w_two_t, w_three, w_three_t, dir_t, grads, back, preds, index, tex
 ):
-    h = half[0]
+    core = position[0] & 1
+    h = core if keep else 1 - core
     for b in range(4):
         for s in range(4):
             tex[b * TEX_ROWS : (b + 1) * TEX_ROWS, s * LANES : (s + 1) * LANES] = recv[4 * b + s, :TEX_ROWS]
@@ -201,7 +204,7 @@
         back[b, :, c * width : (c + 1) * width] = dot(w_one[2 * h + b, :LAT], delta_one[n]).astype(bf16)
 
 
-def texels_kernel(half, back_a, back_b, preds_a, preds_b, index_a, index_b, out):
+def texels_kernel(position, back_a, back_b, preds_a, preds_b, index_a, index_b, *outs):
     acc = jnp.zeros((GROUPS * LAT, LOW), f32)
     for rows_back, index in ((back_a, index_a), (back_b, index_b)):
         for b in range(2):
@@ -214,11 +217,12 @@
                 for r in range(GROUPS)
             ]
             acc = acc + dot_nt(jnp.concatenate(spread, axis=0), low_hot)
-    for b in range(4):
-        for s in range(4):
-            out[4 * b + s, :TEX_ROWS] = acc[b * TEX_ROWS : (b + 1) * TEX_ROWS, s * LANES : (s + 1) * LANES].astype(bf16)
+    *outs, packets = outs
+    for y in range(4):
+        for x in range(4):
+            packets[x, y, :TEX_ROWS] = acc[y * TEX_ROWS : (y + 1) * TEX_ROWS, x * LANES : (x + 1) * LANES].astype(bf16)
     left = iota((8, LANES), 1) < CAP
-    keep = half[0]
+    keep = position[0] & 1
     for j in range(N_EXP // 2):
         cols = slice(j * LANES, (j + 1) * LANES)
         low, high = [], []
@@ -227,15 +231,29 @@
             two = jnp.where(keep == h, preds_b[1, :, cols], preds_a[1, :, cols])
             low.append(jnp.where(left, one, pltpu.roll(two, CAP, 1)))
             high.append(jnp.where(left, pltpu.roll(one, CAP, 1), two))
-        out[2 * j, TEX_ROWS:] = jnp.concatenate(low, axis=0).astype(bf16)
-        out[2 * j + 1, TEX_ROWS:] = jnp.concatenate(high, axis=0).astype(bf16)
+        packets[2 * j % 4, j // 2, TEX_ROWS:] = jnp.concatenate(low, axis=0).astype(bf16)
+        packets[2 * j % 4 + 1, j // 2, TEX_ROWS:] = jnp.concatenate(high, axis=0).astype(bf16)
+    x = position[1] & 3
+    for d in range(4):
+        outs[d][...] = packets[(x + d) & 3]
+
+
+def relay_kernel(position, own, one, two, three, *outs):
+    y = position[1] >> 2
+    for d in range(4):
+        to = (y + d) & 3
+        parts = [part[to] for part in (own, one, two, three)]
+        outs[d][:TEX_ROWS] = sum(part[:TEX_ROWS].astype(f32) for part in parts).astype(bf16)
+        for n in range(4):
+            outs[d][TEX_ROWS + 16 * n : TEX_ROWS + 16 * (n + 1)] = parts[n][TEX_ROWS:]
 
 
 def finish_kernel(
-    packed, got, slot, latents, mean, square, out_one, out_two, out_three, out_latents, out_mean, out_square, out_pred, *scratch
+    position, packed, got_own, got_one, got_two, got_three, slot, latents, mean, square, out_one, out_two, out_three, out_latents, out_mean, out_square, out_pred, *scratch
 ):
-    grad_one, grad_two, grad_three, new_latents, new_mean, new_square, predictions, sems = scratch
+    grad_one, grad_two, grad_three, new_latents, new_mean, new_square, predictions, preds, sems = scratch
     copies = []
+    gots = (got_own, got_one, got_two, got_three)
 
     def leave(source, target):
         copies.append(pltpu.make_async_copy(source, target, sems.at[len(copies)]))
@@ -254,9 +272,7 @@
         leave(grad_two.at[e], out_two.at[e])
     leave(grad_one, out_one)
     leave(grad_three, out_three)
-    texel_grad = jnp.zeros((TEX_ROWS, LANES), f32)
-    for j in range(N_EXP):
-        texel_grad = texel_grad + got[j, :TEX_ROWS].astype(f32)
+    texel_grad = sum(got[:TEX_ROWS].astype(f32) for got in gots)
     next_mean = decay_one * mean[...] + (1.0 - decay_one) * texel_grad
     next_square = decay_two * square[...] + (1.0 - decay_two) * texel_grad * texel_grad
     new_mean[...] = next_mean
@@ -265,7 +281,12 @@
     leave(new_mean, out_mean)
     leave(new_square, out_square)
     leave(new_latents, out_latents)
-    table = jnp.concatenate([got[j, TEX_ROWS:] for j in range(N_EXP)], axis=0)
+    y, x = position[1] >> 2, position[1] & 3
+    for back_y in range(4):
+        for back_x in range(4):
+            first = TEX_ROWS + 16 * back_x
+            preds[((y - back_y) & 3) * 4 + ((x - back_x) & 3)] = gots[back_y][first : first + 16]
+    table = preds[...].reshape(N_EXP * 16, LANES)
     place = slot[...]
     lane = place & (LANES - 1)
     pair = place >> 7
@@ -291,7 +312,7 @@
         kernel,
         out_shape=outs,
         scratch_shapes=list(scratch),
-        compiler_params=pltpu.CompilerParams(vmem_limit_bytes=48 << 20),
+        compiler_params=pltpu.CompilerParams(vmem_limit_bytes=32 << 20),
         cost_estimate=cost,
         **more,
     )
@@ -342,9 +363,9 @@
         jnp.swapaxes(three, 1, 2) * 0.5,
         dir_table.T,
     )
-    core = (lax.axis_index("rep") % 2).astype(jnp.int32).reshape(1)
-    half = lambda kind: call(
-        half_kernel,
+    position = jnp.stack([lax.axis_index("rep"), lax.axis_index("exp")]).astype(jnp.int32)
+    half = lambda keep, kind: call(
+        functools.partial(half_kernel, keep),
         (
             shape((N_REP // 2, GRAD_ROWS, LANES), kind),
             shape((2, LAT, SLOTS), bf16),
@@ -355,33 +376,43 @@
         [smem] + [vmem] * 8,
         2000000000,
     )
-    grads_a, back_a, preds_a, index_a = half(bf16)(1 - core, recv, *weights)
+    grads_a, back_a, preds_a, index_a = half(False, bf16)(position, recv, *weights)
     from_core = lax.ppermute(grads_a, "rep", [(i, i ^ 1) for i in range(N_REP)])
-    grads_b, back_b, preds_b, index_b = half(f32)(core, recv, *weights)
+    grads_b, back_b, preds_b, index_b = half(True, f32)(position, recv, *weights)
     chip = (grads_b + from_core.astype(f32)).astype(bf16)
     chips = [list(range(c, N_REP, 2)) for c in range(2)]
     parts = lax.all_to_all(chip, "rep", 0, 0, tiled=True, axis_index_groups=chips)
-    back = call(
+    along = lambda step_y, step_x: [
+        (4 * y + x, 4 * ((y + step_y) % 4) + (x + step_x) % 4) for y in range(4) for x in range(4)
+    ]
+    rows_x = call(
         texels_kernel,
-        shape((N_EXP, SEND_ROWS, LANES), bf16),
-        (),
+        tuple([shape((4, SEND_ROWS, LANES), bf16)] * 4),
+        [pltpu.VMEM((4, 4, SEND_ROWS, LANES), bf16)],
         [smem] + [vmem] * 6,
         2000000000,
-    )(core, back_a, back_b, preds_a, preds_b, index_a, index_b)
+    )(position, back_a, back_b, preds_a, preds_b, index_a, index_b)
+    got_x = [lax.ppermute(rows_x[d], "exp", along(0, d)) for d in (1, 2, 3)]
+    rows_y = call(
+        relay_kernel,
+        tuple([shape((TEX_ROWS + 64, LANES), bf16)] * 4),
+        (),
+        [smem] + [vmem] * 4,
+    )(position, rows_x[0], *got_x)
+    got_y = [lax.ppermute(rows_y[d], "exp", along(d, 0)) for d in (1, 2, 3)]
     own = jnp.sum(parts.astype(f32), axis=0).astype(bf16)
-    back, own = lax.optimization_barrier((back, own))
-    got = lax.all_to_all(back, "exp", 0, 0, tiled=True)
     packed = lax.all_gather(own, "rep", axis=0, tiled=False)
     plane = (TEX_ROWS, LANES)
     outs = (weight_one.shape, weight_two.shape, (OUTC, 4, HID), plane, plane, plane, (OUTC, ROWS))
     grad_one, grad_two, grad_three, new_latents, new_mean, new_square, predictions = call(
         finish_kernel,
         tuple(shape(dims) for dims in outs),
-        [pltpu.VMEM(dims, f32) for dims in outs] + [pltpu.SemaphoreType.DMA((10,))],
-        [vmem] * 6,
+        [pltpu.VMEM(dims, f32) for dims in outs]
+        + [pltpu.VMEM((N_EXP, 16, LANES), bf16), pltpu.SemaphoreType.DMA((10,))],
+        [smem] + [vmem] * 9,
         0,
         tuple([hbm] * 7),
-    )(packed, got, slot, flat(latents), flat(latent_mean), flat(latent_square))
+    )(position, packed, rows_y[0], *got_y, slot, flat(latents), flat(latent_mean), flat(latent_square))
     grad_three = jnp.swapaxes(grad_three, 0, 1)
     whole = lambda a: a.reshape(latents.shape)
     return (

time: 74.1 us -> 74.4 us (level)
  waiting for transfers between devices: 17.9 us -> 12.4 us
  blocking collectives: 16.9 us -> 19.2 us
  Pallas kernels: 13.1 us -> 15.2 us
  starting transfers between devices: 21.4 us -> 23.3 us
    all_to_all x1, waiting for transfers between devices: 12.1 us -> 1.84 us  [on_device(): lax.all_to_all(chip, 'rep', 0, 0, tiled=True, axis_index_groups=chips)]
    ppermute x0 -> x6, starting transfers between devices: none -> 5.61 us  [the longest x3 2.86 us: on_device(): got_x = [lax.ppermute(rows_x[d], 'exp', along(0, d)) for d in (1, 2, 3)]]
    ppermute x0 -> x6, waiting for transfers between devices: none -> 4.17 us  [the longest x3 4.17 us: on_device(): got_x = [lax.ppermute(rows_x[d], 'exp', along(0, d)) for d in (1, 2, 3)]]
    all_to_all x1 -> x0, starting transfers between devices: 3.55 us -> none  [on_device(): got = lax.all_to_all(back, 'exp', 0, 0, tiled=True)]
    all_gather x1, blocking collectives: 16.9 us -> 19.2 us  [on_device(): packed = lax.all_gather(own, 'rep', axis=0, tiled=False)]
    pallas_call x3 -> x4, Pallas kernels: 9.05 us -> 10.6 us  [the longest x1 4.07 us: on_device(): half(False, bf16)(position, recv, *weights)]
  transfers between devices with their start and end apart: 4 -> 9, of which waited for: 2 -> 4; matrix products, arithmetic and copies ran while one was open for 2% -> 2% of each run, Pallas kernels for 8% -> 9%
where the time goes in v5:
time: 74.4 us; the launch traced here: 74 us
  starting transfers between devices  23.3 us (31%)
  blocking collectives  19.2 us (26%)
  Pallas kernels  15.2 us (20%)
  waiting for transfers between devices  12.4 us (17%)
  local copies, waits for them, and re-layouts  1.83 us (2%)
  other arithmetic  1.11 us (1%)
  between operations  0.98 us (1%)
    all_gather x1, blocking collectives, on_device(): packed = lax.all_gather(own, 'rep', axis=0, tiled=False)  19.2 us
    all_to_all x1, starting transfers between devices, on_device(): lax.all_to_all(chip, 'rep', 0, 0, tiled=True, axis_index_groups=chips)  8.18 us
    all_to_all x1, starting transfers between devices, on_device(): recv = lax.all_to_all(send, 'exp', 0, 0, tiled=True)  7.59 us
    all_to_all x1, waiting for transfers between devices, on_device(): recv = lax.all_to_all(send, 'exp', 0, 0, tiled=True)  6.35 us
    ppermute x3, waiting for transfers between devices, on_device(): got_x = [lax.ppermute(rows_x[d], 'exp', along(0, d)) for d in (1, 2, 3)]  4.17 us
    pallas_call x1, Pallas kernels, on_device(): half(False, bf16)(position, recv, *weights)  4.07 us
    pallas_call x1, Pallas kernels, on_device(): half(True, f32)(position, recv, *weights)  4.06 us
    ppermute x3, starting transfers between devices, on_device(): got_x = [lax.ppermute(rows_x[d], 'exp', along(0, d)) for d in (1, 2, 3)]  2.86 us
  transfers between devices with their start and end apart: 9, of which 4 were waited for; matrix products, arithmetic and copies ran while one was open for 2% of the time, Pallas kernels for 9%

profile of v5, /device:TPU:1, one launch (start us, length us, event | category | flops | bytes accessed | tf_op | source)
XLA Modules:
  0.0 74.0 jit_solution(1181073310751657961)
XLA Ops:
  0.6 2.5 %shard_map.171 = (bf16[16,80,128]{2,1,0:T(8,128)(2,1)}, s32[16,128]{1,0:T(8,128)S(1)}) custom-call(s32[16,128]{1,0:T(8,128)} %bitcast.28, s32[16,128]{1,0:T(8,128)} %bitcast.29, s32[16,128]{1,0:T(8,128)} %bitcast.30, s32[16,128]{1,0:T(8,128)} %bitcast.31, f32[3,2048]{1,0:T(4,128)} %targets_in.1, f32[64,128]{1,0:T(8,128)} %bitcast.22), custom_call_target="tpu_custom_call" | custom-call | tf_op jit(solution)/shard_map/pallas_call | solution.py:345
  3.1 7.6 %all-to-all-start = ((bf16[16,80,128]{2,1,0:T(8,128)(2,1)}), bf16[16,80,128]{2,1,0:T(8,128)(2,1)S(1)}, u32[]{:S(2)}, u32[]{:S(2)}) async-start(bf16[16,80,128]{2,1,0:T(8,128)(2,1)} %get-tuple-element.32), calls=%async_computation | async-start | bytes 655360 | tf_op jit(solution)/shard_map/all_to_all | solution.py:355
  10.7 0.2 copy.29
  10.9 0.1 copy.34
  11.1 0.1 multiply_bitcast_fusion.w_three_t
  11.2 0.8 %copy-done = bf16[4,64,256]{2,1,0:T(8,128)(2,1)S(1)} copy-done((bf16[4,64,256]{2,1,0:T(8,128)(2,1)S(1)}, bf16[4,64,256]{2,1,0:T(8,128)(2,1)}, u32[]{:S(2)}) %copy-start) | copy-done | bytes 131096
  12.0 0.2 copy.26
  12.2 0.0 copy-done.5
  12.2 0.2 copy.28
  12.4 0.1 fusion
  12.5 0.2 copy.30.w_two
  12.7 0.1 pad_add_fusion.position
  12.8 6.3 %all-to-all-done.recv = bf16[16,80,128]{2,1,0:T(8,128)(2,1)S(1)} async-done(((bf16[16,80,128]{2,1,0:T(8,128)(2,1)}), bf16[16,80,128]{2,1,0:T(8,128)(2,1)S(1)}, u32[]{:S(2)}, u32[]{:S(2)}) %all-to-all-start) | async-done | bytes 327712 | tf_op jit(solution)/shard_map/all_to_all | solution.py:355
  19.2 4.1 %shard_map.173 = (bf16[8,168,128]{2,1,0:T(8,128)(2,1)S(1)}, bf16[2,32,1024]{2,1,0:T(8,128)(2,1)S(1)}, f32[2,8,1024]{2,1,0:T(8,128)S(1)}, f32[2,8,1024]{2,1,0:T(8,128)S(1)}) custom-call(s32[2]{0:T(128)S(1)} %pad_add_fusion.position, bf16[16,80,128]{2,1,0:T(8,128)(2,1)S(1)} %all-to-all-done.recv, bf16[4,64,256]{2,1,0:T(8,128)(2,1)S(1)} %copy-done, ...), custom_call_target="tpu_custom_call" | custom-call | flops 2000000000 | tf_op jit(solution)/shard_map/pallas_call | solution.py:379
  23.3 1.9 %collective-permute-start = (bf16[8,168,128]{2,1,0:T(8,128)(2,1)S(1)}, bf16[8,168,128]{2,1,0:T(8,128)(2,1)S(1)}, u32[]{:S(2)}, u32[]{:S(2)}) collective-permute-start(bf16[8,168,128]{2,1,0:T(8,128)(2,1)S(1)} %get-tuple-element.34), channel_id=1, source_target_pairs={{0,16},{16,0},{32,48},{48,32},{64,80},{80,64},{96,112},{112,96},{1... | collective-permute-start | bytes 1032200 | tf_op jit(solution)/shard_map/ppermute | solution.py:380
  25.2 4.1 %shard_map.172 = (f32[8,168,128]{2,1,0:T(8,128)S(1)}, bf16[2,32,1024]{2,1,0:T(8,128)(2,1)S(1)}, f32[2,8,1024]{2,1,0:T(8,128)S(1)}, f32[2,8,1024]{2,1,0:T(8,128)S(1)}) custom-call(s32[2]{0:T(128)S(1)} %pad_add_fusion.position, bf16[16,80,128]{2,1,0:T(8,128)(2,1)S(1)} %all-to-all-done.recv, bf16[4,64,256]{2,1,0:T(8,128)(2,1)S(1)} %copy-done, ...), custom_call_target="tpu_custom_call" | custom-call | flops 2000000000 | tf_op jit(solution)/shard_map/pallas_call | solution.py:381
  29.3 0.8 %add_convert_fusion = bf16[8,168,128]{2,1,0:T(8,128)(2,1)} fusion(f32[8,168,128]{2,1,0:T(8,128)S(1)} %get-tuple-element.33, bf16[8,168,128]{2,1,0:T(8,128)(2,1)S(1)} %collective-permute-done), kind=kLoop, calls=%fused_computation | loop fusion | flops 516096 | bytes 1376256 | tf_op jit(solution)/shard_map/convert_element_type | solution.py:382
  30.1 8.2 %all-to-all-start.1 = ((bf16[8,168,128]{2,1,0:T(8,128)(2,1)}), bf16[8,168,128]{2,1,0:T(8,128)(2,1)S(1)}, u32[]{:S(2)}, u32[]{:S(2)}) async-start(bf16[8,168,128]{2,1,0:T(8,128)(2,1)} %add_convert_fusion), calls=%async_computation.1 | async-start | bytes 688128 | tf_op jit(solution)/shard_map/all_to_all | solution.py:384
  38.3 1.9 %shard_map.174 = (bf16[4,80,128]{2,1,0:T(8,128)(2,1)S(1)}, bf16[4,80,128]{2,1,0:T(8,128)(2,1)S(1)}, bf16[4,80,128]{2,1,0:T(8,128)(2,1)S(1)}, bf16[4,80,128]{2,1,0:T(8,128)(2,1)S(1)}) custom-call(s32[2]{0:T(128)S(1)} %pad_add_fusion.position, bf16[2,32,1024]{2,1,0:T(8,128)(2,1)S(1)} %get-tuple-element.35.back_a, ...), custom_call_target="tpu_custom_call" | custom-call | flops 2000000000 | tf_op jit(solution)/shard_map/pallas_call | solution.py:388
  40.2 0.4 collective-permute-start.1
  40.5 1.2 %collective-permute-start.2 = (bf16[4,80,128]{2,1,0:T(8,128)(2,1)S(1)}, bf16[4,80,128]{2,1,0:T(8,128)(2,1)S(1)}, u32[]{:S(2)}, u32[]{:S(2)}) collective-permute-start(bf16[4,80,128]{2,1,0:T(8,128)(2,1)S(1)} %get-tuple-element.43), channel_id=1, source_target_pairs={{0,2},{1,3},{2,0},{3,1},{4,6},{5,7},{6,4},{7,5},{8,10},{9,11},{10,... | collective-permute-start | bytes 245768 | tf_op jit(solution)/shard_map/ppermute | solution.py:395
  41.8 1.3 %collective-permute-start.3 = (bf16[4,80,128]{2,1,0:T(8,128)(2,1)S(1)}, bf16[4,80,128]{2,1,0:T(8,128)(2,1)S(1)}, u32[]{:S(2)}, u32[]{:S(2)}) collective-permute-start(bf16[4,80,128]{2,1,0:T(8,128)(2,1)S(1)} %get-tuple-element.44), channel_id=1, source_target_pairs={{0,3},{1,0},{2,1},{3,2},{4,7},{5,4},{6,5},{7,6},{8,11},{9,8},{10,9... | collective-permute-start | bytes 245768 | tf_op jit(solution)/shard_map/ppermute | solution.py:395
  43.0 4.0 %collective-permute-done.1.one = bf16[4,80,128]{2,1,0:T(8,128)(2,1)S(1)} collective-permute-done((bf16[4,80,128]{2,1,0:T(8,128)(2,1)S(1)}, bf16[4,80,128]{2,1,0:T(8,128)(2,1)S(1)}, u32[]{:S(2)}, u32[]{:S(2)}) %collective-permute-start.1) | collective-permute-done | bytes 81952 | tf_op jit(solution)/shard_map/ppermute | solution.py:395
  47.0 0.2 collective-permute-done.3.three
  47.2 0.6 shard_map.175
  47.8 0.1 collective-permute-start.4
  47.9 1.7 %collective-permute-start.5 = (bf16[128,128]{1,0:T(8,128)(2,1)S(1)}, bf16[128,128]{1,0:T(8,128)(2,1)S(1)}, u32[]{:S(2)}, u32[]{:S(2)}) collective-permute-start(bf16[128,128]{1,0:T(8,128)(2,1)S(1)} %get-tuple-element.47), channel_id=1, source_target_pairs={{0,8},{1,9},{2,10},{3,11},{4,12},{5,13},{6,14},{7,15},{8,0},{9,1},... | collective-permute-start | bytes 98312 | tf_op jit(solution)/shard_map/ppermute | solution.py:402
  49.6 0.9 %collective-permute-start.6 = (bf16[128,128]{1,0:T(8,128)(2,1)S(1)}, bf16[128,128]{1,0:T(8,128)(2,1)S(1)}, u32[]{:S(2)}, u32[]{:S(2)}) collective-permute-start(bf16[128,128]{1,0:T(8,128)(2,1)S(1)} %get-tuple-element.48), channel_id=1, source_target_pairs={{0,12},{1,13},{2,14},{3,15},{4,0},{5,1},{6,2},{7,3},{8,4},{9,5},{1... | collective-permute-start | bytes 98312 | tf_op jit(solution)/shard_map/ppermute | solution.py:402
  50.5 1.8 %all-to-all-done.1 = bf16[8,168,128]{2,1,0:T(8,128)(2,1)S(1)} async-done(((bf16[8,168,128]{2,1,0:T(8,128)(2,1)}), bf16[8,168,128]{2,1,0:T(8,128)(2,1)S(1)}, u32[]{:S(2)}, u32[]{:S(2)}) %all-to-all-start.1) | async-done | bytes 344096 | tf_op jit(solution)/shard_map/all_to_all | solution.py:384
  52.4 0.1 reduce_sum.12
  52.5 19.2 %all-gather = bf16[2688,128]{1,0:T(8,128)(2,1)S(1)} all-gather(bf16[168,128]{1,0:T(8,128)(2,1)S(1)} %reduce_sum.12), channel_id=2, replica_groups=mesh['rep'=16,'exp'=16] {'rep'}, dimensions={0}, use_global_device_ids=true | all-gather | bytes 731136 | tf_op jit(solution)/shard_map/all_gather | solution.py:404
  71.7 2.1 %shard_map.176 = (f32[4,64,256]{2,1,0:T(8,128)}, f32[4,256,256]{2,1,0:T(8,128)}, f32[3,4,256]{2,1,0:T(4,128)}, f32[64,128]{1,0:T(8,128)}, f32[64,128]{1,0:T(8,12...) custom-call(s32[2]{0:T(128)S(1)} %pad_add_fusion.position, bf16[16,168,128]{2,1,0:T(8,128)(2,1)S(1)} %bitcast.21, ...), custom_call_target="tpu_custom_call" | custom-call | tf_op jit(solution)/shard_map/pallas_call | solution.py:407
  (19 shorter events, 0.1 us)
Async XLA Ops:
  3.1 7.6 %copy-start.6 = (bf16[4,3,256]{2,0,1:T(4,128)(2,1)S(1)}, bf16[4,3,256]{2,0,1:T(4,128)(2,1)}, u32[]{:S(2)}) copy-start(bf16[4,3,256]{2,0,1:T(4,128)(2,1)} %param.17) | copy-start | bytes 18436
  3.1 16.1 %all-to-all-start = ((bf16[16,80,128]{2,1,0:T(8,128)(2,1)}), bf16[16,80,128]{2,1,0:T(8,128)(2,1)S(1)}, u32[]{:S(2)}, u32[]{:S(2)}) async-start(bf16[16,80,128]{2,1,0:T(8,128)(2,1)} %get-tuple-element.32), calls=%async_computation | async-start | bytes 655360 | tf_op jit(solution)/shard_map/all_to_all | solution.py:355
  11.1 0.9 %copy-start = (bf16[4,64,256]{2,1,0:T(8,128)(2,1)S(1)}, bf16[4,64,256]{2,1,0:T(8,128)(2,1)}, u32[]{:S(2)}) copy-start(bf16[4,64,256]{2,1,0:T(8,128)(2,1)} %w_one.3) | copy-start | bytes 393220
  11.1 1.1 %copy-start.5 = (bf16[4,256,256]{2,1,0:T(8,128)(2,1)S(1)}, bf16[4,256,256]{2,1,0:T(8,128)(2,1)}, u32[]{:S(2)}) copy-start(bf16[4,256,256]{2,1,0:T(8,128)(2,1)} %param.16) | copy-start | bytes 1572868
  12.8 6.4 %copy-start.4 = (bf16[256,32]{0,1:T(8,128)(2,1)S(1)}, bf16[256,32]{0,1:T(8,128)(2,1)}, u32[]{:S(2)}) copy-start(bf16[256,32]{0,1:T(8,128)(2,1)} %param.18) | copy-start | bytes 49156
  23.3 6.0 %collective-permute-start = (bf16[8,168,128]{2,1,0:T(8,128)(2,1)S(1)}, bf16[8,168,128]{2,1,0:T(8,128)(2,1)S(1)}, u32[]{:S(2)}, u32[]{:S(2)}) collective-permute-start(bf16[8,168,128]{2,1,0:T(8,128)(2,1)S(1)} %get-tuple-element.34), channel_id=1, source_target_pairs={{0,16},{16,0},{32,48},{48,32},{64,80},{80,64},{96,112},{112,96},{1... | collective-permute-start | bytes 1032200 | tf_op jit(solution)/shard_map/ppermute | solution.py:380
  30.1 22.3 %all-to-all-start.1 = ((bf16[8,168,128]{2,1,0:T(8,128)(2,1)}), bf16[8,168,128]{2,1,0:T(8,128)(2,1)S(1)}, u32[]{:S(2)}, u32[]{:S(2)}) async-start(bf16[8,168,128]{2,1,0:T(8,128)(2,1)} %add_convert_fusion), calls=%async_computation.1 | async-start | bytes 688128 | tf_op jit(solution)/shard_map/all_to_all | solution.py:384
  40.2 6.9 %collective-permute-start.1 = (bf16[4,80,128]{2,1,0:T(8,128)(2,1)S(1)}, bf16[4,80,128]{2,1,0:T(8,128)(2,1)S(1)}, u32[]{:S(2)}, u32[]{:S(2)}) collective-permute-start(bf16[4,80,128]{2,1,0:T(8,128)(2,1)S(1)} %get-tuple-element.42), channel_id=1, source_target_pairs={{0,1},{1,2},{2,3},{3,0},{4,5},{5,6},{6,7},{7,4},{8,9},{9,10},{10,1... | collective-permute-start | bytes 245768 | tf_op jit(solution)/shard_map/ppermute | solution.py:395
  40.5 6.5 %collective-permute-start.2 = (bf16[4,80,128]{2,1,0:T(8,128)(2,1)S(1)}, bf16[4,80,128]{2,1,0:T(8,128)(2,1)S(1)}, u32[]{:S(2)}, u32[]{:S(2)}) collective-permute-start(bf16[4,80,128]{2,1,0:T(8,128)(2,1)S(1)} %get-tuple-element.43), channel_id=1, source_target_pairs={{0,2},{1,3},{2,0},{3,1},{4,6},{5,7},{6,4},{7,5},{8,10},{9,11},{10,... | collective-permute-start | bytes 245768 | tf_op jit(solution)/shard_map/ppermute | solution.py:395
  41.8 5.4 %collective-permute-start.3 = (bf16[4,80,128]{2,1,0:T(8,128)(2,1)S(1)}, bf16[4,80,128]{2,1,0:T(8,128)(2,1)S(1)}, u32[]{:S(2)}, u32[]{:S(2)}) collective-permute-start(bf16[4,80,128]{2,1,0:T(8,128)(2,1)S(1)} %get-tuple-element.44), channel_id=1, source_target_pairs={{0,3},{1,0},{2,1},{3,2},{4,7},{5,4},{6,5},{7,6},{8,11},{9,8},{10,9... | collective-permute-start | bytes 245768 | tf_op jit(solution)/shard_map/ppermute | solution.py:395
  47.8 23.9 %collective-permute-start.4 = (bf16[128,128]{1,0:T(8,128)(2,1)S(1)}, bf16[128,128]{1,0:T(8,128)(2,1)S(1)}, u32[]{:S(2)}, u32[]{:S(2)}) collective-permute-start(bf16[128,128]{1,0:T(8,128)(2,1)S(1)} %get-tuple-element.46), channel_id=1, source_target_pairs={{0,4},{1,5},{2,6},{3,7},{4,8},{5,9},{6,10},{7,11},{8,12},{9,13},{1... | collective-permute-start | bytes 98312 | tf_op jit(solution)/shard_map/ppermute | solution.py:402
  47.9 23.8 %collective-permute-start.5 = (bf16[128,128]{1,0:T(8,128)(2,1)S(1)}, bf16[128,128]{1,0:T(8,128)(2,1)S(1)}, u32[]{:S(2)}, u32[]{:S(2)}) collective-permute-start(bf16[128,128]{1,0:T(8,128)(2,1)S(1)} %get-tuple-element.47), channel_id=1, source_target_pairs={{0,8},{1,9},{2,10},{3,11},{4,12},{5,13},{6,14},{7,15},{8,0},{9,1},... | collective-permute-start | bytes 98312 | tf_op jit(solution)/shard_map/ppermute | solution.py:402
  49.6 22.1 %collective-permute-start.6 = (bf16[128,128]{1,0:T(8,128)(2,1)S(1)}, bf16[128,128]{1,0:T(8,128)(2,1)S(1)}, u32[]{:S(2)}, u32[]{:S(2)}) collective-permute-start(bf16[128,128]{1,0:T(8,128)(2,1)S(1)} %get-tuple-element.48), channel_id=1, source_target_pairs={{0,12},{1,13},{2,14},{3,15},{4,0},{5,1},{6,2},{7,3},{8,4},{9,5},{1... | collective-permute-start | bytes 98312 | tf_op jit(solution)/shard_map/ppermute | solution.py:402
  52.4 19.3 %copy-start.1 = (f32[2,32,128]{2,1,0:T(8,128)S(1)}, f32[2,32,128]{2,1,0:T(8,128)}, u32[]{:S(2)}) copy-start(f32[2,32,128]{2,1,0:T(8,128)} %param.12) | copy-start | bytes 98308
  52.5 19.3 %copy-start.2 = (f32[2,32,128]{2,1,0:T(8,128)S(1)}, f32[2,32,128]{2,1,0:T(8,128)}, u32[]{:S(2)}) copy-start(f32[2,32,128]{2,1,0:T(8,128)} %param.13) | copy-start | bytes 98308
  52.5 19.3 %copy-start.3 = (f32[2,32,128]{2,1,0:T(8,128)S(1)}, f32[2,32,128]{2,1,0:T(8,128)}, u32[]{:S(2)}) copy-start(f32[2,32,128]{2,1,0:T(8,128)} %param.14) | copy-start | bytes 98308

commit v6 on v5

--- a/solution.py
+++ b/solution.py
@@ -131,9 +131,9 @@
 
 
 def half_kernel(
-    keep, position, recv, w_one, w_one_t, w_two, w_two_t, w_three, w_three_t, dir_t, grads, back, preds, index, tex
+    keep, core_at, recv, w_one, w_one_t, w_two, w_two_t, w_three, w_three_t, dir_t, grads, back, preds, index, tex
 ):
-    core = position[0] & 1
+    core = core_at[0]
     h = core if keep else 1 - core
     for b in range(4):
         for s in range(4):
@@ -204,7 +204,7 @@
         back[b, :, c * width : (c + 1) * width] = dot(w_one[2 * h + b, :LAT], delta_one[n]).astype(bf16)
 
 
-def texels_kernel(position, back_a, back_b, preds_a, preds_b, index_a, index_b, *outs):
+def texels_kernel(core_at, x_at, back_a, back_b, preds_a, preds_b, index_a, index_b, *outs):
     acc = jnp.zeros((GROUPS * LAT, LOW), f32)
     for rows_back, index in ((back_a, index_a), (back_b, index_b)):
         for b in range(2):
@@ -222,7 +222,7 @@
         for x in range(4):
             packets[x, y, :TEX_ROWS] = acc[y * TEX_ROWS : (y + 1) * TEX_ROWS, x * LANES : (x + 1) * LANES].astype(bf16)
     left = iota((8, LANES), 1) < CAP
-    keep = position[0] & 1
+    keep = core_at[0]
     for j in range(N_EXP // 2):
         cols = slice(j * LANES, (j + 1) * LANES)
         low, high = [], []
@@ -233,13 +233,13 @@
             high.append(jnp.where(left, pltpu.roll(one, CAP, 1), two))
         packets[2 * j % 4, j // 2, TEX_ROWS:] = jnp.concatenate(low, axis=0).astype(bf16)
         packets[2 * j % 4 + 1, j // 2, TEX_ROWS:] = jnp.concatenate(high, axis=0).astype(bf16)
-    x = position[1] & 3
+    x = x_at[0]
     for d in range(4):
         outs[d][...] = packets[(x + d) & 3]
 
 
-def relay_kernel(position, own, one, two, three, *outs):
-    y = position[1] >> 2
+def relay_kernel(y_at, own, one, two, three, *outs):
+    y = y_at[0]
     for d in range(4):
         to = (y + d) & 3
         parts = [part[to] for part in (own, one, two, three)]
@@ -249,7 +249,7 @@
 
 
 def finish_kernel(
-    position, packed, got_own, got_one, got_two, got_three, slot, latents, mean, square, out_one, out_two, out_three, out_latents, out_mean, out_square, out_pred, *scratch
+    y_at, x_at, packed, got_own, got_one, got_two, got_three, slot, latents, mean, square, out_one, out_two, out_three, out_latents, out_mean, out_square, out_pred, *scratch
 ):
     grad_one, grad_two, grad_three, new_latents, new_mean, new_square, predictions, preds, sems = scratch
     copies = []
@@ -281,7 +281,7 @@
     leave(new_mean, out_mean)
     leave(new_square, out_square)
     leave(new_latents, out_latents)
-    y, x = position[1] >> 2, position[1] & 3
+    y, x = y_at[0], x_at[0]
     for back_y in range(4):
         for back_x in range(4):
             first = TEX_ROWS + 16 * back_x
@@ -363,7 +363,9 @@
         jnp.swapaxes(three, 1, 2) * 0.5,
         dir_table.T,
     )
-    position = jnp.stack([lax.axis_index("rep"), lax.axis_index("exp")]).astype(jnp.int32)
+    core = (lax.axis_index("rep") & 1).astype(jnp.int32).reshape(1)
+    at_y = (lax.axis_index("exp") >> 2).astype(jnp.int32).reshape(1)
+    at_x = (lax.axis_index("exp") & 3).astype(jnp.int32).reshape(1)
     half = lambda keep, kind: call(
         functools.partial(half_kernel, keep),
         (
@@ -376,9 +378,9 @@
         [smem] + [vmem] * 8,
         2000000000,
     )
-    grads_a, back_a, preds_a, index_a = half(False, bf16)(position, recv, *weights)
+    grads_a, back_a, preds_a, index_a = half(False, bf16)(core, recv, *weights)
     from_core = lax.ppermute(grads_a, "rep", [(i, i ^ 1) for i in range(N_REP)])
-    grads_b, back_b, preds_b, index_b = half(True, f32)(position, recv, *weights)
+    grads_b, back_b, preds_b, index_b = half(True, f32)(core, recv, *weights)
     chip = (grads_b + from_core.astype(f32)).astype(bf16)
     chips = [list(range(c, N_REP, 2)) for c in range(2)]
     parts = lax.all_to_all(chip, "rep", 0, 0, tiled=True, axis_index_groups=chips)
@@ -389,17 +391,17 @@
         texels_kernel,
         tuple([shape((4, SEND_ROWS, LANES), bf16)] * 4),
         [pltpu.VMEM((4, 4, SEND_ROWS, LANES), bf16)],
-        [smem] + [vmem] * 6,
+        [smem] * 2 + [vmem] * 6,
         2000000000,
-    )(position, back_a, back_b, preds_a, preds_b, index_a, index_b)
-    got_x = [lax.ppermute(rows_x[d], "exp", along(0, d)) for d in (1, 2, 3)]
+    )(core, at_x, back_a, back_b, preds_a, preds_b, index_a, index_b)
+    got_x = {d: lax.ppermute(rows_x[d], "exp", along(0, d)) for d in (2, 1, 3)}
     rows_y = call(
         relay_kernel,
         tuple([shape((TEX_ROWS + 64, LANES), bf16)] * 4),
         (),
         [smem] + [vmem] * 4,
-    )(position, rows_x[0], *got_x)
-    got_y = [lax.ppermute(rows_y[d], "exp", along(d, 0)) for d in (1, 2, 3)]
+    )(at_y, rows_x[0], got_x[1], got_x[2], got_x[3])
+    got_y = {d: lax.ppermute(rows_y[d], "exp", along(d, 0)) for d in (2, 1, 3)}
     own = jnp.sum(parts.astype(f32), axis=0).astype(bf16)
     packed = lax.all_gather(own, "rep", axis=0, tiled=False)
     plane = (TEX_ROWS, LANES)
@@ -409,10 +411,10 @@
         tuple(shape(dims) for dims in outs),
         [pltpu.VMEM(dims, f32) for dims in outs]
         + [pltpu.VMEM((N_EXP, 16, LANES), bf16), pltpu.SemaphoreType.DMA((10,))],
-        [smem] + [vmem] * 9,
+        [smem] * 2 + [vmem] * 9,
         0,
         tuple([hbm] * 7),
-    )(position, packed, rows_y[0], *got_y, slot, flat(latents), flat(latent_mean), flat(latent_square))
+    )(at_y, at_x, packed, rows_y[0], got_y[1], got_y[2], got_y[3], slot, flat(latents), flat(latent_mean), flat(latent_square))
     grad_three = jnp.swapaxes(grad_three, 0, 1)
     whole = lambda a: a.reshape(latents.shape)
     return (

time: 74.4 us -> 71.7 us (0.964)
  Pallas kernels: 15.2 us -> 12.5 us
  blocking collectives: 19.2 us -> 18.1 us
  waiting for transfers between devices: 12.4 us -> 13.2 us
    pallas_call x2, Pallas kernels: 8.13 us -> 7.04 us  [the longest x1 3.52 us: on_device(): grads_a, back_a, preds_a, index_a = half(False, bf16)(core, recv, *weights)]
    all_gather x1, blocking collectives: 19.2 us -> 18.1 us  [on_device(): packed = lax.all_gather(own, 'rep', axis=0, tiled=False)]
    all_to_all x1, waiting for transfers between devices: 1.84 us -> 2.91 us  [on_device(): lax.all_to_all(chip, 'rep', 0, 0, tiled=True, axis_index_groups=chips)]
  transfers between devices with their start and end apart: 9 -> 9, of which waited for: 4 -> 4; matrix products, arithmetic and copies ran while one was open for 2% -> 2% of each run, Pallas kernels for 9% -> 7%
where the time goes in v6:
time: 71.7 us; the launch traced here: 71.3 us
  starting transfers between devices  23.3 us (32%)
  blocking collectives  18.1 us (25%)
  waiting for transfers between devices  13.2 us (18%)
  Pallas kernels  12.5 us (17%)
  local copies, waits for them, and re-layouts  2.2 us (3%)
  other arithmetic  1.02 us (1%)
  between operations  1 us (1%)
    all_gather x1, blocking collectives, on_device(): packed = lax.all_gather(own, 'rep', axis=0, tiled=False)  18.1 us
    all_to_all x1, starting transfers between devices, on_device(): lax.all_to_all(chip, 'rep', 0, 0, tiled=True, axis_index_groups=chips)  8.18 us
    all_to_all x1, starting transfers between devices, on_device(): recv = lax.all_to_all(send, 'exp', 0, 0, tiled=True)  7.6 us
    all_to_all x1, waiting for transfers between devices, on_device(): recv = lax.all_to_all(send, 'exp', 0, 0, tiled=True)  6.03 us
    ppermute x3, waiting for transfers between devices, on_device(): got_x = {d: lax.ppermute(rows_x[d], 'exp', along(0, d)) for d in (2, 1, 3)}  4.19 us
    pallas_call x1, Pallas kernels, on_device(): grads_a, back_a, preds_a, index_a = half(False, bf16)(core, recv, *weights)  3.52 us
    pallas_call x1, Pallas kernels, on_device(): grads_b, back_b, preds_b, index_b = half(True, f32)(core, recv, *weights)  3.52 us
    all_to_all x1, waiting for transfers between devices, on_device(): lax.all_to_all(chip, 'rep', 0, 0, tiled=True, axis_index_groups=chips)  2.91 us
  transfers between devices with their start and end apart: 9, of which 4 were waited for; matrix products, arithmetic and copies ran while one was open for 2% of the time, Pallas kernels for 7%

profile of v6, /device:TPU:1, one launch (start us, length us, event | category | flops | bytes accessed | tf_op | source)
XLA Modules:
  0.0 71.3 jit_solution(16034597764794541232)
XLA Ops:
  0.6 2.5 %shard_map.171 = (bf16[16,80,128]{2,1,0:T(8,128)(2,1)}, s32[16,128]{1,0:T(8,128)S(1)}) custom-call(s32[16,128]{1,0:T(8,128)} %bitcast.29, s32[16,128]{1,0:T(8,128)} %bitcast.30, s32[16,128]{1,0:T(8,128)} %bitcast.31, s32[16,128]{1,0:T(8,128)} %bitcast.32, f32[3,2048]{1,0:T(4,128)} %targets_in.1, f32[64,128]{1,0:T(8,128)} %bitcast.23), custom_call_target="tpu_custom_call" | custom-call | tf_op jit(solution)/shard_map/pallas_call | solution.py:345
  3.2 7.6 %all-to-all-start = ((bf16[16,80,128]{2,1,0:T(8,128)(2,1)}), bf16[16,80,128]{2,1,0:T(8,128)(2,1)S(1)}, u32[]{:S(2)}, u32[]{:S(2)}) async-start(bf16[16,80,128]{2,1,0:T(8,128)(2,1)} %get-tuple-element.32), calls=%async_computation | async-start | bytes 655360 | tf_op jit(solution)/shard_map/all_to_all | solution.py:355
  10.8 0.2 copy.28
  11.0 0.1 fusion
  11.1 0.2 copy.30.w_two
  11.3 0.5 copy-done.6
  11.8 0.2 copy.29
  12.0 0.0 copy-start
  12.0 0.1 copy.34
  12.1 0.8 %copy-done = bf16[4,64,256]{2,1,0:T(8,128)(2,1)S(1)} copy-done((bf16[4,64,256]{2,1,0:T(8,128)(2,1)S(1)}, bf16[4,64,256]{2,1,0:T(8,128)(2,1)}, u32[]{:S(2)}) %copy-start) | copy-done | bytes 131096
  12.9 0.2 copy.26
  13.1 0.1 multiply_bitcast_fusion.w_three_t
  13.2 6.0 %all-to-all-done.recv = bf16[16,80,128]{2,1,0:T(8,128)(2,1)S(1)} async-done(((bf16[16,80,128]{2,1,0:T(8,128)(2,1)}), bf16[16,80,128]{2,1,0:T(8,128)(2,1)S(1)}, u32[]{:S(2)}, u32[]{:S(2)}) %all-to-all-start) | async-done | bytes 327712 | tf_op jit(solution)/shard_map/all_to_all | solution.py:355
  19.2 3.5 %shard_map.173 = (bf16[8,168,128]{2,1,0:T(8,128)(2,1)S(1)}, bf16[2,32,1024]{2,1,0:T(8,128)(2,1)S(1)}, f32[2,8,1024]{2,1,0:T(8,128)S(1)}, f32[2,8,1024]{2,1,0:T(8,128)S(1)}) custom-call(s32[1]{0:T(128)} %bitcast.2.core_at, bf16[16,80,128]{2,1,0:T(8,128)(2,1)S(1)} %all-to-all-done.recv, bf16[4,64,256]{2,1,0:T(8,128)(2,1)S(1)} %copy-done, ...), custom_call_target="tpu_custom_call" | custom-call | flops 2000000000 | tf_op jit(solution)/shard_map/pallas_call | solution.py:381
  22.8 1.9 %collective-permute-start = (bf16[8,168,128]{2,1,0:T(8,128)(2,1)S(1)}, bf16[8,168,128]{2,1,0:T(8,128)(2,1)S(1)}, u32[]{:S(2)}, u32[]{:S(2)}) collective-permute-start(bf16[8,168,128]{2,1,0:T(8,128)(2,1)S(1)} %get-tuple-element.34), channel_id=1, source_target_pairs={{0,16},{16,0},{32,48},{48,32},{64,80},{80,64},{96,112},{112,96},{1... | collective-permute-start | bytes 1032200 | tf_op jit(solution)/shard_map/ppermute | solution.py:382
  24.7 3.5 %shard_map.172 = (f32[8,168,128]{2,1,0:T(8,128)S(1)}, bf16[2,32,1024]{2,1,0:T(8,128)(2,1)S(1)}, f32[2,8,1024]{2,1,0:T(8,128)S(1)}, f32[2,8,1024]{2,1,0:T(8,128)S(1)}) custom-call(s32[1]{0:T(128)} %bitcast.2.core_at, bf16[16,80,128]{2,1,0:T(8,128)(2,1)S(1)} %all-to-all-done.recv, bf16[4,64,256]{2,1,0:T(8,128)(2,1)S(1)} %copy-done, ...), custom_call_target="tpu_custom_call" | custom-call | flops 2000000000 | tf_op jit(solution)/shard_map/pallas_call | solution.py:383
  28.2 0.0 collective-permute-done
  28.2 0.8 %add_convert_fusion = bf16[8,168,128]{2,1,0:T(8,128)(2,1)} fusion(f32[8,168,128]{2,1,0:T(8,128)S(1)} %get-tuple-element.33, bf16[8,168,128]{2,1,0:T(8,128)(2,1)S(1)} %collective-permute-done), kind=kLoop, calls=%fused_computation | loop fusion | flops 516096 | bytes 1376256 | tf_op jit(solution)/shard_map/convert_element_type | solution.py:384
  29.0 8.2 %all-to-all-start.1 = ((bf16[8,168,128]{2,1,0:T(8,128)(2,1)}), bf16[8,168,128]{2,1,0:T(8,128)(2,1)S(1)}, u32[]{:S(2)}, u32[]{:S(2)}) async-start(bf16[8,168,128]{2,1,0:T(8,128)(2,1)} %add_convert_fusion), calls=%async_computation.1 | async-start | bytes 688128 | tf_op jit(solution)/shard_map/all_to_all | solution.py:386
  37.2 1.4 %shard_map.174 = (bf16[4,80,128]{2,1,0:T(8,128)(2,1)S(1)}, bf16[4,80,128]{2,1,0:T(8,128)(2,1)S(1)}, bf16[4,80,128]{2,1,0:T(8,128)(2,1)S(1)}, bf16[4,80,128]{2,1,0:T(8,128)(2,1)S(1)}) custom-call(s32[1]{0:T(128)} %bitcast.2.core_at, s32[1]{0:T(128)} %bitcast.1.x_at, bf16[2,32,1024]{2,1,0:T(8,128)(2,1)S(1)} %get-tuple-element.35.back_a, ...), custom_call_target="tpu_custom_call" | custom-call | flops 2000000000 | tf_op jit(solution)/shard_map/pallas_call | solution.py:390
  38.6 0.4 collective-permute-start.1
  39.0 1.2 %collective-permute-start.2 = (bf16[4,80,128]{2,1,0:T(8,128)(2,1)S(1)}, bf16[4,80,128]{2,1,0:T(8,128)(2,1)S(1)}, u32[]{:S(2)}, u32[]{:S(2)}) collective-permute-start(bf16[4,80,128]{2,1,0:T(8,128)(2,1)S(1)} %get-tuple-element.43), channel_id=1, source_target_pairs={{0,2},{1,3},{2,0},{3,1},{4,6},{5,7},{6,4},{7,5},{8,10},{9,11},{10,... | collective-permute-start | bytes 245768 | tf_op jit(solution)/shard_map/ppermute | solution.py:397
  40.2 1.3 %collective-permute-start.3 = (bf16[4,80,128]{2,1,0:T(8,128)(2,1)S(1)}, bf16[4,80,128]{2,1,0:T(8,128)(2,1)S(1)}, u32[]{:S(2)}, u32[]{:S(2)}) collective-permute-start(bf16[4,80,128]{2,1,0:T(8,128)(2,1)S(1)} %get-tuple-element.44), channel_id=1, source_target_pairs={{0,3},{1,0},{2,1},{3,2},{4,7},{5,4},{6,5},{7,6},{8,11},{9,8},{10,9... | collective-permute-start | bytes 245768 | tf_op jit(solution)/shard_map/ppermute | solution.py:397
  41.4 4.0 %collective-permute-done.1.one = bf16[4,80,128]{2,1,0:T(8,128)(2,1)S(1)} collective-permute-done((bf16[4,80,128]{2,1,0:T(8,128)(2,1)S(1)}, bf16[4,80,128]{2,1,0:T(8,128)(2,1)S(1)}, u32[]{:S(2)}, u32[]{:S(2)}) %collective-permute-start.1) | collective-permute-done | bytes 81952 | tf_op jit(solution)/shard_map/ppermute | solution.py:397
  45.5 0.2 collective-permute-done.3.three
  45.7 0.1 collective-permute-start.4
  45.8 1.8 %collective-permute-start.5 = (bf16[128,128]{1,0:T(8,128)(2,1)S(1)}, bf16[128,128]{1,0:T(8,128)(2,1)S(1)}, u32[]{:S(2)}, u32[]{:S(2)}) collective-permute-start(bf16[128,128]{1,0:T(8,128)(2,1)S(1)} %get-tuple-element.47), channel_id=1, source_target_pairs={{0,8},{1,9},{2,10},{3,11},{4,12},{5,13},{6,14},{7,15},{8,0},{9,1},... | collective-permute-start | bytes 98312 | tf_op jit(solution)/shard_map/ppermute | solution.py:404
  47.5 0.9 %collective-permute-start.6 = (bf16[128,128]{1,0:T(8,128)(2,1)S(1)}, bf16[128,128]{1,0:T(8,128)(2,1)S(1)}, u32[]{:S(2)}, u32[]{:S(2)}) collective-permute-start(bf16[128,128]{1,0:T(8,128)(2,1)S(1)} %get-tuple-element.48), channel_id=1, source_target_pairs={{0,12},{1,13},{2,14},{3,15},{4,0},{5,1},{6,2},{7,3},{8,4},{9,5},{1... | collective-permute-start | bytes 98312 | tf_op jit(solution)/shard_map/ppermute | solution.py:404
  48.4 2.9 %all-to-all-done.1 = bf16[8,168,128]{2,1,0:T(8,128)(2,1)S(1)} async-done(((bf16[8,168,128]{2,1,0:T(8,128)(2,1)}), bf16[8,168,128]{2,1,0:T(8,128)(2,1)S(1)}, u32[]{:S(2)}, u32[]{:S(2)}) %all-to-all-start.1) | async-done | bytes 344096 | tf_op jit(solution)/shard_map/all_to_all | solution.py:386
  51.4 0.1 reduce_sum.12
  51.4 18.1 %all-gather = bf16[2688,128]{1,0:T(8,128)(2,1)S(1)} all-gather(bf16[168,128]{1,0:T(8,128)(2,1)S(1)} %reduce_sum.12), channel_id=2, replica_groups=mesh['rep'=16,'exp'=16] {'rep'}, dimensions={0}, use_global_device_ids=true | all-gather | bytes 731136 | tf_op jit(solution)/shard_map/all_gather | solution.py:406
  69.6 1.5 %shard_map.176 = (f32[4,64,256]{2,1,0:T(8,128)}, f32[4,256,256]{2,1,0:T(8,128)}, f32[3,4,256]{2,1,0:T(4,128)}, f32[64,128]{1,0:T(8,128)}, f32[64,128]{1,0:T(8,12...) custom-call(s32[1]{0:T(128)} %bitcast.y_at, s32[1]{0:T(128)} %bitcast.1.x_at, bf16[16,168,128]{2,1,0:T(8,128)(2,1)S(1)} %bitcast.22, ...), custom_call_target="tpu_custom_call" | custom-call | tf_op jit(solution)/shard_map/pallas_call | solution.py:409
  (18 shorter events, 0.1 us)
Async XLA Ops:
  0.6 10.1 %copy-start.5 = (bf16[4,256,256]{2,1,0:T(8,128)(2,1)S(1)}, bf16[4,256,256]{2,1,0:T(8,128)(2,1)}, u32[]{:S(2)}) copy-start(bf16[4,256,256]{2,1,0:T(8,128)(2,1)} %param.16) | copy-start | bytes 1572868
  3.2 16.1 %all-to-all-start = ((bf16[16,80,128]{2,1,0:T(8,128)(2,1)}), bf16[16,80,128]{2,1,0:T(8,128)(2,1)S(1)}, u32[]{:S(2)}, u32[]{:S(2)}) async-start(bf16[16,80,128]{2,1,0:T(8,128)(2,1)} %get-tuple-element.32), calls=%async_computation | async-start | bytes 655360 | tf_op jit(solution)/shard_map/all_to_all | solution.py:355
  11.1 0.7 copy-start.6
  12.0 0.9 %copy-start = (bf16[4,64,256]{2,1,0:T(8,128)(2,1)S(1)}, bf16[4,64,256]{2,1,0:T(8,128)(2,1)}, u32[]{:S(2)}) copy-start(bf16[4,64,256]{2,1,0:T(8,128)(2,1)} %w_one.3) | copy-start | bytes 393220
  13.2 6.1 %copy-start.4 = (bf16[256,32]{0,1:T(8,128)(2,1)S(1)}, bf16[256,32]{0,1:T(8,128)(2,1)}, u32[]{:S(2)}) copy-start(bf16[256,32]{0,1:T(8,128)(2,1)} %param.18) | copy-start | bytes 49156
  22.8 5.5 %collective-permute-start = (bf16[8,168,128]{2,1,0:T(8,128)(2,1)S(1)}, bf16[8,168,128]{2,1,0:T(8,128)(2,1)S(1)}, u32[]{:S(2)}, u32[]{:S(2)}) collective-permute-start(bf16[8,168,128]{2,1,0:T(8,128)(2,1)S(1)} %get-tuple-element.34), channel_id=1, source_target_pairs={{0,16},{16,0},{32,48},{48,32},{64,80},{80,64},{96,112},{112,96},{1... | collective-permute-start | bytes 1032200 | tf_op jit(solution)/shard_map/ppermute | solution.py:382
  29.0 22.3 %all-to-all-start.1 = ((bf16[8,168,128]{2,1,0:T(8,128)(2,1)}), bf16[8,168,128]{2,1,0:T(8,128)(2,1)S(1)}, u32[]{:S(2)}, u32[]{:S(2)}) async-start(bf16[8,168,128]{2,1,0:T(8,128)(2,1)} %add_convert_fusion), calls=%async_computation.1 | async-start | bytes 688128 | tf_op jit(solution)/shard_map/all_to_all | solution.py:386
  38.6 6.9 %collective-permute-start.1 = (bf16[4,80,128]{2,1,0:T(8,128)(2,1)S(1)}, bf16[4,80,128]{2,1,0:T(8,128)(2,1)S(1)}, u32[]{:S(2)}, u32[]{:S(2)}) collective-permute-start(bf16[4,80,128]{2,1,0:T(8,128)(2,1)S(1)} %get-tuple-element.42), channel_id=1, source_target_pairs={{0,1},{1,2},{2,3},{3,0},{4,5},{5,6},{6,7},{7,4},{8,9},{9,10},{10,1... | collective-permute-start | bytes 245768 | tf_op jit(solution)/shard_map/ppermute | solution.py:397
  39.0 6.5 %collective-permute-start.2 = (bf16[4,80,128]{2,1,0:T(8,128)(2,1)S(1)}, bf16[4,80,128]{2,1,0:T(8,128)(2,1)S(1)}, u32[]{:S(2)}, u32[]{:S(2)}) collective-permute-start(bf16[4,80,128]{2,1,0:T(8,128)(2,1)S(1)} %get-tuple-element.43), channel_id=1, source_target_pairs={{0,2},{1,3},{2,0},{3,1},{4,6},{5,7},{6,4},{7,5},{8,10},{9,11},{10,... | collective-permute-start | bytes 245768 | tf_op jit(solution)/shard_map/ppermute | solution.py:397
  40.2 5.5 %collective-permute-start.3 = (bf16[4,80,128]{2,1,0:T(8,128)(2,1)S(1)}, bf16[4,80,128]{2,1,0:T(8,128)(2,1)S(1)}, u32[]{:S(2)}, u32[]{:S(2)}) collective-permute-start(bf16[4,80,128]{2,1,0:T(8,128)(2,1)S(1)} %get-tuple-element.44), channel_id=1, source_target_pairs={{0,3},{1,0},{2,1},{3,2},{4,7},{5,4},{6,5},{7,6},{8,11},{9,8},{10,9... | collective-permute-start | bytes 245768 | tf_op jit(solution)/shard_map/ppermute | solution.py:397
  45.7 23.9 %collective-permute-start.4 = (bf16[128,128]{1,0:T(8,128)(2,1)S(1)}, bf16[128,128]{1,0:T(8,128)(2,1)S(1)}, u32[]{:S(2)}, u32[]{:S(2)}) collective-permute-start(bf16[128,128]{1,0:T(8,128)(2,1)S(1)} %get-tuple-element.46), channel_id=1, source_target_pairs={{0,4},{1,5},{2,6},{3,7},{4,8},{5,9},{6,10},{7,11},{8,12},{9,13},{1... | collective-permute-start | bytes 98312 | tf_op jit(solution)/shard_map/ppermute | solution.py:404
  45.8 23.8 %collective-permute-start.5 = (bf16[128,128]{1,0:T(8,128)(2,1)S(1)}, bf16[128,128]{1,0:T(8,128)(2,1)S(1)}, u32[]{:S(2)}, u32[]{:S(2)}) collective-permute-start(bf16[128,128]{1,0:T(8,128)(2,1)S(1)} %get-tuple-element.47), channel_id=1, source_target_pairs={{0,8},{1,9},{2,10},{3,11},{4,12},{5,13},{6,14},{7,15},{8,0},{9,1},... | collective-permute-start | bytes 98312 | tf_op jit(solution)/shard_map/ppermute | solution.py:404
  47.5 22.1 %collective-permute-start.6 = (bf16[128,128]{1,0:T(8,128)(2,1)S(1)}, bf16[128,128]{1,0:T(8,128)(2,1)S(1)}, u32[]{:S(2)}, u32[]{:S(2)}) collective-permute-start(bf16[128,128]{1,0:T(8,128)(2,1)S(1)} %get-tuple-element.48), channel_id=1, source_target_pairs={{0,12},{1,13},{2,14},{3,15},{4,0},{5,1},{6,2},{7,3},{8,4},{9,5},{1... | collective-permute-start | bytes 98312 | tf_op jit(solution)/shard_map/ppermute | solution.py:404
  51.4 18.2 %copy-start.1 = (f32[2,32,128]{2,1,0:T(8,128)S(1)}, f32[2,32,128]{2,1,0:T(8,128)}, u32[]{:S(2)}) copy-start(f32[2,32,128]{2,1,0:T(8,128)} %param.12) | copy-start | bytes 98308
  51.4 18.2 %copy-start.2 = (f32[2,32,128]{2,1,0:T(8,128)S(1)}, f32[2,32,128]{2,1,0:T(8,128)}, u32[]{:S(2)}) copy-start(f32[2,32,128]{2,1,0:T(8,128)} %param.13) | copy-start | bytes 98308
  51.4 18.2 %copy-start.3 = (f32[2,32,128]{2,1,0:T(8,128)S(1)}, f32[2,32,128]{2,1,0:T(8,128)}, u32[]{:S(2)}) copy-start(f32[2,32,128]{2,1,0:T(8,128)} %param.14) | copy-start | bytes 98308

commit v7 on v6

--- a/solution.py
+++ b/solution.py
@@ -23,6 +23,8 @@
 TEX_ROWS = 64
 SEND_ROWS = TEX_ROWS + 16
 GRAD_ROWS = 168
+BACK_ROWS = TEX_ROWS + 8
+RELAY_ROWS = TEX_ROWS + 4 * 8
 
 decay_one = 0.9
 decay_two = 0.99
@@ -231,8 +233,8 @@
             two = jnp.where(keep == h, preds_b[1, :, cols], preds_a[1, :, cols])
             low.append(jnp.where(left, one, pltpu.roll(two, CAP, 1)))
             high.append(jnp.where(left, pltpu.roll(one, CAP, 1), two))
-        packets[2 * j % 4, j // 2, TEX_ROWS:] = jnp.concatenate(low, axis=0).astype(bf16)
-        packets[2 * j % 4 + 1, j // 2, TEX_ROWS:] = jnp.concatenate(high, axis=0).astype(bf16)
+        packets[2 * j % 4, j // 2, TEX_ROWS:] = (low[0] + pltpu.roll(low[1], 4, 0)).astype(bf16)
+        packets[2 * j % 4 + 1, j // 2, TEX_ROWS:] = (high[0] + pltpu.roll(high[1], 4, 0)).astype(bf16)
     x = x_at[0]
     for d in range(4):
         outs[d][...] = packets[(x + d) & 3]
@@ -245,7 +247,7 @@
         parts = [part[to] for part in (own, one, two, three)]
         outs[d][:TEX_ROWS] = sum(part[:TEX_ROWS].astype(f32) for part in parts).astype(bf16)
         for n in range(4):
-            outs[d][TEX_ROWS + 16 * n : TEX_ROWS + 16 * (n + 1)] = parts[n][TEX_ROWS:]
+            outs[d][TEX_ROWS + 8 * n : TEX_ROWS + 8 * (n + 1)] = parts[n][TEX_ROWS:]
 
 
 def finish_kernel(
@@ -284,20 +286,20 @@
     y, x = y_at[0], x_at[0]
     for back_y in range(4):
         for back_x in range(4):
-            first = TEX_ROWS + 16 * back_x
-            preds[((y - back_y) & 3) * 4 + ((x - back_x) & 3)] = gots[back_y][first : first + 16]
-    table = preds[...].reshape(N_EXP * 16, LANES)
+            first = TEX_ROWS + 8 * back_x
+            preds[((y - back_y) & 3) * 4 + ((x - back_x) & 3)] = gots[back_y][first : first + 8].astype(f32)
+    table = preds[...].reshape(N_EXP * 8, LANES).astype(bf16)
     place = slot[...]
     lane = place & (LANES - 1)
     pair = place >> 7
     for i in range(CHUNKS):
         row = slice(i, i + 1)
         picked = dot(table, hot(lane[row], LANES))
-        wide = jnp.broadcast_to(pair[row], (8, LANES))
-        total = jnp.where(wide == 0, picked[:8], 0.0)
-        for g in range(1, 32):
-            total = jnp.where(wide == g, picked[g * 8 : (g + 1) * 8], total)
-        predictions[:, i * LANES : (i + 1) * LANES] = total[:OUTC]
+        owner = jnp.broadcast_to(pair[row] >> 1, (8, LANES))
+        total = jnp.where(owner == 0, picked[:8], 0.0)
+        for j in range(1, N_EXP):
+            total = jnp.where(owner == j, picked[j * 8 : (j + 1) * 8], total)
+        predictions[:, i * LANES : (i + 1) * LANES] = jnp.where((pair[row] & 1) == 0, total, pltpu.roll(total, 4, 0))[:OUTC]
     leave(predictions, out_pred)
     for copy in copies:
         copy.wait()
@@ -389,15 +391,15 @@
     ]
     rows_x = call(
         texels_kernel,
-        tuple([shape((4, SEND_ROWS, LANES), bf16)] * 4),
-        [pltpu.VMEM((4, 4, SEND_ROWS, LANES), bf16)],
+        tuple([shape((4, BACK_ROWS, LANES), bf16)] * 4),
+        [pltpu.VMEM((4, 4, BACK_ROWS, LANES), bf16)],
         [smem] * 2 + [vmem] * 6,
         2000000000,
     )(core, at_x, back_a, back_b, preds_a, preds_b, index_a, index_b)
     got_x = {d: lax.ppermute(rows_x[d], "exp", along(0, d)) for d in (2, 1, 3)}
     rows_y = call(
         relay_kernel,
-        tuple([shape((TEX_ROWS + 64, LANES), bf16)] * 4),
+        tuple([shape((RELAY_ROWS, LANES), bf16)] * 4),
         (),
         [smem] + [vmem] * 4,
     )(at_y, rows_x[0], got_x[1], got_x[2], got_x[3])
@@ -410,7 +412,7 @@
         finish_kernel,
         tuple(shape(dims) for dims in outs),
         [pltpu.VMEM(dims, f32) for dims in outs]
-        + [pltpu.VMEM((N_EXP, 16, LANES), bf16), pltpu.SemaphoreType.DMA((10,))],
+        + [pltpu.VMEM((N_EXP, 8, LANES), f32), pltpu.SemaphoreType.DMA((10,))],
         [smem] * 2 + [vmem] * 9,
         0,
         tuple([hbm] * 7),

time: 71.7 us -> 71.2 us (level)
  no operation moved by 1% of the time
where the time goes in v7:
time: 71.2 us; the launch traced here: 70.8 us
  starting transfers between devices  23.3 us (33%)
  blocking collectives  17.8 us (25%)
  waiting for transfers between devices  13.2 us (19%)
  Pallas kernels  12.4 us (17%)
  local copies, waits for them, and re-layouts  2.2 us (3%)
  other arithmetic  1.02 us (1%)
  between operations  1 us (1%)
    all_gather x1, blocking collectives, on_device(): packed = lax.all_gather(own, 'rep', axis=0, tiled=False)  17.8 us
    all_to_all x1, starting transfers between devices, on_device(): lax.all_to_all(chip, 'rep', 0, 0, tiled=True, axis_index_groups=chips)  8.18 us
    all_to_all x1, starting transfers between devices, on_device(): recv = lax.all_to_all(send, 'exp', 0, 0, tiled=True)  7.6 us
    all_to_all x1, waiting for transfers between devices, on_device(): recv = lax.all_to_all(send, 'exp', 0, 0, tiled=True)  6.03 us
    ppermute x3, waiting for transfers between devices, on_device(): got_x = {d: lax.ppermute(rows_x[d], 'exp', along(0, d)) for d in (2, 1, 3)}  3.84 us
    pallas_call x1, Pallas kernels, on_device(): grads_a, back_a, preds_a, index_a = half(False, bf16)(core, recv, *weights)  3.52 us
    pallas_call x1, Pallas kernels, on_device(): grads_b, back_b, preds_b, index_b = half(True, f32)(core, recv, *weights)  3.52 us
    all_to_all x1, waiting for transfers between devices, on_device(): lax.all_to_all(chip, 'rep', 0, 0, tiled=True, axis_index_groups=chips)  3.27 us
  transfers between devices with their start and end apart: 9, of which 4 were waited for; matrix products, arithmetic and copies ran while one was open for 2% of the time, Pallas kernels for 7%

profile of v7, /device:TPU:1, one launch (start us, length us, event | category | flops | bytes accessed | tf_op | source)
XLA Modules:
  0.0 70.8 jit_solution(13225162236542312257)
XLA Ops:
  0.6 2.5 %shard_map.171 = (bf16[16,80,128]{2,1,0:T(8,128)(2,1)}, s32[16,128]{1,0:T(8,128)S(1)}) custom-call(s32[16,128]{1,0:T(8,128)} %bitcast.29, s32[16,128]{1,0:T(8,128)} %bitcast.30, s32[16,128]{1,0:T(8,128)} %bitcast.31, s32[16,128]{1,0:T(8,128)} %bitcast.32, f32[3,2048]{1,0:T(4,128)} %targets_in.1, f32[64,128]{1,0:T(8,128)} %bitcast.23), custom_call_target="tpu_custom_call" | custom-call | tf_op jit(solution)/shard_map/pallas_call | solution.py:347
  3.2 7.6 %all-to-all-start = ((bf16[16,80,128]{2,1,0:T(8,128)(2,1)}), bf16[16,80,128]{2,1,0:T(8,128)(2,1)S(1)}, u32[]{:S(2)}, u32[]{:S(2)}) async-start(bf16[16,80,128]{2,1,0:T(8,128)(2,1)} %get-tuple-element.32), calls=%async_computation | async-start | bytes 655360 | tf_op jit(solution)/shard_map/all_to_all | solution.py:357
  10.8 0.2 copy.28
  11.0 0.1 fusion
  11.1 0.2 copy.30.w_two
  11.3 0.5 copy-done.6
  11.8 0.2 copy.29
  12.0 0.0 copy-start
  12.0 0.1 copy.34
  12.1 0.8 %copy-done = bf16[4,64,256]{2,1,0:T(8,128)(2,1)S(1)} copy-done((bf16[4,64,256]{2,1,0:T(8,128)(2,1)S(1)}, bf16[4,64,256]{2,1,0:T(8,128)(2,1)}, u32[]{:S(2)}) %copy-start) | copy-done | bytes 131096
  12.9 0.2 copy.26
  13.1 0.1 multiply_bitcast_fusion.w_three_t
  13.2 6.0 %all-to-all-done.recv = bf16[16,80,128]{2,1,0:T(8,128)(2,1)S(1)} async-done(((bf16[16,80,128]{2,1,0:T(8,128)(2,1)}), bf16[16,80,128]{2,1,0:T(8,128)(2,1)S(1)}, u32[]{:S(2)}, u32[]{:S(2)}) %all-to-all-start) | async-done | bytes 327712 | tf_op jit(solution)/shard_map/all_to_all | solution.py:357
  19.2 3.5 %shard_map.173 = (bf16[8,168,128]{2,1,0:T(8,128)(2,1)S(1)}, bf16[2,32,1024]{2,1,0:T(8,128)(2,1)S(1)}, f32[2,8,1024]{2,1,0:T(8,128)S(1)}, f32[2,8,1024]{2,1,0:T(8,128)S(1)}) custom-call(s32[1]{0:T(128)} %bitcast.2.core_at, bf16[16,80,128]{2,1,0:T(8,128)(2,1)S(1)} %all-to-all-done.recv, bf16[4,64,256]{2,1,0:T(8,128)(2,1)S(1)} %copy-done, ...), custom_call_target="tpu_custom_call" | custom-call | flops 2000000000 | tf_op jit(solution)/shard_map/pallas_call | solution.py:383
  22.8 1.9 %collective-permute-start = (bf16[8,168,128]{2,1,0:T(8,128)(2,1)S(1)}, bf16[8,168,128]{2,1,0:T(8,128)(2,1)S(1)}, u32[]{:S(2)}, u32[]{:S(2)}) collective-permute-start(bf16[8,168,128]{2,1,0:T(8,128)(2,1)S(1)} %get-tuple-element.34), channel_id=1, source_target_pairs={{0,16},{16,0},{32,48},{48,32},{64,80},{80,64},{96,112},{112,96},{1... | collective-permute-start | bytes 1032200 | tf_op jit(solution)/shard_map/ppermute | solution.py:384
  24.7 3.5 %shard_map.172 = (f32[8,168,128]{2,1,0:T(8,128)S(1)}, bf16[2,32,1024]{2,1,0:T(8,128)(2,1)S(1)}, f32[2,8,1024]{2,1,0:T(8,128)S(1)}, f32[2,8,1024]{2,1,0:T(8,128)S(1)}) custom-call(s32[1]{0:T(128)} %bitcast.2.core_at, bf16[16,80,128]{2,1,0:T(8,128)(2,1)S(1)} %all-to-all-done.recv, bf16[4,64,256]{2,1,0:T(8,128)(2,1)S(1)} %copy-done, ...), custom_call_target="tpu_custom_call" | custom-call | flops 2000000000 | tf_op jit(solution)/shard_map/pallas_call | solution.py:385
  28.2 0.0 collective-permute-done
  28.2 0.8 %add_convert_fusion = bf16[8,168,128]{2,1,0:T(8,128)(2,1)} fusion(f32[8,168,128]{2,1,0:T(8,128)S(1)} %get-tuple-element.33, bf16[8,168,128]{2,1,0:T(8,128)(2,1)S(1)} %collective-permute-done), kind=kLoop, calls=%fused_computation | loop fusion | flops 516096 | bytes 1376256 | tf_op jit(solution)/shard_map/convert_element_type | solution.py:386
  29.0 8.2 %all-to-all-start.1 = ((bf16[8,168,128]{2,1,0:T(8,128)(2,1)}), bf16[8,168,128]{2,1,0:T(8,128)(2,1)S(1)}, u32[]{:S(2)}, u32[]{:S(2)}) async-start(bf16[8,168,128]{2,1,0:T(8,128)(2,1)} %add_convert_fusion), calls=%async_computation.1 | async-start | bytes 688128 | tf_op jit(solution)/shard_map/all_to_all | solution.py:388
  37.2 1.3 %shard_map.174 = (bf16[4,72,128]{2,1,0:T(8,128)(2,1)S(1)}, bf16[4,72,128]{2,1,0:T(8,128)(2,1)S(1)}, bf16[4,72,128]{2,1,0:T(8,128)(2,1)S(1)}, bf16[4,72,128]{2,1,0:T(8,128)(2,1)S(1)}) custom-call(s32[1]{0:T(128)} %bitcast.2.core_at, s32[1]{0:T(128)} %bitcast.1.x_at, bf16[2,32,1024]{2,1,0:T(8,128)(2,1)S(1)} %get-tuple-element.35.back_a, ...), custom_call_target="tpu_custom_call" | custom-call | flops 2000000000 | tf_op jit(solution)/shard_map/pallas_call | solution.py:392
  38.6 0.4 collective-permute-start.1
  38.9 1.2 %collective-permute-start.2 = (bf16[4,72,128]{2,1,0:T(8,128)(2,1)S(1)}, bf16[4,72,128]{2,1,0:T(8,128)(2,1)S(1)}, u32[]{:S(2)}, u32[]{:S(2)}) collective-permute-start(bf16[4,72,128]{2,1,0:T(8,128)(2,1)S(1)} %get-tuple-element.43), channel_id=1, source_target_pairs={{0,2},{1,3},{2,0},{3,1},{4,6},{5,7},{6,4},{7,5},{8,10},{9,11},{10,... | collective-permute-start | bytes 221192 | tf_op jit(solution)/shard_map/ppermute | solution.py:399
  40.2 1.3 %collective-permute-start.3 = (bf16[4,72,128]{2,1,0:T(8,128)(2,1)S(1)}, bf16[4,72,128]{2,1,0:T(8,128)(2,1)S(1)}, u32[]{:S(2)}, u32[]{:S(2)}) collective-permute-start(bf16[4,72,128]{2,1,0:T(8,128)(2,1)S(1)} %get-tuple-element.44), channel_id=1, source_target_pairs={{0,3},{1,0},{2,1},{3,2},{4,7},{5,4},{6,5},{7,6},{8,11},{9,8},{10,9... | collective-permute-start | bytes 221192 | tf_op jit(solution)/shard_map/ppermute | solution.py:399
  41.4 3.6 %collective-permute-done.1.one = bf16[4,72,128]{2,1,0:T(8,128)(2,1)S(1)} collective-permute-done((bf16[4,72,128]{2,1,0:T(8,128)(2,1)S(1)}, bf16[4,72,128]{2,1,0:T(8,128)(2,1)S(1)}, u32[]{:S(2)}, u32[]{:S(2)}) %collective-permute-start.1) | collective-permute-done | bytes 73760 | tf_op jit(solution)/shard_map/ppermute | solution.py:399
  45.1 0.2 collective-permute-done.3.three
  45.3 0.1 collective-permute-start.4
  45.4 1.7 %collective-permute-start.5 = (bf16[96,128]{1,0:T(8,128)(2,1)S(1)}, bf16[96,128]{1,0:T(8,128)(2,1)S(1)}, u32[]{:S(2)}, u32[]{:S(2)}) collective-permute-start(bf16[96,128]{1,0:T(8,128)(2,1)S(1)} %get-tuple-element.47), channel_id=1, source_target_pairs={{0,8},{1,9},{2,10},{3,11},{4,12},{5,13},{6,14},{7,15},{8,0},{9,1},... | collective-permute-start | bytes 73736 | tf_op jit(solution)/shard_map/ppermute | solution.py:406
  47.2 0.9 %collective-permute-start.6 = (bf16[96,128]{1,0:T(8,128)(2,1)S(1)}, bf16[96,128]{1,0:T(8,128)(2,1)S(1)}, u32[]{:S(2)}, u32[]{:S(2)}) collective-permute-start(bf16[96,128]{1,0:T(8,128)(2,1)S(1)} %get-tuple-element.48), channel_id=1, source_target_pairs={{0,12},{1,13},{2,14},{3,15},{4,0},{5,1},{6,2},{7,3},{8,4},{9,5},{1... | collective-permute-start | bytes 73736 | tf_op jit(solution)/shard_map/ppermute | solution.py:406
  48.1 3.3 %all-to-all-done.1 = bf16[8,168,128]{2,1,0:T(8,128)(2,1)S(1)} async-done(((bf16[8,168,128]{2,1,0:T(8,128)(2,1)}), bf16[8,168,128]{2,1,0:T(8,128)(2,1)S(1)}, u32[]{:S(2)}, u32[]{:S(2)}) %all-to-all-start.1) | async-done | bytes 344096 | tf_op jit(solution)/shard_map/all_to_all | solution.py:388
  51.4 0.1 reduce_sum.12
  51.4 17.8 %all-gather = bf16[2688,128]{1,0:T(8,128)(2,1)S(1)} all-gather(bf16[168,128]{1,0:T(8,128)(2,1)S(1)} %reduce_sum.12), channel_id=2, replica_groups=mesh['rep'=16,'exp'=16] {'rep'}, dimensions={0}, use_global_device_ids=true | all-gather | bytes 731136 | tf_op jit(solution)/shard_map/all_gather | solution.py:408
  69.3 1.4 %shard_map.176 = (f32[4,64,256]{2,1,0:T(8,128)}, f32[4,256,256]{2,1,0:T(8,128)}, f32[3,4,256]{2,1,0:T(4,128)}, f32[64,128]{1,0:T(8,128)}, f32[64,128]{1,0:T(8,12...) custom-call(s32[1]{0:T(128)} %bitcast.y_at, s32[1]{0:T(128)} %bitcast.1.x_at, bf16[16,168,128]{2,1,0:T(8,128)(2,1)S(1)} %bitcast.22, ...), custom_call_target="tpu_custom_call" | custom-call | tf_op jit(solution)/shard_map/pallas_call | solution.py:411
  (18 shorter events, 0.1 us)
Async XLA Ops:
  0.6 10.1 %copy-start.5 = (bf16[4,256,256]{2,1,0:T(8,128)(2,1)S(1)}, bf16[4,256,256]{2,1,0:T(8,128)(2,1)}, u32[]{:S(2)}) copy-start(bf16[4,256,256]{2,1,0:T(8,128)(2,1)} %param.16) | copy-start | bytes 1572868
  3.2 16.1 %all-to-all-start = ((bf16[16,80,128]{2,1,0:T(8,128)(2,1)}), bf16[16,80,128]{2,1,0:T(8,128)(2,1)S(1)}, u32[]{:S(2)}, u32[]{:S(2)}) async-start(bf16[16,80,128]{2,1,0:T(8,128)(2,1)} %get-tuple-element.32), calls=%async_computation | async-start | bytes 655360 | tf_op jit(solution)/shard_map/all_to_all | solution.py:357
  11.1 0.7 copy-start.6
  12.0 0.9 %copy-start = (bf16[4,64,256]{2,1,0:T(8,128)(2,1)S(1)}, bf16[4,64,256]{2,1,0:T(8,128)(2,1)}, u32[]{:S(2)}) copy-start(bf16[4,64,256]{2,1,0:T(8,128)(2,1)} %w_one.3) | copy-start | bytes 393220
  13.2 6.1 %copy-start.4 = (bf16[256,32]{0,1:T(8,128)(2,1)S(1)}, bf16[256,32]{0,1:T(8,128)(2,1)}, u32[]{:S(2)}) copy-start(bf16[256,32]{0,1:T(8,128)(2,1)} %param.18) | copy-start | bytes 49156
  22.8 5.5 %collective-permute-start = (bf16[8,168,128]{2,1,0:T(8,128)(2,1)S(1)}, bf16[8,168,128]{2,1,0:T(8,128)(2,1)S(1)}, u32[]{:S(2)}, u32[]{:S(2)}) collective-permute-start(bf16[8,168,128]{2,1,0:T(8,128)(2,1)S(1)} %get-tuple-element.34), channel_id=1, source_target_pairs={{0,16},{16,0},{32,48},{48,32},{64,80},{80,64},{96,112},{112,96},{1... | collective-permute-start | bytes 1032200 | tf_op jit(solution)/shard_map/ppermute | solution.py:384
  29.0 22.3 %all-to-all-start.1 = ((bf16[8,168,128]{2,1,0:T(8,128)(2,1)}), bf16[8,168,128]{2,1,0:T(8,128)(2,1)S(1)}, u32[]{:S(2)}, u32[]{:S(2)}) async-start(bf16[8,168,128]{2,1,0:T(8,128)(2,1)} %add_convert_fusion), calls=%async_computation.1 | async-start | bytes 688128 | tf_op jit(solution)/shard_map/all_to_all | solution.py:388
  38.6 6.5 %collective-permute-start.1 = (bf16[4,72,128]{2,1,0:T(8,128)(2,1)S(1)}, bf16[4,72,128]{2,1,0:T(8,128)(2,1)S(1)}, u32[]{:S(2)}, u32[]{:S(2)}) collective-permute-start(bf16[4,72,128]{2,1,0:T(8,128)(2,1)S(1)} %get-tuple-element.42), channel_id=1, source_target_pairs={{0,1},{1,2},{2,3},{3,0},{4,5},{5,6},{6,7},{7,4},{8,9},{9,10},{10,1... | collective-permute-start | bytes 221192 | tf_op jit(solution)/shard_map/ppermute | solution.py:399
  38.9 6.1 %collective-permute-start.2 = (bf16[4,72,128]{2,1,0:T(8,128)(2,1)S(1)}, bf16[4,72,128]{2,1,0:T(8,128)(2,1)S(1)}, u32[]{:S(2)}, u32[]{:S(2)}) collective-permute-start(bf16[4,72,128]{2,1,0:T(8,128)(2,1)S(1)} %get-tuple-element.43), channel_id=1, source_target_pairs={{0,2},{1,3},{2,0},{3,1},{4,6},{5,7},{6,4},{7,5},{8,10},{9,11},{10,... | collective-permute-start | bytes 221192 | tf_op jit(solution)/shard_map/ppermute | solution.py:399
  40.2 5.1 %collective-permute-start.3 = (bf16[4,72,128]{2,1,0:T(8,128)(2,1)S(1)}, bf16[4,72,128]{2,1,0:T(8,128)(2,1)S(1)}, u32[]{:S(2)}, u32[]{:S(2)}) collective-permute-start(bf16[4,72,128]{2,1,0:T(8,128)(2,1)S(1)} %get-tuple-element.44), channel_id=1, source_target_pairs={{0,3},{1,0},{2,1},{3,2},{4,7},{5,4},{6,5},{7,6},{8,11},{9,8},{10,9... | collective-permute-start | bytes 221192 | tf_op jit(solution)/shard_map/ppermute | solution.py:399
  45.3 23.9 %collective-permute-start.4 = (bf16[96,128]{1,0:T(8,128)(2,1)S(1)}, bf16[96,128]{1,0:T(8,128)(2,1)S(1)}, u32[]{:S(2)}, u32[]{:S(2)}) collective-permute-start(bf16[96,128]{1,0:T(8,128)(2,1)S(1)} %get-tuple-element.46), channel_id=1, source_target_pairs={{0,4},{1,5},{2,6},{3,7},{4,8},{5,9},{6,10},{7,11},{8,12},{9,13},{1... | collective-permute-start | bytes 73736 | tf_op jit(solution)/shard_map/ppermute | solution.py:406
  45.4 23.8 %collective-permute-start.5 = (bf16[96,128]{1,0:T(8,128)(2,1)S(1)}, bf16[96,128]{1,0:T(8,128)(2,1)S(1)}, u32[]{:S(2)}, u32[]{:S(2)}) collective-permute-start(bf16[96,128]{1,0:T(8,128)(2,1)S(1)} %get-tuple-element.47), channel_id=1, source_target_pairs={{0,8},{1,9},{2,10},{3,11},{4,12},{5,13},{6,14},{7,15},{8,0},{9,1},... | collective-permute-start | bytes 73736 | tf_op jit(solution)/shard_map/ppermute | solution.py:406
  47.2 22.1 %collective-permute-start.6 = (bf16[96,128]{1,0:T(8,128)(2,1)S(1)}, bf16[96,128]{1,0:T(8,128)(2,1)S(1)}, u32[]{:S(2)}, u32[]{:S(2)}) collective-permute-start(bf16[96,128]{1,0:T(8,128)(2,1)S(1)} %get-tuple-element.48), channel_id=1, source_target_pairs={{0,12},{1,13},{2,14},{3,15},{4,0},{5,1},{6,2},{7,3},{8,4},{9,5},{1... | collective-permute-start | bytes 73736 | tf_op jit(solution)/shard_map/ppermute | solution.py:406
  51.4 17.8 %copy-start.1 = (f32[2,32,128]{2,1,0:T(8,128)S(1)}, f32[2,32,128]{2,1,0:T(8,128)}, u32[]{:S(2)}) copy-start(f32[2,32,128]{2,1,0:T(8,128)} %param.12) | copy-start | bytes 98308
  51.4 17.8 %copy-start.2 = (f32[2,32,128]{2,1,0:T(8,128)S(1)}, f32[2,32,128]{2,1,0:T(8,128)}, u32[]{:S(2)}) copy-start(f32[2,32,128]{2,1,0:T(8,128)} %param.13) | copy-start | bytes 98308
  51.4 17.8 %copy-start.3 = (f32[2,32,128]{2,1,0:T(8,128)S(1)}, f32[2,32,128]{2,1,0:T(8,128)}, u32[]{:S(2)}) copy-start(f32[2,32,128]{2,1,0:T(8,128)} %param.14) | copy-start | bytes 98308

commit v8 on v7

--- a/solution.py
+++ b/solution.py
@@ -240,7 +240,7 @@
         outs[d][...] = packets[(x + d) & 3]
 
 
-def relay_kernel(y_at, own, one, two, three, *outs):
+def relay_kernel(y_at, own, two, one, three, *outs):
     y = y_at[0]
     for d in range(4):
         to = (y + d) & 3
@@ -251,7 +251,7 @@
 
 
 def finish_kernel(
-    y_at, x_at, packed, got_own, got_one, got_two, got_three, slot, latents, mean, square, out_one, out_two, out_three, out_latents, out_mean, out_square, out_pred, *scratch
+    y_at, x_at, packed, got_own, got_two, got_one, got_three, slot, latents, mean, square, out_one, out_two, out_three, out_latents, out_mean, out_square, out_pred, *scratch
 ):
     grad_one, grad_two, grad_three, new_latents, new_mean, new_square, predictions, preds, sems = scratch
     copies = []
@@ -402,7 +402,7 @@
         tuple([shape((RELAY_ROWS, LANES), bf16)] * 4),
         (),
         [smem] + [vmem] * 4,
-    )(at_y, rows_x[0], got_x[1], got_x[2], got_x[3])
+    )(at_y, rows_x[0], got_x[2], got_x[1], got_x[3])
     got_y = {d: lax.ppermute(rows_y[d], "exp", along(d, 0)) for d in (2, 1, 3)}
     own = jnp.sum(parts.astype(f32), axis=0).astype(bf16)
     packed = lax.all_gather(own, "rep", axis=0, tiled=False)
@@ -416,7 +416,7 @@
         [smem] * 2 + [vmem] * 9,
         0,
         tuple([hbm] * 7),
-    )(at_y, at_x, packed, rows_y[0], got_y[1], got_y[2], got_y[3], slot, flat(latents), flat(latent_mean), flat(latent_square))
+    )(at_y, at_x, packed, rows_y[0], got_y[2], got_y[1], got_y[3], slot, flat(latents), flat(latent_mean), flat(latent_square))
     grad_three = jnp.swapaxes(grad_three, 0, 1)
     whole = lambda a: a.reshape(latents.shape)
     return (

time: 71.2 us -> 71.6 us (level)
  starting transfers between devices: 23.3 us -> 24.1 us
  waiting for transfers between devices: 13.2 us -> 12.4 us
    all_to_all x1, waiting for transfers between devices: 3.27 us -> 2.4 us  [on_device(): lax.all_to_all(chip, 'rep', 0, 0, tiled=True, axis_index_groups=chips)]
where the time goes in v8:
time: 71.6 us; the launch traced here: 71.2 us
  starting transfers between devices  24.1 us (34%)
  blocking collectives  18.1 us (25%)
  Pallas kernels  12.4 us (17%)
  waiting for transfers between devices  12.4 us (17%)
  local copies, waits for them, and re-layouts  2.2 us (3%)
  other arithmetic  1.02 us (1%)
  between operations  0.99 us (1%)
    all_gather x1, blocking collectives, on_device(): packed = lax.all_gather(own, 'rep', axis=0, tiled=False)  18.1 us
    all_to_all x1, starting transfers between devices, on_device(): lax.all_to_all(chip, 'rep', 0, 0, tiled=True, axis_index_groups=chips)  8.18 us
    all_to_all x1, starting transfers between devices, on_device(): recv = lax.all_to_all(send, 'exp', 0, 0, tiled=True)  7.6 us
    all_to_all x1, waiting for transfers between devices, on_device(): recv = lax.all_to_all(send, 'exp', 0, 0, tiled=True)  6.03 us
    ppermute x3, waiting for transfers between devices, on_device(): got_x = {d: lax.ppermute(rows_x[d], 'exp', along(0, d)) for d in (2, 1, 3)}  3.9 us
    pallas_call x1, Pallas kernels, on_device(): grads_a, back_a, preds_a, index_a = half(False, bf16)(core, recv, *weights)  3.52 us
    pallas_call x1, Pallas kernels, on_device(): grads_b, back_b, preds_b, index_b = half(True, f32)(core, recv, *weights)  3.52 us
    ppermute x3, starting transfers between devices, on_device(): got_x = {d: lax.ppermute(rows_x[d], 'exp', along(0, d)) for d in (2, 1, 3)}  3.34 us
  transfers between devices with their start and end apart: 9, of which 4 were waited for; matrix products, arithmetic and copies ran while one was open for 2% of the time, Pallas kernels for 7%

profile of v8, /device:TPU:1, one launch (start us, length us, event | category | flops | bytes accessed | tf_op | source)
XLA Modules:
  0.0 71.2 jit_solution(4668777742449277157)
XLA Ops:
  0.6 2.5 %shard_map.171 = (bf16[16,80,128]{2,1,0:T(8,128)(2,1)}, s32[16,128]{1,0:T(8,128)S(1)}) custom-call(s32[16,128]{1,0:T(8,128)} %bitcast.29, s32[16,128]{1,0:T(8,128)} %bitcast.30, s32[16,128]{1,0:T(8,128)} %bitcast.31, s32[16,128]{1,0:T(8,128)} %bitcast.32, f32[3,2048]{1,0:T(4,128)} %targets_in.1, f32[64,128]{1,0:T(8,128)} %bitcast.23), custom_call_target="tpu_custom_call" | custom-call | tf_op jit(solution)/shard_map/pallas_call | solution.py:347
  3.2 7.6 %all-to-all-start = ((bf16[16,80,128]{2,1,0:T(8,128)(2,1)}), bf16[16,80,128]{2,1,0:T(8,128)(2,1)S(1)}, u32[]{:S(2)}, u32[]{:S(2)}) async-start(bf16[16,80,128]{2,1,0:T(8,128)(2,1)} %get-tuple-element.32), calls=%async_computation | async-start | bytes 655360 | tf_op jit(solution)/shard_map/all_to_all | solution.py:357
  10.8 0.2 copy.28
  11.0 0.1 fusion
  11.1 0.2 copy.30.w_two
  11.3 0.5 copy-done.6
  11.8 0.2 copy.29
  12.0 0.0 copy-start
  12.0 0.1 copy.34
  12.1 0.8 %copy-done = bf16[4,64,256]{2,1,0:T(8,128)(2,1)S(1)} copy-done((bf16[4,64,256]{2,1,0:T(8,128)(2,1)S(1)}, bf16[4,64,256]{2,1,0:T(8,128)(2,1)}, u32[]{:S(2)}) %copy-start) | copy-done | bytes 131096
  12.9 0.2 copy.26
  13.1 0.1 multiply_bitcast_fusion.w_three_t
  13.2 6.0 %all-to-all-done.recv = bf16[16,80,128]{2,1,0:T(8,128)(2,1)S(1)} async-done(((bf16[16,80,128]{2,1,0:T(8,128)(2,1)}), bf16[16,80,128]{2,1,0:T(8,128)(2,1)S(1)}, u32[]{:S(2)}, u32[]{:S(2)}) %all-to-all-start) | async-done | bytes 327712 | tf_op jit(solution)/shard_map/all_to_all | solution.py:357
  19.2 3.5 %shard_map.173 = (bf16[8,168,128]{2,1,0:T(8,128)(2,1)S(1)}, bf16[2,32,1024]{2,1,0:T(8,128)(2,1)S(1)}, f32[2,8,1024]{2,1,0:T(8,128)S(1)}, f32[2,8,1024]{2,1,0:T(8,128)S(1)}) custom-call(s32[1]{0:T(128)} %bitcast.2.core_at, bf16[16,80,128]{2,1,0:T(8,128)(2,1)S(1)} %all-to-all-done.recv, bf16[4,64,256]{2,1,0:T(8,128)(2,1)S(1)} %copy-done, ...), custom_call_target="tpu_custom_call" | custom-call | flops 2000000000 | tf_op jit(solution)/shard_map/pallas_call | solution.py:383
  22.8 1.9 %collective-permute-start = (bf16[8,168,128]{2,1,0:T(8,128)(2,1)S(1)}, bf16[8,168,128]{2,1,0:T(8,128)(2,1)S(1)}, u32[]{:S(2)}, u32[]{:S(2)}) collective-permute-start(bf16[8,168,128]{2,1,0:T(8,128)(2,1)S(1)} %get-tuple-element.34), channel_id=1, source_target_pairs={{0,16},{16,0},{32,48},{48,32},{64,80},{80,64},{96,112},{112,96},{1... | collective-permute-start | bytes 1032200 | tf_op jit(solution)/shard_map/ppermute | solution.py:384
  24.7 3.5 %shard_map.172 = (f32[8,168,128]{2,1,0:T(8,128)S(1)}, bf16[2,32,1024]{2,1,0:T(8,128)(2,1)S(1)}, f32[2,8,1024]{2,1,0:T(8,128)S(1)}, f32[2,8,1024]{2,1,0:T(8,128)S(1)}) custom-call(s32[1]{0:T(128)} %bitcast.2.core_at, bf16[16,80,128]{2,1,0:T(8,128)(2,1)S(1)} %all-to-all-done.recv, bf16[4,64,256]{2,1,0:T(8,128)(2,1)S(1)} %copy-done, ...), custom_call_target="tpu_custom_call" | custom-call | flops 2000000000 | tf_op jit(solution)/shard_map/pallas_call | solution.py:385
  28.2 0.0 collective-permute-done
  28.2 0.8 %add_convert_fusion = bf16[8,168,128]{2,1,0:T(8,128)(2,1)} fusion(f32[8,168,128]{2,1,0:T(8,128)S(1)} %get-tuple-element.33, bf16[8,168,128]{2,1,0:T(8,128)(2,1)S(1)} %collective-permute-done), kind=kLoop, calls=%fused_computation | loop fusion | flops 516096 | bytes 1376256 | tf_op jit(solution)/shard_map/convert_element_type | solution.py:386
  29.0 8.2 %all-to-all-start.1 = ((bf16[8,168,128]{2,1,0:T(8,128)(2,1)}), bf16[8,168,128]{2,1,0:T(8,128)(2,1)S(1)}, u32[]{:S(2)}, u32[]{:S(2)}) async-start(bf16[8,168,128]{2,1,0:T(8,128)(2,1)} %add_convert_fusion), calls=%async_computation.1 | async-start | bytes 688128 | tf_op jit(solution)/shard_map/all_to_all | solution.py:388
  37.2 1.3 %shard_map.174 = (bf16[4,72,128]{2,1,0:T(8,128)(2,1)S(1)}, bf16[4,72,128]{2,1,0:T(8,128)(2,1)S(1)}, bf16[4,72,128]{2,1,0:T(8,128)(2,1)S(1)}, bf16[4,72,128]{2,1,0:T(8,128)(2,1)S(1)}) custom-call(s32[1]{0:T(128)} %bitcast.2.core_at, s32[1]{0:T(128)} %bitcast.1.x_at, bf16[2,32,1024]{2,1,0:T(8,128)(2,1)S(1)} %get-tuple-element.35.back_a, ...), custom_call_target="tpu_custom_call" | custom-call | flops 2000000000 | tf_op jit(solution)/shard_map/pallas_call | solution.py:392
  38.6 0.7 collective-permute-start.1
  39.2 0.3 collective-permute-start.2
  39.6 2.4 %collective-permute-start.3 = (bf16[4,72,128]{2,1,0:T(8,128)(2,1)S(1)}, bf16[4,72,128]{2,1,0:T(8,128)(2,1)S(1)}, u32[]{:S(2)}, u32[]{:S(2)}) collective-permute-start(bf16[4,72,128]{2,1,0:T(8,128)(2,1)S(1)} %get-tuple-element.44), channel_id=1, source_target_pairs={{0,3},{1,0},{2,1},{3,2},{4,7},{5,4},{6,5},{7,6},{8,11},{9,8},{10,9... | collective-permute-start | bytes 221192 | tf_op jit(solution)/shard_map/ppermute | solution.py:399
  41.9 1.8 %collective-permute-done.1.two = bf16[4,72,128]{2,1,0:T(8,128)(2,1)S(1)} collective-permute-done((bf16[4,72,128]{2,1,0:T(8,128)(2,1)S(1)}, bf16[4,72,128]{2,1,0:T(8,128)(2,1)S(1)}, u32[]{:S(2)}, u32[]{:S(2)}) %collective-permute-start.1) | collective-permute-done | bytes 73760 | tf_op jit(solution)/shard_map/ppermute | solution.py:399
  43.7 2.1 %collective-permute-done.2.one = bf16[4,72,128]{2,1,0:T(8,128)(2,1)S(1)} collective-permute-done((bf16[4,72,128]{2,1,0:T(8,128)(2,1)S(1)}, bf16[4,72,128]{2,1,0:T(8,128)(2,1)S(1)}, u32[]{:S(2)}, u32[]{:S(2)}) %collective-permute-start.2) | collective-permute-done | bytes 73760 | tf_op jit(solution)/shard_map/ppermute | solution.py:399
  45.9 0.4 collective-permute-start.4
  46.3 0.7 collective-permute-start.5
  47.0 2.0 %collective-permute-start.6 = (bf16[96,128]{1,0:T(8,128)(2,1)S(1)}, bf16[96,128]{1,0:T(8,128)(2,1)S(1)}, u32[]{:S(2)}, u32[]{:S(2)}) collective-permute-start(bf16[96,128]{1,0:T(8,128)(2,1)S(1)} %get-tuple-element.48), channel_id=1, source_target_pairs={{0,12},{1,13},{2,14},{3,15},{4,0},{5,1},{6,2},{7,3},{8,4},{9,5},{1... | collective-permute-start | bytes 73736 | tf_op jit(solution)/shard_map/ppermute | solution.py:406
  48.9 2.4 %all-to-all-done.1 = bf16[8,168,128]{2,1,0:T(8,128)(2,1)S(1)} async-done(((bf16[8,168,128]{2,1,0:T(8,128)(2,1)}), bf16[8,168,128]{2,1,0:T(8,128)(2,1)S(1)}, u32[]{:S(2)}, u32[]{:S(2)}) %all-to-all-start.1) | async-done | bytes 344096 | tf_op jit(solution)/shard_map/all_to_all | solution.py:388
  51.4 0.1 reduce_sum.12
  51.4 18.1 %all-gather = bf16[2688,128]{1,0:T(8,128)(2,1)S(1)} all-gather(bf16[168,128]{1,0:T(8,128)(2,1)S(1)} %reduce_sum.12), channel_id=2, replica_groups=mesh['rep'=16,'exp'=16] {'rep'}, dimensions={0}, use_global_device_ids=true | all-gather | bytes 731136 | tf_op jit(solution)/shard_map/all_gather | solution.py:408
  69.6 1.4 %shard_map.176 = (f32[4,64,256]{2,1,0:T(8,128)}, f32[4,256,256]{2,1,0:T(8,128)}, f32[3,4,256]{2,1,0:T(4,128)}, f32[64,128]{1,0:T(8,128)}, f32[64,128]{1,0:T(8,12...) custom-call(s32[1]{0:T(128)} %bitcast.y_at, s32[1]{0:T(128)} %bitcast.1.x_at, bf16[16,168,128]{2,1,0:T(8,128)(2,1)S(1)} %bitcast.22, ...), custom_call_target="tpu_custom_call" | custom-call | tf_op jit(solution)/shard_map/pallas_call | solution.py:411
  (18 shorter events, 0.1 us)
Async XLA Ops:
  0.6 10.1 %copy-start.5 = (bf16[4,256,256]{2,1,0:T(8,128)(2,1)S(1)}, bf16[4,256,256]{2,1,0:T(8,128)(2,1)}, u32[]{:S(2)}) copy-start(bf16[4,256,256]{2,1,0:T(8,128)(2,1)} %param.16) | copy-start | bytes 1572868
  3.2 16.1 %all-to-all-start = ((bf16[16,80,128]{2,1,0:T(8,128)(2,1)}), bf16[16,80,128]{2,1,0:T(8,128)(2,1)S(1)}, u32[]{:S(2)}, u32[]{:S(2)}) async-start(bf16[16,80,128]{2,1,0:T(8,128)(2,1)} %get-tuple-element.32), calls=%async_computation | async-start | bytes 655360 | tf_op jit(solution)/shard_map/all_to_all | solution.py:357
  11.1 0.7 copy-start.6
  12.0 0.9 %copy-start = (bf16[4,64,256]{2,1,0:T(8,128)(2,1)S(1)}, bf16[4,64,256]{2,1,0:T(8,128)(2,1)}, u32[]{:S(2)}) copy-start(bf16[4,64,256]{2,1,0:T(8,128)(2,1)} %w_one.3) | copy-start | bytes 393220
  13.2 6.1 %copy-start.4 = (bf16[256,32]{0,1:T(8,128)(2,1)S(1)}, bf16[256,32]{0,1:T(8,128)(2,1)}, u32[]{:S(2)}) copy-start(bf16[256,32]{0,1:T(8,128)(2,1)} %param.18) | copy-start | bytes 49156
  22.8 5.5 %collective-permute-start = (bf16[8,168,128]{2,1,0:T(8,128)(2,1)S(1)}, bf16[8,168,128]{2,1,0:T(8,128)(2,1)S(1)}, u32[]{:S(2)}, u32[]{:S(2)}) collective-permute-start(bf16[8,168,128]{2,1,0:T(8,128)(2,1)S(1)} %get-tuple-element.34), channel_id=1, source_target_pairs={{0,16},{16,0},{32,48},{48,32},{64,80},{80,64},{96,112},{112,96},{1... | collective-permute-start | bytes 1032200 | tf_op jit(solution)/shard_map/ppermute | solution.py:384
  29.0 22.3 %all-to-all-start.1 = ((bf16[8,168,128]{2,1,0:T(8,128)(2,1)}), bf16[8,168,128]{2,1,0:T(8,128)(2,1)S(1)}, u32[]{:S(2)}, u32[]{:S(2)}) async-start(bf16[8,168,128]{2,1,0:T(8,128)(2,1)} %add_convert_fusion), calls=%async_computation.1 | async-start | bytes 688128 | tf_op jit(solution)/shard_map/all_to_all | solution.py:388
  38.6 5.2 %collective-permute-start.1 = (bf16[4,72,128]{2,1,0:T(8,128)(2,1)S(1)}, bf16[4,72,128]{2,1,0:T(8,128)(2,1)S(1)}, u32[]{:S(2)}, u32[]{:S(2)}) collective-permute-start(bf16[4,72,128]{2,1,0:T(8,128)(2,1)S(1)} %get-tuple-element.42), channel_id=1, source_target_pairs={{0,2},{1,3},{2,0},{3,1},{4,6},{5,7},{6,4},{7,5},{8,10},{9,11},{10,... | collective-permute-start | bytes 221192 | tf_op jit(solution)/shard_map/ppermute | solution.py:399
  39.2 6.6 %collective-permute-start.2 = (bf16[4,72,128]{2,1,0:T(8,128)(2,1)S(1)}, bf16[4,72,128]{2,1,0:T(8,128)(2,1)S(1)}, u32[]{:S(2)}, u32[]{:S(2)}) collective-permute-start(bf16[4,72,128]{2,1,0:T(8,128)(2,1)S(1)} %get-tuple-element.43), channel_id=1, source_target_pairs={{0,1},{1,2},{2,3},{3,0},{4,5},{5,6},{6,7},{7,4},{8,9},{9,10},{10,1... | collective-permute-start | bytes 221192 | tf_op jit(solution)/shard_map/ppermute | solution.py:399
  39.6 6.3 %collective-permute-start.3 = (bf16[4,72,128]{2,1,0:T(8,128)(2,1)S(1)}, bf16[4,72,128]{2,1,0:T(8,128)(2,1)S(1)}, u32[]{:S(2)}, u32[]{:S(2)}) collective-permute-start(bf16[4,72,128]{2,1,0:T(8,128)(2,1)S(1)} %get-tuple-element.44), channel_id=1, source_target_pairs={{0,3},{1,0},{2,1},{3,2},{4,7},{5,4},{6,5},{7,6},{8,11},{9,8},{10,9... | collective-permute-start | bytes 221192 | tf_op jit(solution)/shard_map/ppermute | solution.py:399
  45.9 23.7 %collective-permute-start.4 = (bf16[96,128]{1,0:T(8,128)(2,1)S(1)}, bf16[96,128]{1,0:T(8,128)(2,1)S(1)}, u32[]{:S(2)}, u32[]{:S(2)}) collective-permute-start(bf16[96,128]{1,0:T(8,128)(2,1)S(1)} %get-tuple-element.46), channel_id=1, source_target_pairs={{0,8},{1,9},{2,10},{3,11},{4,12},{5,13},{6,14},{7,15},{8,0},{9,1},... | collective-permute-start | bytes 73736 | tf_op jit(solution)/shard_map/ppermute | solution.py:406
  46.3 23.3 %collective-permute-start.5 = (bf16[96,128]{1,0:T(8,128)(2,1)S(1)}, bf16[96,128]{1,0:T(8,128)(2,1)S(1)}, u32[]{:S(2)}, u32[]{:S(2)}) collective-permute-start(bf16[96,128]{1,0:T(8,128)(2,1)S(1)} %get-tuple-element.47), channel_id=1, source_target_pairs={{0,4},{1,5},{2,6},{3,7},{4,8},{5,9},{6,10},{7,11},{8,12},{9,13},{1... | collective-permute-start | bytes 73736 | tf_op jit(solution)/shard_map/ppermute | solution.py:406
  47.0 22.6 %collective-permute-start.6 = (bf16[96,128]{1,0:T(8,128)(2,1)S(1)}, bf16[96,128]{1,0:T(8,128)(2,1)S(1)}, u32[]{:S(2)}, u32[]{:S(2)}) collective-permute-start(bf16[96,128]{1,0:T(8,128)(2,1)S(1)} %get-tuple-element.48), channel_id=1, source_target_pairs={{0,12},{1,13},{2,14},{3,15},{4,0},{5,1},{6,2},{7,3},{8,4},{9,5},{1... | collective-permute-start | bytes 73736 | tf_op jit(solution)/shard_map/ppermute | solution.py:406
  51.4 18.2 %copy-start.1 = (f32[2,32,128]{2,1,0:T(8,128)S(1)}, f32[2,32,128]{2,1,0:T(8,128)}, u32[]{:S(2)}) copy-start(f32[2,32,128]{2,1,0:T(8,128)} %param.12) | copy-start | bytes 98308
  51.4 18.2 %copy-start.2 = (f32[2,32,128]{2,1,0:T(8,128)S(1)}, f32[2,32,128]{2,1,0:T(8,128)}, u32[]{:S(2)}) copy-start(f32[2,32,128]{2,1,0:T(8,128)} %param.13) | copy-start | bytes 98308
  51.4 18.2 %copy-start.3 = (f32[2,32,128]{2,1,0:T(8,128)S(1)}, f32[2,32,128]{2,1,0:T(8,128)}, u32[]{:S(2)}) copy-start(f32[2,32,128]{2,1,0:T(8,128)} %param.14) | copy-start | bytes 98308

commit v9 on v8

--- a/solution.py
+++ b/solution.py
@@ -17,8 +17,8 @@
 ROWS = 2048
 CHUNKS = ROWS // LANES
 SLOTS = N_EXP * CAP
-GROUPS = 8
-LOW = 512
+GROUPS = 16
+LOW = 256
 PIECES = 2
 TEX_ROWS = 64
 SEND_ROWS = TEX_ROWS + 16
@@ -63,11 +63,7 @@
 
 
 def split_index(rows):
-    high = rows[3:4].astype(jnp.int32) - 1
-    group = high >> 1
-    bit = high & 1
-    low = jnp.concatenate([hot_wide(jnp.where(bit == b, rows[4:5], -1.0)) for b in range(2)], axis=0)
-    return group, low
+    return rows[3:4] - 1.0, hot_wide(rows[4:5])
 
 
 def route_kernel(mat, tile_in, texel_in, direction_in, targets_in, latents_in, send, slot, *scratch):
@@ -104,8 +100,7 @@
     pair = material >> 1
     slot[...] = pair * LANES + lane
     texels = texel[...]
-    group = (texels >> 9) * 2 + tile[...]
-    high = (group * 2 + ((texels >> 8) & 1) + 1).astype(f32)
+    high = ((texels >> 8) * 2 + tile[...] + 1).astype(f32)
     low = (texels & 255).astype(f32)
     heading = (direction[...] + 1).astype(f32)
     values = []
@@ -137,9 +132,9 @@
 ):
     core = core_at[0]
     h = core if keep else 1 - core
-    for b in range(4):
-        for s in range(4):
-            tex[b * TEX_ROWS : (b + 1) * TEX_ROWS, s * LANES : (s + 1) * LANES] = recv[4 * b + s, :TEX_ROWS]
+    for b in range(8):
+        for s in range(2):
+            tex[b * TEX_ROWS : (b + 1) * TEX_ROWS, s * LANES : (s + 1) * LANES] = recv[2 * b + s, :TEX_ROWS]
     left = iota((8, LANES), 1) < CAP
     sides = ([], [])
     for j in range(N_EXP // 2):
@@ -222,7 +217,8 @@
     *outs, packets = outs
     for y in range(4):
         for x in range(4):
-            packets[x, y, :TEX_ROWS] = acc[y * TEX_ROWS : (y + 1) * TEX_ROWS, x * LANES : (x + 1) * LANES].astype(bf16)
+            first = (2 * y + x // 2) * TEX_ROWS
+            packets[x, y, :TEX_ROWS] = acc[first : first + TEX_ROWS, x % 2 * LANES : (x % 2 + 1) * LANES].astype(bf16)
     left = iota((8, LANES), 1) < CAP
     keep = core_at[0]
     for j in range(N_EXP // 2):

time: 71.6 us -> 71.7 us (level)
  no operation moved by 1% of the time
where the time goes in v9:
time: 71.7 us; the launch traced here: 71.3 us
  starting transfers between devices  24.3 us (34%)
  blocking collectives  18.3 us (26%)
  Pallas kernels  12.2 us (17%)
  waiting for transfers between devices  12.2 us (17%)
  local copies, waits for them, and re-layouts  2.2 us (3%)
  other arithmetic  1.02 us (1%)
  between operations  0.99 us (1%)
    all_gather x1, blocking collectives, on_device(): packed = lax.all_gather(own, 'rep', axis=0, tiled=False)  18.3 us
    all_to_all x1, starting transfers between devices, on_device(): lax.all_to_all(chip, 'rep', 0, 0, tiled=True, axis_index_groups=chips)  8.17 us
    all_to_all x1, starting transfers between devices, on_device(): recv = lax.all_to_all(send, 'exp', 0, 0, tiled=True)  7.6 us
    all_to_all x1, waiting for transfers between devices, on_device(): recv = lax.all_to_all(send, 'exp', 0, 0, tiled=True)  6.03 us
    ppermute x3, waiting for transfers between devices, on_device(): got_x = {d: lax.ppermute(rows_x[d], 'exp', along(0, d)) for d in (2, 1, 3)}  3.86 us
    pallas_call x1, Pallas kernels, on_device(): grads_b, back_b, preds_b, index_b = half(True, f32)(core, recv, *weights)  3.47 us
    pallas_call x1, Pallas kernels, on_device(): grads_a, back_a, preds_a, index_a = half(False, bf16)(core, recv, *weights)  3.46 us
    ppermute x3, starting transfers between devices, on_device(): got_x = {d: lax.ppermute(rows_x[d], 'exp', along(0, d)) for d in (2, 1, 3)}  3.37 us
  transfers between devices with their start and end apart: 9, of which 4 were waited for; matrix products, arithmetic and copies ran while one was open for 2% of the time, Pallas kernels for 7%

profile of v9, /device:TPU:1, one launch (start us, length us, event | category | flops | bytes accessed | tf_op | source)
XLA Modules:
  0.0 71.3 jit_solution(10872690467311462912)
XLA Ops:
  0.6 2.5 %shard_map.171 = (bf16[16,80,128]{2,1,0:T(8,128)(2,1)}, s32[16,128]{1,0:T(8,128)S(1)}) custom-call(s32[16,128]{1,0:T(8,128)} %bitcast.29, s32[16,128]{1,0:T(8,128)} %bitcast.30, s32[16,128]{1,0:T(8,128)} %bitcast.31, s32[16,128]{1,0:T(8,128)} %bitcast.32, f32[3,2048]{1,0:T(4,128)} %targets_in.1, f32[64,128]{1,0:T(8,128)} %bitcast.23), custom_call_target="tpu_custom_call" | custom-call | tf_op jit(solution)/shard_map/pallas_call | solution.py:343
  3.2 7.6 %all-to-all-start = ((bf16[16,80,128]{2,1,0:T(8,128)(2,1)}), bf16[16,80,128]{2,1,0:T(8,128)(2,1)S(1)}, u32[]{:S(2)}, u32[]{:S(2)}) async-start(bf16[16,80,128]{2,1,0:T(8,128)(2,1)} %get-tuple-element.32), calls=%async_computation | async-start | bytes 655360 | tf_op jit(solution)/shard_map/all_to_all | solution.py:353
  10.8 0.2 copy.28
  11.0 0.1 fusion
  11.1 0.0 copy-start.6
  11.1 0.2 copy.30.w_two
  11.3 0.5 copy-done.6
  11.8 0.2 copy.29
  12.0 0.1 copy.34
  12.1 0.8 %copy-done = bf16[4,64,256]{2,1,0:T(8,128)(2,1)S(1)} copy-done((bf16[4,64,256]{2,1,0:T(8,128)(2,1)S(1)}, bf16[4,64,256]{2,1,0:T(8,128)(2,1)}, u32[]{:S(2)}) %copy-start) | copy-done | bytes 131096
  12.9 0.2 copy.26
  13.1 0.1 multiply_bitcast_fusion.w_three_t
  13.2 6.0 %all-to-all-done.recv = bf16[16,80,128]{2,1,0:T(8,128)(2,1)S(1)} async-done(((bf16[16,80,128]{2,1,0:T(8,128)(2,1)}), bf16[16,80,128]{2,1,0:T(8,128)(2,1)S(1)}, u32[]{:S(2)}, u32[]{:S(2)}) %all-to-all-start) | async-done | bytes 327712 | tf_op jit(solution)/shard_map/all_to_all | solution.py:353
  19.2 3.5 %shard_map.173 = (bf16[8,168,128]{2,1,0:T(8,128)(2,1)S(1)}, bf16[2,32,1024]{2,1,0:T(8,128)(2,1)S(1)}, f32[2,8,1024]{2,1,0:T(8,128)S(1)}, f32[2,8,1024]{2,1,0:T(8,128)S(1)}) custom-call(s32[1]{0:T(128)} %bitcast.2.core_at, bf16[16,80,128]{2,1,0:T(8,128)(2,1)S(1)} %all-to-all-done.recv, bf16[4,64,256]{2,1,0:T(8,128)(2,1)S(1)} %copy-done, ...), custom_call_target="tpu_custom_call" | custom-call | flops 2000000000 | tf_op jit(solution)/shard_map/pallas_call | solution.py:379
  22.7 1.9 %collective-permute-start = (bf16[8,168,128]{2,1,0:T(8,128)(2,1)S(1)}, bf16[8,168,128]{2,1,0:T(8,128)(2,1)S(1)}, u32[]{:S(2)}, u32[]{:S(2)}) collective-permute-start(bf16[8,168,128]{2,1,0:T(8,128)(2,1)S(1)} %get-tuple-element.34), channel_id=1, source_target_pairs={{0,16},{16,0},{32,48},{48,32},{64,80},{80,64},{96,112},{112,96},{1... | collective-permute-start | bytes 1032200 | tf_op jit(solution)/shard_map/ppermute | solution.py:380
  24.7 3.5 %shard_map.172 = (f32[8,168,128]{2,1,0:T(8,128)S(1)}, bf16[2,32,1024]{2,1,0:T(8,128)(2,1)S(1)}, f32[2,8,1024]{2,1,0:T(8,128)S(1)}, f32[2,8,1024]{2,1,0:T(8,128)S(1)}) custom-call(s32[1]{0:T(128)} %bitcast.2.core_at, bf16[16,80,128]{2,1,0:T(8,128)(2,1)S(1)} %all-to-all-done.recv, bf16[4,64,256]{2,1,0:T(8,128)(2,1)S(1)} %copy-done, ...), custom_call_target="tpu_custom_call" | custom-call | flops 2000000000 | tf_op jit(solution)/shard_map/pallas_call | solution.py:381
  28.1 0.0 collective-permute-done
  28.1 0.8 %add_convert_fusion = bf16[8,168,128]{2,1,0:T(8,128)(2,1)} fusion(f32[8,168,128]{2,1,0:T(8,128)S(1)} %get-tuple-element.33, bf16[8,168,128]{2,1,0:T(8,128)(2,1)S(1)} %collective-permute-done), kind=kLoop, calls=%fused_computation | loop fusion | flops 516096 | bytes 1376256 | tf_op jit(solution)/shard_map/convert_element_type | solution.py:382
  28.9 8.2 %all-to-all-start.1 = ((bf16[8,168,128]{2,1,0:T(8,128)(2,1)}), bf16[8,168,128]{2,1,0:T(8,128)(2,1)S(1)}, u32[]{:S(2)}, u32[]{:S(2)}) async-start(bf16[8,168,128]{2,1,0:T(8,128)(2,1)} %add_convert_fusion), calls=%async_computation.1 | async-start | bytes 688128 | tf_op jit(solution)/shard_map/all_to_all | solution.py:384
  37.1 1.3 %shard_map.174 = (bf16[4,72,128]{2,1,0:T(8,128)(2,1)S(1)}, bf16[4,72,128]{2,1,0:T(8,128)(2,1)S(1)}, bf16[4,72,128]{2,1,0:T(8,128)(2,1)S(1)}, bf16[4,72,128]{2,1,0:T(8,128)(2,1)S(1)}) custom-call(s32[1]{0:T(128)} %bitcast.2.core_at, s32[1]{0:T(128)} %bitcast.1.x_at, bf16[2,32,1024]{2,1,0:T(8,128)(2,1)S(1)} %get-tuple-element.35.back_a, ...), custom_call_target="tpu_custom_call" | custom-call | flops 2000000000 | tf_op jit(solution)/shard_map/pallas_call | solution.py:388
  38.4 0.7 collective-permute-start.1
  39.1 0.3 collective-permute-start.2
  39.5 2.4 %collective-permute-start.3 = (bf16[4,72,128]{2,1,0:T(8,128)(2,1)S(1)}, bf16[4,72,128]{2,1,0:T(8,128)(2,1)S(1)}, u32[]{:S(2)}, u32[]{:S(2)}) collective-permute-start(bf16[4,72,128]{2,1,0:T(8,128)(2,1)S(1)} %get-tuple-element.44), channel_id=1, source_target_pairs={{0,3},{1,0},{2,1},{3,2},{4,7},{5,4},{6,5},{7,6},{8,11},{9,8},{10,9... | collective-permute-start | bytes 221192 | tf_op jit(solution)/shard_map/ppermute | solution.py:395
  41.8 1.8 %collective-permute-done.1.two = bf16[4,72,128]{2,1,0:T(8,128)(2,1)S(1)} collective-permute-done((bf16[4,72,128]{2,1,0:T(8,128)(2,1)S(1)}, bf16[4,72,128]{2,1,0:T(8,128)(2,1)S(1)}, u32[]{:S(2)}, u32[]{:S(2)}) %collective-permute-start.1) | collective-permute-done | bytes 73760 | tf_op jit(solution)/shard_map/ppermute | solution.py:395
  43.6 2.1 %collective-permute-done.2.one = bf16[4,72,128]{2,1,0:T(8,128)(2,1)S(1)} collective-permute-done((bf16[4,72,128]{2,1,0:T(8,128)(2,1)S(1)}, bf16[4,72,128]{2,1,0:T(8,128)(2,1)S(1)}, u32[]{:S(2)}, u32[]{:S(2)}) %collective-permute-start.2) | collective-permute-done | bytes 73760 | tf_op jit(solution)/shard_map/ppermute | solution.py:395
  45.7 0.6 collective-permute-start.4
  46.3 0.7 collective-permute-start.5
  47.0 2.0 %collective-permute-start.6 = (bf16[96,128]{1,0:T(8,128)(2,1)S(1)}, bf16[96,128]{1,0:T(8,128)(2,1)S(1)}, u32[]{:S(2)}, u32[]{:S(2)}) collective-permute-start(bf16[96,128]{1,0:T(8,128)(2,1)S(1)} %get-tuple-element.48), channel_id=1, source_target_pairs={{0,12},{1,13},{2,14},{3,15},{4,0},{5,1},{6,2},{7,3},{8,4},{9,5},{1... | collective-permute-start | bytes 73736 | tf_op jit(solution)/shard_map/ppermute | solution.py:402
  49.0 2.3 %all-to-all-done.1 = bf16[8,168,128]{2,1,0:T(8,128)(2,1)S(1)} async-done(((bf16[8,168,128]{2,1,0:T(8,128)(2,1)}), bf16[8,168,128]{2,1,0:T(8,128)(2,1)S(1)}, u32[]{:S(2)}, u32[]{:S(2)}) %all-to-all-start.1) | async-done | bytes 344096 | tf_op jit(solution)/shard_map/all_to_all | solution.py:384
  51.2 0.1 reduce_sum.12
  51.3 18.3 %all-gather = bf16[2688,128]{1,0:T(8,128)(2,1)S(1)} all-gather(bf16[168,128]{1,0:T(8,128)(2,1)S(1)} %reduce_sum.12), channel_id=2, replica_groups=mesh['rep'=16,'exp'=16] {'rep'}, dimensions={0}, use_global_device_ids=true | all-gather | bytes 731136 | tf_op jit(solution)/shard_map/all_gather | solution.py:404
  69.7 1.4 %shard_map.176 = (f32[4,64,256]{2,1,0:T(8,128)}, f32[4,256,256]{2,1,0:T(8,128)}, f32[3,4,256]{2,1,0:T(4,128)}, f32[64,128]{1,0:T(8,128)}, f32[64,128]{1,0:T(8,12...) custom-call(s32[1]{0:T(128)} %bitcast.y_at, s32[1]{0:T(128)} %bitcast.1.x_at, bf16[16,168,128]{2,1,0:T(8,128)(2,1)S(1)} %bitcast.22, ...), custom_call_target="tpu_custom_call" | custom-call | tf_op jit(solution)/shard_map/pallas_call | solution.py:407
  (18 shorter events, 0.1 us)
Async XLA Ops:
  0.6 10.1 %copy-start.5 = (bf16[4,256,256]{2,1,0:T(8,128)(2,1)S(1)}, bf16[4,256,256]{2,1,0:T(8,128)(2,1)}, u32[]{:S(2)}) copy-start(bf16[4,256,256]{2,1,0:T(8,128)(2,1)} %param.16) | copy-start | bytes 1572868
  3.2 16.1 %all-to-all-start = ((bf16[16,80,128]{2,1,0:T(8,128)(2,1)}), bf16[16,80,128]{2,1,0:T(8,128)(2,1)S(1)}, u32[]{:S(2)}, u32[]{:S(2)}) async-start(bf16[16,80,128]{2,1,0:T(8,128)(2,1)} %get-tuple-element.32), calls=%async_computation | async-start | bytes 655360 | tf_op jit(solution)/shard_map/all_to_all | solution.py:353
  11.1 0.7 copy-start.6
  12.0 0.9 %copy-start = (bf16[4,64,256]{2,1,0:T(8,128)(2,1)S(1)}, bf16[4,64,256]{2,1,0:T(8,128)(2,1)}, u32[]{:S(2)}) copy-start(bf16[4,64,256]{2,1,0:T(8,128)(2,1)} %w_one.3) | copy-start | bytes 393220
  13.2 6.1 %copy-start.4 = (bf16[256,32]{0,1:T(8,128)(2,1)S(1)}, bf16[256,32]{0,1:T(8,128)(2,1)}, u32[]{:S(2)}) copy-start(bf16[256,32]{0,1:T(8,128)(2,1)} %param.18) | copy-start | bytes 49156
  22.7 5.4 %collective-permute-start = (bf16[8,168,128]{2,1,0:T(8,128)(2,1)S(1)}, bf16[8,168,128]{2,1,0:T(8,128)(2,1)S(1)}, u32[]{:S(2)}, u32[]{:S(2)}) collective-permute-start(bf16[8,168,128]{2,1,0:T(8,128)(2,1)S(1)} %get-tuple-element.34), channel_id=1, source_target_pairs={{0,16},{16,0},{32,48},{48,32},{64,80},{80,64},{96,112},{112,96},{1... | collective-permute-start | bytes 1032200 | tf_op jit(solution)/shard_map/ppermute | solution.py:380
  28.9 22.3 %all-to-all-start.1 = ((bf16[8,168,128]{2,1,0:T(8,128)(2,1)}), bf16[8,168,128]{2,1,0:T(8,128)(2,1)S(1)}, u32[]{:S(2)}, u32[]{:S(2)}) async-start(bf16[8,168,128]{2,1,0:T(8,128)(2,1)} %add_convert_fusion), calls=%async_computation.1 | async-start | bytes 688128 | tf_op jit(solution)/shard_map/all_to_all | solution.py:384
  38.4 5.2 %collective-permute-start.1 = (bf16[4,72,128]{2,1,0:T(8,128)(2,1)S(1)}, bf16[4,72,128]{2,1,0:T(8,128)(2,1)S(1)}, u32[]{:S(2)}, u32[]{:S(2)}) collective-permute-start(bf16[4,72,128]{2,1,0:T(8,128)(2,1)S(1)} %get-tuple-element.42), channel_id=1, source_target_pairs={{0,2},{1,3},{2,0},{3,1},{4,6},{5,7},{6,4},{7,5},{8,10},{9,11},{10,... | collective-permute-start | bytes 221192 | tf_op jit(solution)/shard_map/ppermute | solution.py:395
  39.1 6.5 %collective-permute-start.2 = (bf16[4,72,128]{2,1,0:T(8,128)(2,1)S(1)}, bf16[4,72,128]{2,1,0:T(8,128)(2,1)S(1)}, u32[]{:S(2)}, u32[]{:S(2)}) collective-permute-start(bf16[4,72,128]{2,1,0:T(8,128)(2,1)S(1)} %get-tuple-element.43), channel_id=1, source_target_pairs={{0,1},{1,2},{2,3},{3,0},{4,5},{5,6},{6,7},{7,4},{8,9},{9,10},{10,1... | collective-permute-start | bytes 221192 | tf_op jit(solution)/shard_map/ppermute | solution.py:395
  39.5 6.2 %collective-permute-start.3 = (bf16[4,72,128]{2,1,0:T(8,128)(2,1)S(1)}, bf16[4,72,128]{2,1,0:T(8,128)(2,1)S(1)}, u32[]{:S(2)}, u32[]{:S(2)}) collective-permute-start(bf16[4,72,128]{2,1,0:T(8,128)(2,1)S(1)} %get-tuple-element.44), channel_id=1, source_target_pairs={{0,3},{1,0},{2,1},{3,2},{4,7},{5,4},{6,5},{7,6},{8,11},{9,8},{10,9... | collective-permute-start | bytes 221192 | tf_op jit(solution)/shard_map/ppermute | solution.py:395
  45.7 24.0 %collective-permute-start.4 = (bf16[96,128]{1,0:T(8,128)(2,1)S(1)}, bf16[96,128]{1,0:T(8,128)(2,1)S(1)}, u32[]{:S(2)}, u32[]{:S(2)}) collective-permute-start(bf16[96,128]{1,0:T(8,128)(2,1)S(1)} %get-tuple-element.46), channel_id=1, source_target_pairs={{0,8},{1,9},{2,10},{3,11},{4,12},{5,13},{6,14},{7,15},{8,0},{9,1},... | collective-permute-start | bytes 73736 | tf_op jit(solution)/shard_map/ppermute | solution.py:402
  46.3 23.4 %collective-permute-start.5 = (bf16[96,128]{1,0:T(8,128)(2,1)S(1)}, bf16[96,128]{1,0:T(8,128)(2,1)S(1)}, u32[]{:S(2)}, u32[]{:S(2)}) collective-permute-start(bf16[96,128]{1,0:T(8,128)(2,1)S(1)} %get-tuple-element.47), channel_id=1, source_target_pairs={{0,4},{1,5},{2,6},{3,7},{4,8},{5,9},{6,10},{7,11},{8,12},{9,13},{1... | collective-permute-start | bytes 73736 | tf_op jit(solution)/shard_map/ppermute | solution.py:402
  47.0 22.7 %collective-permute-start.6 = (bf16[96,128]{1,0:T(8,128)(2,1)S(1)}, bf16[96,128]{1,0:T(8,128)(2,1)S(1)}, u32[]{:S(2)}, u32[]{:S(2)}) collective-permute-start(bf16[96,128]{1,0:T(8,128)(2,1)S(1)} %get-tuple-element.48), channel_id=1, source_target_pairs={{0,12},{1,13},{2,14},{3,15},{4,0},{5,1},{6,2},{7,3},{8,4},{9,5},{1... | collective-permute-start | bytes 73736 | tf_op jit(solution)/shard_map/ppermute | solution.py:402
  51.3 18.4 %copy-start.1 = (f32[2,32,128]{2,1,0:T(8,128)S(1)}, f32[2,32,128]{2,1,0:T(8,128)}, u32[]{:S(2)}) copy-start(f32[2,32,128]{2,1,0:T(8,128)} %param.12) | copy-start | bytes 98308
  51.3 18.4 %copy-start.2 = (f32[2,32,128]{2,1,0:T(8,128)S(1)}, f32[2,32,128]{2,1,0:T(8,128)}, u32[]{:S(2)}) copy-start(f32[2,32,128]{2,1,0:T(8,128)} %param.13) | copy-start | bytes 98308
  51.3 18.4 %copy-start.3 = (f32[2,32,128]{2,1,0:T(8,128)S(1)}, f32[2,32,128]{2,1,0:T(8,128)}, u32[]{:S(2)}) copy-start(f32[2,32,128]{2,1,0:T(8,128)} %param.14) | copy-start | bytes 98308
